TPU v7x, 256 devices: a whole 4x4x8 slice. The times are simulated.
256 devices in a mesh: rep: 16 (over z_hi, y), tp: 4 (over x), cp: 4 (over z_lo, core).
Axes of the slice: x: 4, y: 4, z: 8 (z_hi: 4, z_lo: 2; z = z_hi * 2 + z_lo), core: 2. Of those that a mesh axis runs over, the one named last changes fastest.
Arguments:
- tokens: bfloat16 [16, 3072, 1280], P('rep', 'cp', 'tp'), may hold values from -6 to 6
- qkv_weight: float32 [1280, 3, 1280], P(('rep', 'cp'), None, 'tp'), may hold values from -0.3 to 0.3
- out_weight: float32 [1280, 1280], P('tp', ('rep', 'cp')), may hold values from -0.3 to 0.3
- gate_up_weight: float32 [1280, 2, 5120], P(('rep', 'cp'), None, 'tp'), may hold values from -0.3 to 0.3
- down_weight: float32 [5120, 1280], P('tp', ('rep', 'cp')), may hold values from -0.15 to 0.15
- qk_scale: float32 [1280], P('tp'), may hold values from 0.9 to 6.6, as said below
- attn_rate: float32 [1280], replicated, may hold values from 0.05 to 0.6
- mlp_rate: float32 [1280], replicated, may hold values from 0.05 to 0.6
- up_scale: float32 [5120], P('tp'), may hold values from 0.5 to 2
- gate_scale: float32 [5120], P('tp'), may hold values from 0.5 to 2
- segment_ids: int32 [16, 3072], P('rep'), may hold values from 0 to 23, never falling along the last dimension, each value on 1 to 512 neighbouring positions
Outputs:
- next_state: bfloat16 [16, 3072, 1280], P('rep', 'cp', 'tp')
Inputs may be any that keep to these rules, and one draw needn't show every extreme that they name: `segment_ids`: along each replica's row the ids never fall, and each prompt covers 1 to 512 positions; some prompt covers exactly 512. `qk_scale`: positive channel scales.
All inputs are finite; a program needn't handle non-finite values.
Results may differ from a plain program's by a relative error of at most 0.015.
Values may be sent and summed in bfloat16 or wider, within the bound.
No kernel may reach another device: no remote copies, remote signals or barrier semaphores. Data moves between devices by JAX's collectives and lax.ppermute only.
A program may use at most 128 MiB of HBM per device.

v0:
```python
import math

import jax
import jax.numpy as jnp
from jax import lax
from jax.experimental import pallas as pl
from jax.experimental.pallas import tpu as pltpu
from jax.sharding import Mesh, PartitionSpec as P

D = 1280
HD = 64
EPS = 1e-06
F32 = jnp.float32
BF16 = jnp.bfloat16
Z = ("zh", "zl")
BLOCK = 256
LOG2E = 1.4426950408889634


def ring(count, step):
    return [(i, (i + step) % count) for i in range(count)]


def shift(block, axis, count, step):
    return lax.ppermute(block, axis, ring(count, step))


def swap_core(block):
    return lax.ppermute(block, "co", [(0, 1), (1, 0)])


SHARDS = 64
SHARD = 20
PADDED = 24
WIDE = SHARDS * PADDED
GROUP = 16 * PADDED
SMALL = pl.BlockSpec(memory_space=pltpu.SMEM)
NEAR = pl.BlockSpec(memory_space=pltpu.VMEM)
FAR = pl.BlockSpec(memory_space=pl.ANY)


def four_blocks(block, axis):
    return [block] + [shift(block, axis, 4, 4 - away) for away in (1, 2, 3)]


def after(blocks, *earlier):
    return list(lax.optimization_barrier((tuple(blocks), earlier))[0])


def strip(block):
    shards = [block[shard * PADDED : shard * PADDED + SHARD] for shard in range(16)]
    return jnp.concatenate(shards, axis=0)


def chunk_squares(read, count, width):
    def step(index, total):
        wide = read(index).astype(F32)
        return total + jnp.sum((wide * wide).reshape(-1, 8, width), axis=0)

    return jnp.sum(lax.fori_loop(0, count, step, jnp.zeros((8, width), F32)), axis=0, keepdims=True)


def attention_kernel(start_ref, q_ref, before_ref, own_ref, o_ref):
    heads = q_ref.shape[0] // HD

    def window(kind, head, block):
        rows = pl.ds(pl.multiple_of((kind * heads + head) * HD, HD), HD)
        ref, block = (before_ref, block) if block < 2 else (own_ref, block - 2)
        return ref[rows, block * BLOCK : (block + 1) * BLOCK]

    key_row = lax.broadcasted_iota(jnp.int32, (BLOCK, BLOCK), 0)
    query_col = lax.broadcasted_iota(jnp.int32, (BLOCK, BLOCK), 1)
    causal = key_row <= query_col

    def one_head(head, carry):
        rows = pl.ds(pl.multiple_of(head * HD, HD), HD)
        for part in range(q_ref.shape[1] // BLOCK):
            cols = slice(part * BLOCK, (part + 1) * BLOCK)
            query = q_ref[rows, cols]
            start = start_ref[:, cols]
            scores = []
            for step in range(3):
                base = (part + step) * BLOCK
                keys = window(0, head, part + step)
                score = lax.dot_general(
                    keys, query, (((0,), (0,)), ((), ())), preferred_element_type=F32
                )
                allowed = key_row >= start - base
                if step == 2:
                    allowed = allowed & causal
                scores.append(jnp.where(allowed, score, -1e30))
            top = jnp.maximum(jnp.maximum(scores[0], scores[1]), scores[2])
            top = jnp.max(top, axis=0, keepdims=True)
            total = jnp.zeros((1, BLOCK), F32)
            mixed = jnp.zeros((HD, BLOCK), F32)
            for step in range(3):
                weight = jnp.exp2((scores[step] - top) * (math.sqrt(HD) * LOG2E))
                total = total + jnp.sum(weight, axis=0, keepdims=True)
                mixed = mixed + jnp.dot(
                    window(1, head, part + step),
                    weight.astype(BF16),
                    preferred_element_type=F32,
                )
            o_ref[rows, cols] = (mixed / total).astype(BF16)
        return carry

    lax.fori_loop(0, heads, one_head, 0)


def attention(start, query, before, own):
    return pl.pallas_call(
        attention_kernel,
        out_shape=jax.ShapeDtypeStruct(query.shape, BF16),
        in_specs=[pl.BlockSpec(memory_space=pltpu.VMEM)] * 4,
        out_specs=pl.BlockSpec(memory_space=pltpu.VMEM),
        cost_estimate=pl.CostEstimate(flops=800_000_000, bytes_accessed=4_000_000, transcendentals=3_000_000),
        name="attention",
    )(start, query, before, own)


def stream_starts(segment):
    order = jnp.arange(segment.shape[0], dtype=jnp.int32)
    earlier = jnp.concatenate([segment[:1], segment[:-1]])
    return lax.cummax(jnp.where(segment != earlier, order, jnp.zeros_like(order)))


def project_kernel(
    place_ref, x0_ref, x1_ref, x2_ref, x3_ref, w0_ref, w1_ref, w2_ref, w3_ref, far_ref, gain_ref, cos_ref, sin_ref,
    query_ref, own_ref, features_ref, size_ref, held, weight, result,
):
    tp, core, spot_y = place_ref[0], place_ref[1], place_ref[2]
    rows = query_ref.shape[1]
    local = query_ref.shape[0]
    held[...] = jnp.zeros_like(held)
    for away, ref in enumerate((x0_ref, x1_ref, x2_ref, x3_ref)):
        for shard in range(16):
            held[(tp + away) % 4, shard, :SHARD] = ref[shard * SHARD : (shard + 1) * SHARD]
    for away, ref in enumerate((w0_ref, w1_ref, w2_ref, w3_ref)):
        y = (spot_y + away) % 4
        for z in range(8):
            weight[z // 2, y, z % 2, core] = ref[z]
            weight[z // 2, y, z % 2, 1 - core] = far_ref[away, z]
    features_ref[...] = held[...].reshape(WIDE, rows)
    size = lax.rsqrt(
        chunk_squares(lambda i: features_ref[pl.ds(pl.multiple_of(i * 128, 128), 128), :], WIDE // 128, rows) + EPS
    )
    size_ref[...] = size
    for kind in range(3):
        part = weight[..., kind * local : (kind + 1) * local].reshape(WIDE, local)
        turned = jnp.transpose(part)
        wide = turned.astype(F32)
        length = lax.rsqrt(jnp.sum(wide * wide, axis=1, keepdims=True) + EPS)
        raw = jnp.dot(turned, features_ref[...], preferred_element_type=F32)
        result[kind * local : (kind + 1) * local] = raw * length * size
    half = HD // 2
    cosine, sine = cos_ref[...], sin_ref[...]

    def one_head(index, carry):
        span = pl.ds(pl.multiple_of(index * HD, HD), HD)
        gain = gain_ref[span, :]
        for kind, target in ((0, query_ref), (1, own_ref)):
            part = result[pl.ds(pl.multiple_of(kind * local + index * HD, HD), HD), :]
            length = lax.rsqrt(jnp.sum(part * part, axis=0, keepdims=True) + EPS)
            part = (gain * (part * length)).astype(BF16).astype(F32)
            first, second = part[:half], part[half:]
            both = [first * cosine - second * sine, first * sine + second * cosine]
            target[span, :] = jnp.concatenate(both, axis=0).astype(BF16)
        spot = pl.ds(pl.multiple_of(local + index * HD, HD), HD)
        own_ref[spot, :] = result[pl.ds(pl.multiple_of(2 * local + index * HD, HD), HD), :].astype(BF16)
        return carry

    lax.fori_loop(0, local // HD, one_head, 0)


def project(spot, blocks, near, far, gain, cosine, sine):
    local, rows = blocks[0].shape
    return pl.pallas_call(
        project_kernel,
        out_shape=[
            jax.ShapeDtypeStruct((local, rows), BF16),
            jax.ShapeDtypeStruct((2 * local, rows), BF16),
            jax.ShapeDtypeStruct((WIDE, rows), BF16),
            jax.ShapeDtypeStruct((1, rows), F32),
        ],
        in_specs=[SMALL] + [NEAR] * 12,
        out_specs=[NEAR] * 4,
        scratch_shapes=[
            pltpu.VMEM((4, 16, PADDED, rows), BF16),
            pltpu.VMEM((4, 4, 2, 2, PADDED, 3 * local), BF16),
            pltpu.VMEM((3 * local, rows), F32),
        ],
        compiler_params=pltpu.CompilerParams(vmem_limit_bytes=40 * 2**20),
        cost_estimate=pl.CostEstimate(flops=1_900_000_000, bytes_accessed=12_000_000, transcendentals=0),
        name="project",
    )(spot, *blocks, *near, far, gain, cosine, sine)


def layer_kernel(
    place_ref, a0_ref, a1_ref, a2_ref, a3_ref, features_ref, size_ref, attn_ref, up_ref, gate_ref, weight_ref,
    part_ref, mixed_ref, attended, state, turned, inner, weight, sems,
):
    tp = place_ref[0]
    rows = features_ref.shape[1]
    hidden = up_ref.shape[1]
    bounds = (0, D, D + 2 * hidden, D + 3 * hidden)
    copies = []
    for kind in range(3):
        cols = slice(bounds[kind], bounds[kind + 1])
        copies.append(pltpu.make_async_copy(weight_ref.at[:, :, cols], weight.at[:, :, cols], sems.at[kind]))
        copies[kind].start()
    for away, ref in enumerate((a0_ref, a1_ref, a2_ref, a3_ref)):
        attended[away * 320 : (away + 1) * 320] = ref[...]
    copies[0].wait()

    def group(index, cols):
        return weight[pl.ds(16 * index, 16), :, cols].reshape(GROUP, -1)

    def eighth(index):
        return weight[pl.ds(8 * index, 8), :, :D].reshape(8 * PADDED, D)

    out_length = lax.rsqrt(chunk_squares(eighth, 8, D) + EPS)

    def project_out(index, total):
        left = (group(index, slice(0, D)).astype(F32) * out_length).astype(BF16)
        block = jnp.dot(left, attended[...], preferred_element_type=F32)
        state[pl.ds(pl.multiple_of(index * GROUP, GROUP), GROUP), :] = block
        return total + jnp.sum((block * block).reshape(-1, 8, rows), axis=0)

    zero = jnp.zeros((8, rows), F32)
    total = jnp.sum(lax.fori_loop(0, 4, project_out, zero), axis=0, keepdims=True)
    pull = lax.rsqrt(total + EPS)
    size = size_ref[...]

    def mix(index, total):
        span = pl.ds(pl.multiple_of(index * 128, 128), 128)
        before = features_ref[span, :].astype(F32) * size
        mixed = before + attn_ref[span, :] * (state[span, :] * pull - before)
        state[span, :] = mixed
        return total + jnp.sum((mixed * mixed).reshape(-1, 8, rows), axis=0)

    total = jnp.sum(lax.fori_loop(0, WIDE // 128, mix, zero), axis=0, keepdims=True)
    scale = lax.rsqrt(total + EPS)

    def turn(index, carry):
        span = pl.ds(pl.multiple_of(index * 128, 128), 128)
        mixed = state[span, :] * scale
        state[span, :] = mixed
        turned[:, span] = jnp.transpose(mixed).astype(BF16)
        return carry

    lax.fori_loop(0, WIDE // 128, turn, 0)
    mixed_ref[...] = strip(state[pl.ds(pl.multiple_of(tp * GROUP, GROUP), GROUP), :])
    copies[1].wait()
    copies[2].wait()

    def columns(start, index):
        return weight[:, :, pl.ds(pl.multiple_of(start + index * BLOCK, BLOCK), BLOCK)].reshape(WIDE, BLOCK)

    def length(part):
        wide = part.astype(F32)
        return lax.rsqrt(jnp.sum(wide * wide, axis=0, keepdims=True) + EPS)

    def expand(index, carry):
        cols = pl.ds(pl.multiple_of(index * BLOCK, BLOCK), BLOCK)
        up_part, gate_part = columns(D, index), columns(D + hidden, index)
        up = jnp.dot(turned[...], up_part, preferred_element_type=F32)
        gate = jnp.dot(turned[...], gate_part, preferred_element_type=F32)
        up = up * (up_ref[:, cols] * length(up_part) * length(columns(D + 2 * hidden, index)))
        gate = gate * (gate_ref[:, cols] * length(gate_part) * math.sqrt(D))
        inner[:, cols] = (up * (gate / (1.0 + jnp.exp(-gate)))).astype(BF16)
        return carry

    lax.fori_loop(0, hidden // BLOCK, expand, 0)

    def contract(index, carry):
        block = lax.dot_general(
            group(index, slice(D + 2 * hidden, D + 3 * hidden)),
            inner[...],
            (((1,), (1,)), ((), ())),
            preferred_element_type=F32,
        )
        part_ref[index] = strip(block).astype(BF16)
        return carry

    lax.fori_loop(0, 4, contract, 0)


def layer(spot, attended, features, size, attn_step, up_scale, gate_scale, weight):
    local, rows = attended[0].shape
    hidden = up_scale.shape[1]
    return pl.pallas_call(
        layer_kernel,
        out_shape=[
            jax.ShapeDtypeStruct((4, local, rows), BF16),
            jax.ShapeDtypeStruct((local, rows), F32),
        ],
        in_specs=[SMALL] + [NEAR] * 9 + [FAR],
        out_specs=[NEAR] * 2,
        scratch_shapes=[
            pltpu.VMEM((D, rows), BF16),
            pltpu.VMEM((WIDE, rows), F32),
            pltpu.VMEM((rows, WIDE), BF16),
            pltpu.VMEM((rows, hidden), BF16),
            pltpu.VMEM((SHARDS, PADDED, D + 3 * hidden), BF16),
            pltpu.SemaphoreType.DMA((3,)),
        ],
        compiler_params=pltpu.CompilerParams(vmem_limit_bytes=56 * 2**20),
        cost_estimate=pl.CostEstimate(flops=10_000_000_000, bytes_accessed=20_000_000, transcendentals=1_000_000),
        name="layer",
    )(spot, *attended, features, size, attn_step, up_scale, gate_scale, weight)


def body(
    tokens,
    qkv_weight,
    out_weight,
    gate_up_weight,
    down_weight,
    qk_scale,
    attn_rate,
    mlp_rate,
    up_scale,
    gate_scale,
    segment_ids,
):
    rows = tokens.shape[1]
    local = tokens.shape[2]
    hidden = gate_up_weight.shape[2]
    tp = lax.axis_index("tp")
    core = lax.axis_index("co")
    spot_y = lax.axis_index("y")
    piece = lax.axis_index("zl") * 2 + core
    spot = jnp.stack([tp, core, spot_y]).astype(jnp.int32)

    def pad(shard):
        return jnp.pad(shard, ((0, PADDED - SHARD), (0, 0)))

    out_rows = four_blocks(out_weight.T.astype(BF16), "tp")
    wide = gate_up_weight.astype(BF16).reshape(SHARD, 2 * hidden)
    rest = pad(jnp.concatenate(out_rows + [wide, down_weight.T.astype(BF16)], axis=1))
    weight = lax.all_gather(rest, ("zh", "y", "zl", "co"))

    own_tokens, qkv = after([tokens[0].T, pad(qkv_weight.astype(BF16).reshape(SHARD, 3 * local))], rest)
    blocks = four_blocks(own_tokens, "tp")
    everywhere = jnp.broadcast_to(qkv[None], (8,) + qkv.shape)
    qkv_z = lax.all_to_all(everywhere, Z, 0, 0, tiled=True)
    (qkv_z,) = after([qkv_z], *blocks)
    qkv_near = four_blocks(qkv_z, "y")
    qkv_far = swap_core(jnp.stack(qkv_near))

    starts = stream_starts(segment_ids[0])
    own_first = piece * rows
    own_start = lax.dynamic_slice_in_dim(starts, own_first, rows)
    position = own_first + jnp.arange(rows, dtype=jnp.int32) - own_start
    frequency = jnp.exp(-math.log(10000.0) * jnp.arange(HD // 2, dtype=F32) * 2.0 / HD)
    angles = frequency[:, None] * position.astype(F32)[None]
    query, own, features, size = project(
        spot, blocks, qkv_near, qkv_far, qk_scale[:, None], jnp.cos(angles), jnp.sin(angles)
    )
    window = 2 * BLOCK
    before = lax.ppermute(own[:, rows - window :], ("zl", "co"), [(i, i + 1) for i in range(3)])
    attended = attention((own_start - own_first + window)[None], query, before, own)

    parts, mixed = layer(
        spot,
        four_blocks(attended, "tp"),
        features,
        size,
        jnp.pad(attn_rate.reshape(SHARDS, SHARD), ((0, 0), (0, PADDED - SHARD))).reshape(WIDE, 1),
        up_scale[None],
        gate_scale[None],
        weight,
    )
    landed = lax.all_to_all(parts, "tp", 0, 0, tiled=True).astype(F32)
    mlp_block = landed[0] + landed[1] + landed[2] + landed[3]

    step_block = lax.dynamic_slice_in_dim(mlp_rate, tp * local, local)[:, None]
    kept = mixed - step_block * mixed
    moved = step_block * mlp_block
    sums = jnp.stack(
        [
            jnp.sum(mlp_block * mlp_block, axis=0),
            jnp.sum(kept * kept, axis=0),
            jnp.sum(kept * moved, axis=0),
            jnp.sum(moved * moved, axis=0),
        ]
    )
    sums = sum(four_blocks(sums, "tp"))
    pull = lax.rsqrt(sums[0] + EPS)
    length = jnp.maximum(sums[1] + 2.0 * pull * sums[2] + pull * pull * sums[3], 0.0)
    final = math.sqrt(D) * lax.rsqrt(length + EPS)
    result = ((kept + pull[None] * moved) * final[None]).astype(BF16)
    return result.T[None]


def solution(mesh):
    fine = Mesh(mesh.devices.reshape(4, 4, 4, 2, 2), ("zh", "y", "tp", "zl", "co"))
    rep, cp = ("zh", "y"), ("zl", "co")
    in_specs = (
        P(rep, cp, "tp"),
        P(rep + cp, None, "tp"),
        P("tp", rep + cp),
        P(rep + cp, None, "tp"),
        P("tp", rep + cp),
        P("tp"),
        P(),
        P(),
        P("tp"),
        P("tp"),
        P(rep, None),
    )
    return jax.shard_map(
        body, mesh=fine, in_specs=in_specs, out_specs=P(rep, cp, "tp"), check_vma=False
    )
```

profile of v0, /device:TPU:16, one launch (start us, length us, event | category | flops | bytes accessed | tf_op | source)
XLA Modules:
  0.0 234.5 jit_solution(15013975319065024097)
XLA Ops:
  7.3 2.8 %collective-permute-start = (bf16[20,320]{1,0:T(8,128)(2,1)S(1)}, bf16[20,320]{1,0:T(8,128)(2,1)S(1)}, u32[]{:S(2)}, u32[]{:S(2)}) collective-permute-start(bf16[20,320]{1,0:T(8,128)(2,1)S(1)} %convert_bitcast_fusion.1), channel_id=1, source_target_pairs={{0,12},{4,0},{8,4},{12,8},{1,13},{5,1},{9,5},{13,9},{2,14},{6,2},{... | collective-permute-start | bytes 38408 | tf_op jit(solution)/shard_map/ppermute | solution.py:25
  13.8 1.5 collective-permute-done.1
  17.7 8.5 %all-to-all-start = ((bf16[8,24,960]{2,1,0:T(8,128)(2,1)}), bf16[8,24,960]{2,1,0:T(8,128)(2,1)S(1)}, u32[]{:S(2)}, u32[]{:S(2)}) async-start(bf16[8,24,960]{2,1,0:T(8,128)(2,1)} %broadcast_in_dim.31), calls=%async_computation | async-start | bytes 786432 | tf_op jit(solution)/shard_map/all_to_all | solution.py:346
  26.6 1.5 collective-permute-start.4
  29.2 11.2 %collective-permute-done.3.x1_ref = bf16[320,768]{1,0:T(8,128)(2,1)S(1)} collective-permute-done((bf16[320,768]{1,0:T(8,128)(2,1)S(1)}, bf16[320,768]{1,0:T(8,128)(2,1)S(1)}, u32[]{:S(2)}, u32[]{:S(2)}) %collective-permute-start.3) | collective-permute-done | bytes 491552 | tf_op jit(solution)/shard_map/ppermute | solution.py:25
  40.4 1.9 collective-permute-done.4.x2_ref
  42.3 7.9 %collective-permute-done.5.x3_ref = bf16[320,768]{1,0:T(8,128)(2,1)S(1)} collective-permute-done((bf16[320,768]{1,0:T(8,128)(2,1)S(1)}, bf16[320,768]{1,0:T(8,128)(2,1)S(1)}, u32[]{:S(2)}, u32[]{:S(2)}) %collective-permute-start.5) | collective-permute-done | bytes 491552 | tf_op jit(solution)/shard_map/ppermute | solution.py:25
  51.4 2.9 %collective-permute-start.7 = (bf16[8,24,960]{2,1,0:T(8,128)(2,1)S(1)}, bf16[8,24,960]{2,1,0:T(8,128)(2,1)S(1)}, u32[]{:S(2)}, u32[]{:S(2)}) collective-permute-start(bf16[8,24,960]{2,1,0:T(8,128)(2,1)S(1)} %all-to-all-done.w0_ref), channel_id=1, source_target_pairs={{0,32},{16,48},{32,0},{48,16},{1,33},{17,49},{33,1},{49,17},{2,34}... | collective-permute-start | bytes 1105928 | tf_op jit(solution)/shard_map/ppermute | solution.py:25
  54.3 15.8 %collective-permute-done.6.w1_ref = bf16[8,24,960]{2,1,0:T(8,128)(2,1)S(1)} collective-permute-done((bf16[8,24,960]{2,1,0:T(8,128)(2,1)S(1)}, bf16[8,24,960]{2,1,0:T(8,128)(2,1)S(1)}, u32[]{:S(2)}, u32[]{:S(2)}) %collective-permute-start.6) | collective-permute-done | bytes 368672 | tf_op jit(solution)/shard_map/ppermute | solution.py:25
  70.1 3.2 %collective-permute-done.7.w2_ref = bf16[8,24,960]{2,1,0:T(8,128)(2,1)S(1)} collective-permute-done((bf16[8,24,960]{2,1,0:T(8,128)(2,1)S(1)}, bf16[8,24,960]{2,1,0:T(8,128)(2,1)S(1)}, u32[]{:S(2)}, u32[]{:S(2)}) %collective-permute-start.7) | collective-permute-done | bytes 368672 | tf_op jit(solution)/shard_map/ppermute | solution.py:25
  73.3 8.3 %collective-permute-done.8.w3_ref = bf16[8,24,960]{2,1,0:T(8,128)(2,1)S(1)} collective-permute-done((bf16[8,24,960]{2,1,0:T(8,128)(2,1)S(1)}, bf16[8,24,960]{2,1,0:T(8,128)(2,1)S(1)}, u32[]{:S(2)}, u32[]{:S(2)}) %collective-permute-start.8) | collective-permute-done | bytes 368672 | tf_op jit(solution)/shard_map/ppermute | solution.py:25
  81.6 1.4 pad_maximum_fusion
  85.5 1.2 collective-permute-done.9.far_ref
  89.8 6.2 %project.1 = (bf16[320,768]{1,0:T(8,128)(2,1)S(1)}, bf16[640,768]{1,0:T(8,128)(2,1)S(1)}, bf16[1536,768]{1,0:T(8,128)(2,1)S(1)}, f32[1,768]{1,0:T(1,128)S(1)}) custom-call(s32[3]{0:T(128)S(1)} %pad_add_fusion.place_ref, bf16[320,768]{1,0:T(8,128)(2,1)S(1)} %bitcast.44, bf16[320,768]{1,0:T(8,128)(2,1)S(1)} %copy-done.4, bf16[320,768]{1,0:T(8,128)(2,1)S(1)} %copy-done.6, ...), custom_call_target="tpu_custom_call" | custom-call | flops 1900000000 | bytes 12000000 | tf_op jit(solution)/shard_map/project/pallas_call | solution.py:177
  96.0 1.4 copy-done.9
  98.8 2.1 collective-permute-start.10
  101.5 1.1 collective-permute-done.10.before_ref
  103.5 9.6 %attention.1.a0_ref = bf16[320,768]{1,0:T(8,128)(2,1)} custom-call(s32[1,768]{1,0:T(1,128)} %broadcast_in_dim.30.start_ref, bf16[320,768]{1,0:T(8,128)(2,1)} %copy-done.10, bf16[640,512]{1,0:T(8,128)(2,1)} %copy-done.19, bf16[640,768]{1,0:T(8,128)(2,1)} %copy-done), custom_call_target="tpu_custom_call" | custom-call | flops 800000000 | bytes 4000000 | tf_op jit(solution)/shard_map/attention/pallas_call | solution.py:111
  113.1 1.7 collective-permute-start.12
  114.8 1.4 collective-permute-start.13
  116.3 1.2 reshape.47.attn_ref
  118.7 3.3 %collective-permute-done.11.a1_ref = bf16[320,768]{1,0:T(8,128)(2,1)S(1)} collective-permute-done((bf16[320,768]{1,0:T(8,128)(2,1)}, bf16[320,768]{1,0:T(8,128)(2,1)S(1)}, u32[]{:S(2)}, u32[]{:S(2)}) %collective-permute-start.11) | collective-permute-done | bytes 491552 | tf_op jit(solution)/shard_map/ppermute | solution.py:25
  122.1 1.7 collective-permute-done.12.a2_ref
  123.7 14.6 %collective-permute-done.13.a3_ref = bf16[320,768]{1,0:T(8,128)(2,1)S(1)} collective-permute-done((bf16[320,768]{1,0:T(8,128)(2,1)}, bf16[320,768]{1,0:T(8,128)(2,1)S(1)}, u32[]{:S(2)}, u32[]{:S(2)}) %collective-permute-start.13) | collective-permute-done | bytes 491552 | tf_op jit(solution)/shard_map/ppermute | solution.py:25
  138.3 25.8 %all-gather.3.cloned.1.call-done = bf16[1536,5120]{1,0:T(8,128)(2,1)} async-done(((bf16[24,5120]{1,0:T(8,128)(2,1)}), bf16[1536,5120]{1,0:T(8,128)(2,1)}) %all-gather.3.cloned.1.call-update) | async-done | bytes 15728656 | tf_op jit(solution)/shard_map/all_gather | solution.py:341
  164.1 24.7 %layer.1 = (bf16[4,320,768]{2,1,0:T(8,128)(2,1)}, f32[320,768]{1,0:T(8,128)}) custom-call(s32[3]{0:T(128)} %copy-done.1, bf16[320,768]{1,0:T(8,128)(2,1)} %attention.1.a0_ref, bf16[320,768]{1,0:T(8,128)(2,1)} %copy-done.20, bf16[320,768]{1,0:T(8,128)(2,1)} %copy-done.21, bf16[320,768]{1,0:T(8,128)(2,1)} %copy-done.22, bf16[1536,768]{1,0:T(8,128)(2,1)} %copy-done.9, ...), custom_call_target="tpu_custom_call" | custom-call | flops 10000000000 | bytes 20000000 | tf_op jit(solution)/shard_map/layer/pallas_call | solution.py:291
  188.8 3.8 %all-to-all-start.1 = ((bf16[4,320,768]{2,1,0:T(8,128)(2,1)}), bf16[4,320,768]{2,1,0:T(8,128)(2,1)S(1)}, u32[]{:S(2)}, u32[]{:S(2)}) async-start(bf16[4,320,768]{2,1,0:T(8,128)(2,1)} %get-tuple-element.22), calls=%async_computation.1 | async-start | bytes 3932160 | tf_op jit(solution)/shard_map/all_to_all | solution.py:374
  193.4 24.6 %all-to-all-done.1 = bf16[4,320,768]{2,1,0:T(8,128)(2,1)S(1)} async-done(((bf16[4,320,768]{2,1,0:T(8,128)(2,1)}), bf16[4,320,768]{2,1,0:T(8,128)(2,1)S(1)}, u32[]{:S(2)}, u32[]{:S(2)}) %all-to-all-start.1) | async-done | bytes 1966112 | tf_op jit(solution)/shard_map/all_to_all | solution.py:374
  218.9 1.2 collective-permute-start.14
  220.1 1.5 collective-permute-start.15
  222.7 2.7 %collective-permute-done.15 = f32[4,768]{1,0:T(4,128)S(1)} collective-permute-done((f32[4,768]{1,0:T(4,128)S(1)}, f32[4,768]{1,0:T(4,128)S(1)}, u32[]{:S(2)}, u32[]{:S(2)}) %collective-permute-start.15) | collective-permute-done | bytes 12320 | tf_op jit(solution)/shard_map/ppermute | solution.py:25
  225.3 1.2 collective-permute-done.16
  (101 shorter events, 23.2 us)
Async XLA Ops:
  6.5 10.2 %copy-start.13 = (f32[20,3,320]{2,0,1:T(8,128)S(1)}, f32[20,3,320]{2,0,1:T(8,128)}, u32[]{:S(2)}) copy-start(f32[20,3,320]{2,0,1:T(8,128)} %param.12) | copy-start | bytes 230404
  6.5 157.5 %all-gather.3.cloned.1.call-start = ((), (), s32[]{:S(2)}) async-start(), calls=%async_computation.2 | async-start | bytes 15974400 | tf_op jit(solution)/shard_map/all_gather | solution.py:341
  7.3 6.5 %collective-permute-start = (bf16[20,320]{1,0:T(8,128)(2,1)S(1)}, bf16[20,320]{1,0:T(8,128)(2,1)S(1)}, u32[]{:S(2)}, u32[]{:S(2)}) collective-permute-start(bf16[20,320]{1,0:T(8,128)(2,1)S(1)} %convert_bitcast_fusion.1), channel_id=1, source_target_pairs={{0,12},{4,0},{8,4},{12,8},{1,13},{5,1},{9,5},{13,9},{2,14},{6,2},{... | collective-permute-start | bytes 38408 | tf_op jit(solution)/shard_map/ppermute | solution.py:25
  10.1 5.3 %collective-permute-start.1 = (bf16[20,320]{1,0:T(8,128)(2,1)S(1)}, bf16[20,320]{1,0:T(8,128)(2,1)S(1)}, u32[]{:S(2)}, u32[]{:S(2)}) collective-permute-start(bf16[20,320]{1,0:T(8,128)(2,1)S(1)} %convert_bitcast_fusion.1), channel_id=1, source_target_pairs={{0,8},{4,12},{8,0},{12,4},{1,9},{5,13},{9,1},{13,5},{2,10},{6,14},... | collective-permute-start | bytes 38408 | tf_op jit(solution)/shard_map/ppermute | solution.py:25
  10.9 5.0 %collective-permute-start.2 = (bf16[20,320]{1,0:T(8,128)(2,1)S(1)}, bf16[20,320]{1,0:T(8,128)(2,1)S(1)}, u32[]{:S(2)}, u32[]{:S(2)}) collective-permute-start(bf16[20,320]{1,0:T(8,128)(2,1)S(1)} %convert_bitcast_fusion.1), channel_id=1, source_target_pairs={{0,4},{4,8},{8,12},{12,0},{1,5},{5,9},{9,13},{13,1},{2,6},{6,10},{... | collective-permute-start | bytes 38408 | tf_op jit(solution)/shard_map/ppermute | solution.py:25
  13.8 12.4 %copy-start.2 = (bf16[1,768,320]{1,2,0:T(8,128)(2,1)S(1)}, bf16[1,768,320]{1,2,0:T(8,128)(2,1)}, u32[]{:S(2)}) copy-start(bf16[1,768,320]{1,2,0:T(8,128)(2,1)} %param.11) | copy-start | bytes 1474564
  17.7 33.3 %all-to-all-start = ((bf16[8,24,960]{2,1,0:T(8,128)(2,1)}), bf16[8,24,960]{2,1,0:T(8,128)(2,1)S(1)}, u32[]{:S(2)}, u32[]{:S(2)}) async-start(bf16[8,24,960]{2,1,0:T(8,128)(2,1)} %broadcast_in_dim.31), calls=%async_computation | async-start | bytes 786432 | tf_op jit(solution)/shard_map/all_to_all | solution.py:346
  26.2 14.2 %collective-permute-start.3 = (bf16[320,768]{1,0:T(8,128)(2,1)S(1)}, bf16[320,768]{1,0:T(8,128)(2,1)S(1)}, u32[]{:S(2)}, u32[]{:S(2)}) collective-permute-start(bf16[320,768]{1,0:T(8,128)(2,1)S(1)} %bitcast.41), channel_id=1, source_target_pairs={{0,12},{4,0},{8,4},{12,8},{1,13},{5,1},{9,5},{13,9},{2,14},{6,2},{... | collective-permute-start | bytes 1474568 | tf_op jit(solution)/shard_map/ppermute | solution.py:25
  26.6 15.7 %collective-permute-start.4 = (bf16[320,768]{1,0:T(8,128)(2,1)S(1)}, bf16[320,768]{1,0:T(8,128)(2,1)S(1)}, u32[]{:S(2)}, u32[]{:S(2)}) collective-permute-start(bf16[320,768]{1,0:T(8,128)(2,1)S(1)} %bitcast.42), channel_id=1, source_target_pairs={{0,8},{4,12},{8,0},{12,4},{1,9},{5,13},{9,1},{13,5},{2,10},{6,14},... | collective-permute-start | bytes 1474568 | tf_op jit(solution)/shard_map/ppermute | solution.py:25
  28.1 22.1 %collective-permute-start.5 = (bf16[320,768]{1,0:T(8,128)(2,1)S(1)}, bf16[320,768]{1,0:T(8,128)(2,1)S(1)}, u32[]{:S(2)}, u32[]{:S(2)}) collective-permute-start(bf16[320,768]{1,0:T(8,128)(2,1)S(1)} %bitcast.43), channel_id=1, source_target_pairs={{0,4},{4,8},{8,12},{12,0},{1,5},{5,9},{9,13},{13,1},{2,6},{6,10},{... | collective-permute-start | bytes 1474568 | tf_op jit(solution)/shard_map/ppermute | solution.py:25
  40.4 42.5 %copy-start.3 = (bf16[320,768]{1,0:T(8,128)(2,1)}, bf16[320,768]{1,0:T(8,128)(2,1)S(1)}, u32[]{:S(2)}) copy-start(bf16[320,768]{1,0:T(8,128)(2,1)S(1)} %collective-permute-done.3.x1_ref) | copy-start | bytes 1474564
  42.3 40.7 %copy-start.5 = (bf16[320,768]{1,0:T(8,128)(2,1)}, bf16[320,768]{1,0:T(8,128)(2,1)S(1)}, u32[]{:S(2)}) copy-start(bf16[320,768]{1,0:T(8,128)(2,1)S(1)} %collective-permute-done.4.x2_ref) | copy-start | bytes 1474564
  51.0 19.1 %collective-permute-start.6 = (bf16[8,24,960]{2,1,0:T(8,128)(2,1)S(1)}, bf16[8,24,960]{2,1,0:T(8,128)(2,1)S(1)}, u32[]{:S(2)}, u32[]{:S(2)}) collective-permute-start(bf16[8,24,960]{2,1,0:T(8,128)(2,1)S(1)} %all-to-all-done.w0_ref), channel_id=1, source_target_pairs={{0,48},{16,0},{32,16},{48,32},{1,49},{17,1},{33,17},{49,33},{2,50}... | collective-permute-start | bytes 1105928 | tf_op jit(solution)/shard_map/ppermute | solution.py:25
  51.4 21.9 %collective-permute-start.7 = (bf16[8,24,960]{2,1,0:T(8,128)(2,1)S(1)}, bf16[8,24,960]{2,1,0:T(8,128)(2,1)S(1)}, u32[]{:S(2)}, u32[]{:S(2)}) collective-permute-start(bf16[8,24,960]{2,1,0:T(8,128)(2,1)S(1)} %all-to-all-done.w0_ref), channel_id=1, source_target_pairs={{0,32},{16,48},{32,0},{48,16},{1,33},{17,49},{33,1},{49,17},{2,34}... | collective-permute-start | bytes 1105928 | tf_op jit(solution)/shard_map/ppermute | solution.py:25
  54.3 27.2 %collective-permute-start.8 = (bf16[8,24,960]{2,1,0:T(8,128)(2,1)S(1)}, bf16[8,24,960]{2,1,0:T(8,128)(2,1)S(1)}, u32[]{:S(2)}, u32[]{:S(2)}) collective-permute-start(bf16[8,24,960]{2,1,0:T(8,128)(2,1)S(1)} %all-to-all-done.w0_ref), channel_id=1, source_target_pairs={{0,16},{16,32},{32,48},{48,0},{1,17},{17,33},{33,49},{49,1},{2,18}... | collective-permute-start | bytes 1105928 | tf_op jit(solution)/shard_map/ppermute | solution.py:25
  83.0 3.8 %collective-permute-start.9 = (bf16[4,8,24,960]{3,2,1,0:T(8,128)(2,1)}, bf16[4,8,24,960]{3,2,1,0:T(8,128)(2,1)}, u32[]{:S(2)}, u32[]{:S(2)}) collective-permute-start(bf16[4,8,24,960]{3,2,1,0:T(8,128)(2,1)} %pad_maximum_fusion), channel_id=1, source_target_pairs={{0,1},{1,0},{2,3},{3,2},{4,5},{5,4},{6,7},{7,6},{8,9},{9,8},{10,11... | collective-permute-start | bytes 4423688 | tf_op jit(solution)/shard_map/ppermute | solution.py:29
  84.8 11.2 %copy-start.1 = (s32[3]{0:T(128)}, s32[3]{0:T(128)S(1)}, u32[]{:S(2)}) copy-start(s32[3]{0:T(128)S(1)} %pad_add_fusion.place_ref) | copy-start | bytes 40
  98.8 3.8 %collective-permute-start.10 = (bf16[640,512]{1,0:T(8,128)(2,1)S(1)}, bf16[640,512]{1,0:T(8,128)(2,1)S(1)}, u32[]{:S(2)}, u32[]{:S(2)}) collective-permute-start(bf16[640,512]{1,0:T(8,128)(2,1)S(1)} %slice.52), channel_id=1, source_target_pairs={{0,1},{1,2},{2,3},{4,5},{5,6},{6,7},{8,9},{9,10},{10,11},{12,13},{... | collective-permute-start | bytes 1966088 | tf_op jit(solution)/shard_map/ppermute | solution.py:361
  103.4 12.8 %copy-start.15 = (f32[1280]{0:T(1024)S(1)}, f32[1280]{0:T(1024)}, u32[]{:S(2)}) copy-start(f32[1280]{0:T(1024)} %param.17) | copy-start | bytes 15364
  103.5 14.1 %copy-start.16 = (f32[1280]{0:T(1024)S(1)}, f32[1280]{0:T(1024)}, u32[]{:S(2)}) copy-start(f32[1280]{0:T(1024)} %param.19) | copy-start | bytes 15364
  103.5 14.7 %copy-start.17 = (f32[1280]{0:T(1024)S(1)}, f32[1280]{0:T(1024)}, u32[]{:S(2)}) copy-start(f32[1280]{0:T(1024)} %param.20) | copy-start | bytes 15364
  113.0 9.0 %collective-permute-start.11 = (bf16[320,768]{1,0:T(8,128)(2,1)}, bf16[320,768]{1,0:T(8,128)(2,1)S(1)}, u32[]{:S(2)}, u32[]{:S(2)}) collective-permute-start(bf16[320,768]{1,0:T(8,128)(2,1)} %attention.1.a0_ref), channel_id=1, source_target_pairs={{0,12},{4,0},{8,4},{12,8},{1,13},{5,1},{9,5},{13,9},{2,14},{6,2},{... | collective-permute-start | bytes 1474568 | tf_op jit(solution)/shard_map/ppermute | solution.py:25
  113.1 10.6 %collective-permute-start.12 = (bf16[320,768]{1,0:T(8,128)(2,1)}, bf16[320,768]{1,0:T(8,128)(2,1)S(1)}, u32[]{:S(2)}, u32[]{:S(2)}) collective-permute-start(bf16[320,768]{1,0:T(8,128)(2,1)} %attention.1.a0_ref), channel_id=1, source_target_pairs={{0,8},{4,12},{8,0},{12,4},{1,9},{5,13},{9,1},{13,5},{2,10},{6,14},... | collective-permute-start | bytes 1474568 | tf_op jit(solution)/shard_map/ppermute | solution.py:25
  114.8 23.5 %collective-permute-start.13 = (bf16[320,768]{1,0:T(8,128)(2,1)}, bf16[320,768]{1,0:T(8,128)(2,1)S(1)}, u32[]{:S(2)}, u32[]{:S(2)}) collective-permute-start(bf16[320,768]{1,0:T(8,128)(2,1)} %attention.1.a0_ref), channel_id=1, source_target_pairs={{0,4},{4,8},{8,12},{12,0},{1,5},{5,9},{9,13},{13,1},{2,6},{6,10},{... | collective-permute-start | bytes 1474568 | tf_op jit(solution)/shard_map/ppermute | solution.py:25
  122.0 42.0 %copy-start.20 = (bf16[320,768]{1,0:T(8,128)(2,1)}, bf16[320,768]{1,0:T(8,128)(2,1)S(1)}, u32[]{:S(2)}) copy-start(bf16[320,768]{1,0:T(8,128)(2,1)S(1)} %collective-permute-done.11.a1_ref) | copy-start | bytes 1474564
  123.7 40.3 %copy-start.21 = (bf16[320,768]{1,0:T(8,128)(2,1)}, bf16[320,768]{1,0:T(8,128)(2,1)S(1)}, u32[]{:S(2)}) copy-start(bf16[320,768]{1,0:T(8,128)(2,1)S(1)} %collective-permute-done.12.a2_ref) | copy-start | bytes 1474564
  138.3 25.8 %copy-start.22 = (bf16[320,768]{1,0:T(8,128)(2,1)}, bf16[320,768]{1,0:T(8,128)(2,1)S(1)}, u32[]{:S(2)}) copy-start(bf16[320,768]{1,0:T(8,128)(2,1)S(1)} %collective-permute-done.13.a3_ref) | copy-start | bytes 1474564
  188.8 29.2 %all-to-all-start.1 = ((bf16[4,320,768]{2,1,0:T(8,128)(2,1)}), bf16[4,320,768]{2,1,0:T(8,128)(2,1)S(1)}, u32[]{:S(2)}, u32[]{:S(2)}) async-start(bf16[4,320,768]{2,1,0:T(8,128)(2,1)} %get-tuple-element.22), calls=%async_computation.1 | async-start | bytes 3932160 | tf_op jit(solution)/shard_map/all_to_all | solution.py:374
  193.4 24.9 %copy-start.12 = (f32[320,768]{1,0:T(8,128)S(1)}, f32[320,768]{1,0:T(8,128)}, u32[]{:S(2)}) copy-start(f32[320,768]{1,0:T(8,128)} %get-tuple-element.21) | copy-start | bytes 2949124
  218.9 3.8 %collective-permute-start.14 = (f32[4,768]{1,0:T(4,128)S(1)}, f32[4,768]{1,0:T(4,128)S(1)}, u32[]{:S(2)}, u32[]{:S(2)}) collective-permute-start(f32[4,768]{1,0:T(4,128)S(1)} %pad_maximum_fusion.1), channel_id=1, source_target_pairs={{0,12},{4,0},{8,4},{12,8},{1,13},{5,1},{9,5},{13,9},{2,14},{6,2},{... | collective-permute-start | bytes 36872 | tf_op jit(solution)/shard_map/ppermute | solution.py:25
  220.1 5.2 %collective-permute-start.15 = (f32[4,768]{1,0:T(4,128)S(1)}, f32[4,768]{1,0:T(4,128)S(1)}, u32[]{:S(2)}, u32[]{:S(2)}) collective-permute-start(f32[4,768]{1,0:T(4,128)S(1)} %pad_maximum_fusion.1), channel_id=1, source_target_pairs={{0,8},{4,12},{8,0},{12,4},{1,9},{5,13},{9,1},{13,5},{2,10},{6,14},... | collective-permute-start | bytes 36872 | tf_op jit(solution)/shard_map/ppermute | solution.py:25
  221.6 4.9 %collective-permute-start.16 = (f32[4,768]{1,0:T(4,128)S(1)}, f32[4,768]{1,0:T(4,128)S(1)}, u32[]{:S(2)}, u32[]{:S(2)}) collective-permute-start(f32[4,768]{1,0:T(4,128)S(1)} %pad_maximum_fusion.1), channel_id=1, source_target_pairs={{0,4},{4,8},{8,12},{12,0},{1,5},{5,9},{9,13},{13,1},{2,6},{6,10},{... | collective-permute-start | bytes 36872 | tf_op jit(solution)/shard_map/ppermute | solution.py:25
  (11 other events, 15.8 us)
Sparse Core Ops, SparseCore 0:
  16.8 147.1 all-gather.2
where the time goes:
time: 236 us; the launch traced here: 235 us
  waiting for transfers between devices  127 us (54%)
  Pallas kernels  40.4 us (17%)
  starting transfers between devices  31.1 us (13%)
  local copies, waits for them, and re-layouts  14.1 us (6%)
  between operations  13.7 us (6%)
  other arithmetic  7.8 us (3%)
    ppermute x15, waiting for transfers between devices, shift(): return lax.ppermute(block, axis, ring(count, step))  74.7 us
    all_gather x1, waiting for transfers between devices, body(): weight = lax.all_gather(rest, ('zh', 'y', 'zl', 'co'))  25.8 us
    pallas_call x1, Pallas kernels, layer(): pl.pallas_call(layer_kernel, out_shape=[jax.ShapeDtypeStruct((4, local, r...  24.7 us
    all_to_all x1, waiting for transfers between devices, body(): landed = lax.all_to_all(parts, 'tp', 0, 0, tiled=True).astype(F32)  24.6 us
    ppermute x15, starting transfers between devices, shift(): return lax.ppermute(block, axis, ring(count, step))  16.7 us
    pallas_call x1, Pallas kernels, attention(): pl.pallas_call(attention_kernel, out_shape=jax.ShapeDtypeStruct(query.sha...  9.55 us
    all_to_all x1, starting transfers between devices, body(): qkv_z = lax.all_to_all(everywhere, Z, 0, 0, tiled=True)  8.47 us
    unnamed x48, local copies, waits for them, and re-layouts  7.64 us
  transfers between devices with their start and end apart: 20, of which 18 were waited for; matrix products, arithmetic and copies ran while one was open for 5% of the time, Pallas kernels for 7%

commit v1 on v0

--- a/solution.py
+++ b/solution.py
@@ -1,3 +1,4 @@
+import functools
 import math
 
 import jax
@@ -29,11 +30,8 @@
     return lax.ppermute(block, "co", [(0, 1), (1, 0)])
 
 
-SHARDS = 64
 SHARD = 20
-PADDED = 24
-WIDE = SHARDS * PADDED
-GROUP = 16 * PADDED
+RING_ORDER = (0, 7, 1, 6, 2, 5, 3, 4)
 SMALL = pl.BlockSpec(memory_space=pltpu.SMEM)
 NEAR = pl.BlockSpec(memory_space=pltpu.VMEM)
 FAR = pl.BlockSpec(memory_space=pl.ANY)
@@ -47,9 +45,39 @@
     return list(lax.optimization_barrier((tuple(blocks), earlier))[0])
 
 
-def strip(block):
-    shards = [block[shard * PADDED : shard * PADDED + SHARD] for shard in range(16)]
-    return jnp.concatenate(shards, axis=0)
+def order_kernel(which, aways, place_ref, *refs):
+    count = len(aways)
+    blocks, whole_ref, held = refs[:count], refs[count], refs[count + 1]
+    me = place_ref[which]
+    for block, away in zip(blocks, aways):
+        held[(me + away) % count] = block[...]
+    whole_ref[...] = jnp.concatenate([held[slot] for slot in range(count)], axis=0)
+
+
+def in_order(spot, which, blocks, aways):
+    rows, cols = blocks[0].shape
+    count = len(blocks)
+    return pl.pallas_call(
+        functools.partial(order_kernel, which, aways),
+        out_shape=jax.ShapeDtypeStruct((count * rows, cols), BF16),
+        in_specs=[SMALL] + [NEAR] * count,
+        out_specs=NEAR,
+        scratch_shapes=[pltpu.VMEM((count, rows, cols), BF16)],
+        cost_estimate=pl.CostEstimate(flops=0, bytes_accessed=count * rows * cols * 4, transcendentals=0),
+        name="in_order",
+    )(spot, *blocks)
+
+
+def ring_z(start, waits):
+    ahead = behind = start
+    blocks = [start]
+    for step in range(1, 5):
+        ahead = shift(ahead, Z, 8, 1)
+        if step < 4:
+            behind = shift(behind, Z, 8, -1)
+            ahead, behind = after([ahead, behind], *waits.get(step, ()))
+            blocks += [ahead, behind]
+    return blocks + [ahead]
 
 
 def chunk_squares(read, count, width):
@@ -124,29 +152,22 @@
     return lax.cummax(jnp.where(segment != earlier, order, jnp.zeros_like(order)))
 
 
-def project_kernel(
-    place_ref, x0_ref, x1_ref, x2_ref, x3_ref, w0_ref, w1_ref, w2_ref, w3_ref, far_ref, gain_ref, cos_ref, sin_ref,
-    query_ref, own_ref, features_ref, size_ref, held, weight, result,
-):
-    tp, core, spot_y = place_ref[0], place_ref[1], place_ref[2]
-    rows = query_ref.shape[1]
-    local = query_ref.shape[0]
-    held[...] = jnp.zeros_like(held)
-    for away, ref in enumerate((x0_ref, x1_ref, x2_ref, x3_ref)):
-        for shard in range(16):
-            held[(tp + away) % 4, shard, :SHARD] = ref[shard * SHARD : (shard + 1) * SHARD]
-    for away, ref in enumerate((w0_ref, w1_ref, w2_ref, w3_ref)):
-        y = (spot_y + away) % 4
-        for z in range(8):
-            weight[z // 2, y, z % 2, core] = ref[z]
-            weight[z // 2, y, z % 2, 1 - core] = far_ref[away, z]
-    features_ref[...] = held[...].reshape(WIDE, rows)
+def project_kernel(place_ref, *refs):
+    x_refs, w_refs, gain_ref, cos_ref, sin_ref = refs[:4], refs[4:12], *refs[12:15]
+    query_ref, own_ref, features_ref, size_ref, weight, result = refs[15:]
+    tp, ring = place_ref[0], place_ref[2]
+    local, rows = query_ref.shape
+    for away, ref in enumerate(x_refs):
+        block = (tp + away) % 4
+        features_ref[pl.ds(pl.multiple_of(block * local, local), local), :] = ref[...]
+    for away, ref in zip(RING_ORDER, w_refs):
+        weight[(ring + away) % 8] = ref[...]
     size = lax.rsqrt(
-        chunk_squares(lambda i: features_ref[pl.ds(pl.multiple_of(i * 128, 128), 128), :], WIDE // 128, rows) + EPS
+        chunk_squares(lambda i: features_ref[pl.ds(pl.multiple_of(i * 128, 128), 128), :], D // 128, rows) + EPS
     )
     size_ref[...] = size
     for kind in range(3):
-        part = weight[..., kind * local : (kind + 1) * local].reshape(WIDE, local)
+        part = weight[..., kind * local : (kind + 1) * local].reshape(D, local)
         turned = jnp.transpose(part)
         wide = turned.astype(F32)
         length = lax.rsqrt(jnp.sum(wide * wide, axis=1, keepdims=True) + EPS)
@@ -172,58 +193,61 @@
     lax.fori_loop(0, local // HD, one_head, 0)
 
 
-def project(spot, blocks, near, far, gain, cosine, sine):
+def project(spot, blocks, weights, gain, cosine, sine):
     local, rows = blocks[0].shape
     return pl.pallas_call(
         project_kernel,
         out_shape=[
             jax.ShapeDtypeStruct((local, rows), BF16),
             jax.ShapeDtypeStruct((2 * local, rows), BF16),
-            jax.ShapeDtypeStruct((WIDE, rows), BF16),
+            jax.ShapeDtypeStruct((D, rows), BF16),
             jax.ShapeDtypeStruct((1, rows), F32),
         ],
-        in_specs=[SMALL] + [NEAR] * 12,
+        in_specs=[SMALL] + [NEAR] * 15,
         out_specs=[NEAR] * 4,
         scratch_shapes=[
-            pltpu.VMEM((4, 16, PADDED, rows), BF16),
-            pltpu.VMEM((4, 4, 2, 2, PADDED, 3 * local), BF16),
+            pltpu.VMEM((8, 160, 3 * local), BF16),
             pltpu.VMEM((3 * local, rows), F32),
         ],
         compiler_params=pltpu.CompilerParams(vmem_limit_bytes=40 * 2**20),
         cost_estimate=pl.CostEstimate(flops=1_900_000_000, bytes_accessed=12_000_000, transcendentals=0),
         name="project",
-    )(spot, *blocks, *near, far, gain, cosine, sine)
-
-
-def layer_kernel(
-    place_ref, a0_ref, a1_ref, a2_ref, a3_ref, features_ref, size_ref, attn_ref, up_ref, gate_ref, weight_ref,
-    part_ref, mixed_ref, attended, state, turned, inner, weight, sems,
-):
-    tp = place_ref[0]
-    rows = features_ref.shape[1]
+    )(spot, *blocks, *weights, gain, cosine, sine)
+
+
+def layer_kernel(place_ref, *refs):
+    a_refs, features_ref, size_ref, attn_ref, up_ref, gate_ref = refs[:4], *refs[4:9]
+    near_refs, far_refs = refs[9:17], refs[17:25]
+    part_ref, mixed_ref, attended, state, turned, inner, weight, sems = refs[25:]
+    tp, core, ring = place_ref[0], place_ref[1], place_ref[2]
+    local, rows = a_refs[0].shape
     hidden = up_ref.shape[1]
     bounds = (0, D, D + 2 * hidden, D + 3 * hidden)
     copies = []
     for kind in range(3):
         cols = slice(bounds[kind], bounds[kind + 1])
-        copies.append(pltpu.make_async_copy(weight_ref.at[:, :, cols], weight.at[:, :, cols], sems.at[kind]))
-        copies[kind].start()
-    for away, ref in enumerate((a0_ref, a1_ref, a2_ref, a3_ref)):
-        attended[away * 320 : (away + 1) * 320] = ref[...]
-    copies[0].wait()
+        for side, blocks in ((core, near_refs), (1 - core, far_refs)):
+            for away, block in zip(RING_ORDER, blocks):
+                target = weight.at[(ring + away) % 8, side, :, cols]
+                copies.append(pltpu.make_async_copy(block.at[:, cols], target, sems.at[len(copies)]))
+                copies[-1].start()
+    for away, ref in enumerate(a_refs):
+        attended[away * local : (away + 1) * local] = ref[...]
+    for copy in copies[:16]:
+        copy.wait()
 
     def group(index, cols):
-        return weight[pl.ds(16 * index, 16), :, cols].reshape(GROUP, -1)
+        return weight[pl.ds(2 * index, 2), :, :, cols].reshape(local, -1)
 
     def eighth(index):
-        return weight[pl.ds(8 * index, 8), :, :D].reshape(8 * PADDED, D)
+        return weight[index, :, :, :D].reshape(D // 8, D)
 
     out_length = lax.rsqrt(chunk_squares(eighth, 8, D) + EPS)
 
     def project_out(index, total):
         left = (group(index, slice(0, D)).astype(F32) * out_length).astype(BF16)
         block = jnp.dot(left, attended[...], preferred_element_type=F32)
-        state[pl.ds(pl.multiple_of(index * GROUP, GROUP), GROUP), :] = block
+        state[pl.ds(pl.multiple_of(index * local, local), local), :] = block
         return total + jnp.sum((block * block).reshape(-1, 8, rows), axis=0)
 
     zero = jnp.zeros((8, rows), F32)
@@ -238,7 +262,7 @@
         state[span, :] = mixed
         return total + jnp.sum((mixed * mixed).reshape(-1, 8, rows), axis=0)
 
-    total = jnp.sum(lax.fori_loop(0, WIDE // 128, mix, zero), axis=0, keepdims=True)
+    total = jnp.sum(lax.fori_loop(0, D // 128, mix, zero), axis=0, keepdims=True)
     scale = lax.rsqrt(total + EPS)
 
     def turn(index, carry):
@@ -248,13 +272,14 @@
         turned[:, span] = jnp.transpose(mixed).astype(BF16)
         return carry
 
-    lax.fori_loop(0, WIDE // 128, turn, 0)
-    mixed_ref[...] = strip(state[pl.ds(pl.multiple_of(tp * GROUP, GROUP), GROUP), :])
-    copies[1].wait()
-    copies[2].wait()
+    lax.fori_loop(0, D // 128, turn, 0)
+    mixed_ref[...] = state[pl.ds(pl.multiple_of(tp * local, local), local), :]
+    for copy in copies[16:]:
+        copy.wait()
 
     def columns(start, index):
-        return weight[:, :, pl.ds(pl.multiple_of(start + index * BLOCK, BLOCK), BLOCK)].reshape(WIDE, BLOCK)
+        cols = pl.ds(pl.multiple_of(start + index * BLOCK, BLOCK), BLOCK)
+        return weight[..., cols].reshape(D, BLOCK)
 
     def length(part):
         wide = part.astype(F32)
@@ -279,13 +304,13 @@
             (((1,), (1,)), ((), ())),
             preferred_element_type=F32,
         )
-        part_ref[index] = strip(block).astype(BF16)
+        part_ref[index] = block.astype(BF16)
         return carry
 
     lax.fori_loop(0, 4, contract, 0)
 
 
-def layer(spot, attended, features, size, attn_step, up_scale, gate_scale, weight):
+def layer(spot, attended, features, size, attn_step, up_scale, gate_scale, near, far):
     local, rows = attended[0].shape
     hidden = up_scale.shape[1]
     return pl.pallas_call(
@@ -294,20 +319,32 @@
             jax.ShapeDtypeStruct((4, local, rows), BF16),
             jax.ShapeDtypeStruct((local, rows), F32),
         ],
-        in_specs=[SMALL] + [NEAR] * 9 + [FAR],
+        in_specs=[SMALL] + [NEAR] * 9 + [FAR] * 16,
         out_specs=[NEAR] * 2,
         scratch_shapes=[
             pltpu.VMEM((D, rows), BF16),
-            pltpu.VMEM((WIDE, rows), F32),
-            pltpu.VMEM((rows, WIDE), BF16),
+            pltpu.VMEM((D, rows), F32),
+            pltpu.VMEM((rows, D), BF16),
             pltpu.VMEM((rows, hidden), BF16),
-            pltpu.VMEM((SHARDS, PADDED, D + 3 * hidden), BF16),
-            pltpu.SemaphoreType.DMA((3,)),
+            pltpu.VMEM((8, 2, 80, D + 3 * hidden), BF16),
+            pltpu.SemaphoreType.DMA((48,)),
         ],
         compiler_params=pltpu.CompilerParams(vmem_limit_bytes=56 * 2**20),
         cost_estimate=pl.CostEstimate(flops=10_000_000_000, bytes_accessed=20_000_000, transcendentals=1_000_000),
         name="layer",
-    )(spot, *attended, features, size, attn_step, up_scale, gate_scale, weight)
+    )(spot, *attended, features, size, attn_step, up_scale, gate_scale, *near, *far)
+
+
+def kernel_order(array):
+    shape = array.shape
+    parts = array.reshape((shape[0] // 320, 4, 2, 2, SHARD) + shape[1:])
+    return jnp.moveaxis(parts, 1, 3).reshape(shape)
+
+
+def outer_order(array):
+    shape = array.shape
+    parts = array.reshape((shape[0] // 320, 2, 2, 4, SHARD) + shape[1:])
+    return jnp.moveaxis(parts, 3, 1).reshape(shape)
 
 
 def body(
@@ -330,23 +367,17 @@
     core = lax.axis_index("co")
     spot_y = lax.axis_index("y")
     piece = lax.axis_index("zl") * 2 + core
-    spot = jnp.stack([tp, core, spot_y]).astype(jnp.int32)
-
-    def pad(shard):
-        return jnp.pad(shard, ((0, PADDED - SHARD), (0, 0)))
-
-    out_rows = four_blocks(out_weight.T.astype(BF16), "tp")
-    wide = gate_up_weight.astype(BF16).reshape(SHARD, 2 * hidden)
-    rest = pad(jnp.concatenate(out_rows + [wide, down_weight.T.astype(BF16)], axis=1))
-    weight = lax.all_gather(rest, ("zh", "y", "zl", "co"))
-
-    own_tokens, qkv = after([tokens[0].T, pad(qkv_weight.astype(BF16).reshape(SHARD, 3 * local))], rest)
-    blocks = four_blocks(own_tokens, "tp")
-    everywhere = jnp.broadcast_to(qkv[None], (8,) + qkv.shape)
-    qkv_z = lax.all_to_all(everywhere, Z, 0, 0, tiled=True)
-    (qkv_z,) = after([qkv_z], *blocks)
-    qkv_near = four_blocks(qkv_z, "y")
-    qkv_far = swap_core(jnp.stack(qkv_near))
+    spot_z = lax.axis_index("zh") * 2 + lax.axis_index("zl")
+    spot = jnp.stack([tp, core, spot_z, spot_y]).astype(jnp.int32)
+
+    qkv = qkv_weight.astype(BF16).reshape(SHARD, 3 * local)
+    qkv_y = in_order(spot, 3, four_blocks(qkv, "y"), (0, 1, 2, 3))
+    blocks = four_blocks(kernel_order(tokens[0].T), "tp")
+    qkv_far = swap_core(qkv_y)
+    first = core == 0
+    qkv_both = jnp.concatenate(
+        [jnp.where(first, qkv_y, qkv_far), jnp.where(first, qkv_far, qkv_y)], axis=0
+    )
 
     starts = stream_starts(segment_ids[0])
     own_first = piece * rows
@@ -354,27 +385,34 @@
     position = own_first + jnp.arange(rows, dtype=jnp.int32) - own_start
     frequency = jnp.exp(-math.log(10000.0) * jnp.arange(HD // 2, dtype=F32) * 2.0 / HD)
     angles = frequency[:, None] * position.astype(F32)[None]
-    query, own, features, size = project(
-        spot, blocks, qkv_near, qkv_far, qk_scale[:, None], jnp.cos(angles), jnp.sin(angles)
-    )
     window = 2 * BLOCK
+    cosine, sine = jnp.cos(angles), jnp.sin(angles)
+    key_start = (own_start - own_first + window)[None]
+    gain = qk_scale[:, None]
+    attn_step = kernel_order(attn_rate)[:, None]
+    step_block = lax.dynamic_slice_in_dim(kernel_order(mlp_rate), tp * local, local)[:, None]
+
+    out_rows = four_blocks(out_weight.T.astype(BF16), "tp")
+    wide = gate_up_weight.astype(BF16).reshape(SHARD, 2 * hidden)
+    rest = jnp.concatenate(out_rows + [wide, down_weight.T.astype(BF16)], axis=1)
+    (rest,) = after([rest], qkv_y)
+    rest_y = in_order(spot, 3, four_blocks(rest, "y"), (0, 1, 2, 3))
+
+    waits = {1: (blocks[1], blocks[3], cosine, sine, key_start, gain), 2: (blocks[2], attn_step, step_block)}
+    qkv_blocks = ring_z(qkv_both, waits)
+    (rest_y,) = after([rest_y], *qkv_blocks)
+    query, own, features, size = project(spot, blocks, qkv_blocks, gain, cosine, sine)
     before = lax.ppermute(own[:, rows - window :], ("zl", "co"), [(i, i + 1) for i in range(3)])
-    attended = attention((own_start - own_first + window)[None], query, before, own)
-
+    attended = attention(key_start, query, before, own)
+    everyone = four_blocks(attended, "tp")
+    near = ring_z(rest_y, {1: (query,), 2: (attended,), 3: (everyone[1], everyone[3])})
+    far = [swap_core(block) for block in near]
     parts, mixed = layer(
-        spot,
-        four_blocks(attended, "tp"),
-        features,
-        size,
-        jnp.pad(attn_rate.reshape(SHARDS, SHARD), ((0, 0), (0, PADDED - SHARD))).reshape(WIDE, 1),
-        up_scale[None],
-        gate_scale[None],
-        weight,
+        spot, everyone, features, size, attn_step, up_scale[None], gate_scale[None], near, far
     )
     landed = lax.all_to_all(parts, "tp", 0, 0, tiled=True).astype(F32)
     mlp_block = landed[0] + landed[1] + landed[2] + landed[3]
 
-    step_block = lax.dynamic_slice_in_dim(mlp_rate, tp * local, local)[:, None]
     kept = mixed - step_block * mixed
     moved = step_block * mlp_block
     sums = jnp.stack(
@@ -390,7 +428,7 @@
     length = jnp.maximum(sums[1] + 2.0 * pull * sums[2] + pull * pull * sums[3], 0.0)
     final = math.sqrt(D) * lax.rsqrt(length + EPS)
     result = ((kept + pull[None] * moved) * final[None]).astype(BF16)
-    return result.T[None]
+    return outer_order(result).T[None]
 
 
 def solution(mesh):

time: 236 us -> 249 us (1.055); the launches traced: 235 us -> 244 us
  starting transfers between devices: 31.1 us -> 77.7 us
  waiting for transfers between devices: 127 us -> 102 us
  between operations: 13.7 us -> 0.74 us
    ppermute x15 -> x32, starting transfers between devices: 16.7 us -> 71 us  [shift(): return lax.ppermute(block, axis, ring(count, step))]
    all_gather x1 -> x0, waiting for transfers between devices: 25.8 us -> none  [body(): weight = lax.all_gather(rest, ('zh', 'y', 'zl', 'co'))]
    all_to_all x1 -> x0, starting transfers between devices: 8.47 us -> none  [body(): qkv_z = lax.all_to_all(everywhere, Z, 0, 0, tiled=True)]
    pallas_call x0 -> x2, Pallas kernels: none -> 4.09 us  [in_order(): pl.pallas_call(functools.partial(order_kernel, which, aways), out_shape=j...]
    unnamed x48 -> x66, local copies, waits for them, and re-layouts: 7.64 us -> 8.35 us
    ppermute x15 -> x32, waiting for transfers between devices: 74.7 us -> 74 us  [shift(): return lax.ppermute(block, axis, ring(count, step))]
  transfers between devices with their start and end apart: 20 -> 43, of which waited for: 18 -> 24; matrix products, arithmetic and copies ran while one was open for 5% -> 5% of each run, Pallas kernels for 7% -> 8%
where the time goes in v1:
time: 249 us; the launch traced here: 244 us
  waiting for transfers between devices  102 us (41%)
  starting transfers between devices  77.7 us (31%)
  Pallas kernels  40.9 us (16%)
  local copies, waits for them, and re-layouts  16 us (6%)
  other arithmetic  7.29 us (3%)
    ppermute x32, waiting for transfers between devices, shift(): return lax.ppermute(block, axis, ring(count, step))  74 us
    ppermute x32, starting transfers between devices, shift(): return lax.ppermute(block, axis, ring(count, step))  71 us
    all_to_all x1, waiting for transfers between devices, body(): landed = lax.all_to_all(parts, 'tp', 0, 0, tiled=True).astype(F32)  25.5 us
    pallas_call x1, Pallas kernels, layer(): pl.pallas_call(layer_kernel, out_shape=[jax.ShapeDtypeStruct((4, local, r...  22.3 us
    pallas_call x1, Pallas kernels, attention(): pl.pallas_call(attention_kernel, out_shape=jax.ShapeDtypeStruct(query.sha...  9.43 us
    unnamed x66, local copies, waits for them, and re-layouts  8.35 us
    pallas_call x1, Pallas kernels, project(): pl.pallas_call(project_kernel, out_shape=[jax.ShapeDtypeStruct((local, ro...  5.03 us
  transfers between devices with their start and end apart: 43, of which 24 were waited for; matrix products, arithmetic and copies ran while one was open for 5% of the time, Pallas kernels for 8%

profile of v1, /device:TPU:16, one launch (start us, length us, event | category | flops | bytes accessed | tf_op | source)
XLA Modules:
  0.0 244.2 jit_solution(1489742309121691785)
XLA Ops:
  1.6 2.9 %collective-permute-start.4 = (bf16[20,960]{1,0:T(8,128)(2,1)S(1)}, bf16[20,960]{1,0:T(8,128)(2,1)S(1)}, u32[]{:S(2)}, u32[]{:S(2)}) collective-permute-start(bf16[20,960]{1,0:T(8,128)(2,1)S(1)} %reshape.58.refs_0_), channel_id=1, source_target_pairs={{0,32},{16,48},{32,0},{48,16},{1,33},{17,49},{33,1},{49,17},{2,34}... | collective-permute-start | bytes 115208 | tf_op jit(solution)/shard_map/ppermute | solution.py:26
  18.8 2.0 collective-permute-start.7
  20.8 4.0 %collective-permute-start.8 = (bf16[160,960]{1,0:T(8,128)(2,1)S(1)}, bf16[160,960]{1,0:T(8,128)(2,1)S(1)}, u32[]{:S(2)}, u32[]{:S(2)}) collective-permute-start(bf16[160,960]{1,0:T(8,128)(2,1)S(1)} %pad_maximum_fusion.refs_4_), channel_id=1, source_target_pairs={{0,194},{2,0},{64,2},{66,64},{128,66},{130,128},{192,130},{194,192... | collective-permute-start | bytes 921608 | tf_op jit(solution)/shard_map/ppermute | solution.py:26
  25.3 3.9 %collective-permute-done.refs_1_ = bf16[320,768]{1,0:T(8,128)(2,1)S(1)} collective-permute-done((bf16[320,768]{1,0:T(8,128)(2,1)S(1)}, bf16[320,768]{1,0:T(8,128)(2,1)S(1)}, u32[]{:S(2)}, u32[]{:S(2)}) %collective-permute-start) | collective-permute-done | bytes 491552 | tf_op jit(solution)/shard_map/ppermute | solution.py:26
  29.1 3.4 %collective-permute-done.2.refs_3_ = bf16[320,768]{1,0:T(8,128)(2,1)S(1)} collective-permute-done((bf16[320,768]{1,0:T(8,128)(2,1)S(1)}, bf16[320,768]{1,0:T(8,128)(2,1)S(1)}, u32[]{:S(2)}, u32[]{:S(2)}) %collective-permute-start.2) | collective-permute-done | bytes 491552 | tf_op jit(solution)/shard_map/ppermute | solution.py:26
  32.8 5.7 %collective-permute-start.10 = (bf16[160,960]{1,0:T(8,128)(2,1)S(1)}, bf16[160,960]{1,0:T(8,128)(2,1)}, u32[]{:S(2)}, u32[]{:S(2)}) collective-permute-start(bf16[160,960]{1,0:T(8,128)(2,1)S(1)} %collective-permute-done.8.refs_6_), channel_id=1, source_target_pairs={{0,194},{2,0},{64,2},{66,64},{128,66},{130,128},{192,130},{194,192... | collective-permute-start | bytes 921608 | tf_op jit(solution)/shard_map/ppermute | solution.py:26
  38.7 4.3 %collective-permute-done.10.refs_8_ = bf16[160,960]{1,0:T(8,128)(2,1)} collective-permute-done((bf16[160,960]{1,0:T(8,128)(2,1)S(1)}, bf16[160,960]{1,0:T(8,128)(2,1)}, u32[]{:S(2)}, u32[]{:S(2)}) %collective-permute-start.10) | collective-permute-done | bytes 307232 | tf_op jit(solution)/shard_map/ppermute | solution.py:26
  43.1 4.4 %collective-permute-done.9.refs_7_ = bf16[160,960]{1,0:T(8,128)(2,1)} collective-permute-done((bf16[160,960]{1,0:T(8,128)(2,1)S(1)}, bf16[160,960]{1,0:T(8,128)(2,1)}, u32[]{:S(2)}, u32[]{:S(2)}) %collective-permute-start.9) | collective-permute-done | bytes 307232 | tf_op jit(solution)/shard_map/ppermute | solution.py:26
  47.4 3.2 %collective-permute-start.12 = (bf16[160,960]{1,0:T(8,128)(2,1)}, bf16[160,960]{1,0:T(8,128)(2,1)S(1)}, u32[]{:S(2)}, u32[]{:S(2)}) collective-permute-start(bf16[160,960]{1,0:T(8,128)(2,1)} %collective-permute-done.10.refs_8_), channel_id=1, source_target_pairs={{0,194},{2,0},{64,2},{66,64},{128,66},{130,128},{192,130},{194,192... | collective-permute-start | bytes 921608 | tf_op jit(solution)/shard_map/ppermute | solution.py:26
  50.8 2.2 collective-permute-start.19
  53.2 3.7 %collective-permute-done.11.refs_9_ = bf16[160,960]{1,0:T(8,128)(2,1)} collective-permute-done((bf16[160,960]{1,0:T(8,128)(2,1)}, bf16[160,960]{1,0:T(8,128)(2,1)}, u32[]{:S(2)}, u32[]{:S(2)}) %collective-permute-start.11) | collective-permute-done | bytes 307232 | tf_op jit(solution)/shard_map/ppermute | solution.py:26
  63.7 3.4 %collective-permute-done.21.refs_1_ = bf16[20,5120]{1,0:T(8,128)(2,1)} collective-permute-done((bf16[20,5120]{1,0:T(8,128)(2,1)}, bf16[20,5120]{1,0:T(8,128)(2,1)}, u32[]{:S(2)}, u32[]{:S(2)}) %collective-permute-start.21) | collective-permute-done | bytes 204832 | tf_op jit(solution)/shard_map/ppermute | solution.py:26
  67.1 2.5 %collective-permute-done.22.refs_2_ = bf16[20,5120]{1,0:T(8,128)(2,1)} collective-permute-done((bf16[20,5120]{1,0:T(8,128)(2,1)}, bf16[20,5120]{1,0:T(8,128)(2,1)}, u32[]{:S(2)}, u32[]{:S(2)}) %collective-permute-start.22) | collective-permute-done | bytes 204832 | tf_op jit(solution)/shard_map/ppermute | solution.py:26
  69.6 2.5 %collective-permute-done.23.refs_3_ = bf16[20,5120]{1,0:T(8,128)(2,1)} collective-permute-done((bf16[20,5120]{1,0:T(8,128)(2,1)}, bf16[20,5120]{1,0:T(8,128)(2,1)}, u32[]{:S(2)}, u32[]{:S(2)}) %collective-permute-start.23) | collective-permute-done | bytes 204832 | tf_op jit(solution)/shard_map/ppermute | solution.py:26
  72.1 2.5 %in_order.3.refs_9_ = bf16[80,5120]{1,0:T(8,128)(2,1)} custom-call(s32[4]{0:T(128)} %pad_add_fusion.place_ref, bf16[20,5120]{1,0:T(8,128)(2,1)} %concatenate.14.refs_0_, bf16[20,5120]{1,0:T(8,128)(2,1)} %collective-permute-done.21.refs_1_, bf16[20,5120]{1,0:T(8,128)(2,1)} %collective-permute-done.22.refs_2_, bf16[20,5120]{1,0:T(8,128)(2,1)} %collective-permute-done.23.refs_3_), custom_call_target="tpu_custom_call" | custom-call | bytes 1638400 | tf_op jit(solution)/shard_map/in_order/pallas_call | solution.py:60
  81.1 5.0 %project.1 = (bf16[320,768]{1,0:T(8,128)(2,1)S(1)}, bf16[640,768]{1,0:T(8,128)(2,1)S(1)}, bf16[1280,768]{1,0:T(8,128)(2,1)S(1)}, f32[1,768]{1,0:T(1,128)S(1)}) custom-call(s32[4]{0:T(128)S(1)} %copy-done.1, bf16[320,768]{1,0:T(8,128)(2,1)S(1)} %reshape.57.refs_0_, bf16[320,768]{1,0:T(8,128)(2,1)S(1)} %collective-permute-done.refs_1_, ...), custom_call_target="tpu_custom_call" | custom-call | flops 1900000000 | bytes 12000000 | tf_op jit(solution)/shard_map/project/pallas_call | solution.py:198
  88.8 3.4 %collective-permute-done.24.refs_10_ = bf16[80,5120]{1,0:T(8,128)(2,1)} collective-permute-done((bf16[80,5120]{1,0:T(8,128)(2,1)}, bf16[80,5120]{1,0:T(8,128)(2,1)}, u32[]{:S(2)}, u32[]{:S(2)}) %collective-permute-start.24) | collective-permute-done | bytes 819232 | tf_op jit(solution)/shard_map/ppermute | solution.py:26
  92.2 2.2 collective-permute-done.25.refs_11_
  97.7 2.3 collective-permute-start.14
  101.0 9.4 %attention.1.refs_0_ = bf16[320,768]{1,0:T(8,128)(2,1)} custom-call(s32[1,768]{1,0:T(1,128)} %broadcast_in_dim.24.start_ref, bf16[320,768]{1,0:T(8,128)(2,1)} %copy-done.9, bf16[640,512]{1,0:T(8,128)(2,1)} %collective-permute-done.14.before_ref, bf16[640,768]{1,0:T(8,128)(2,1)} %copy-done), custom_call_target="tpu_custom_call" | custom-call | flops 800000000 | bytes 4000000 | tf_op jit(solution)/shard_map/attention/pallas_call | solution.py:139
  110.4 4.6 %collective-permute-done.26.refs_12_ = bf16[80,5120]{1,0:T(8,128)(2,1)S(1)} collective-permute-done((bf16[80,5120]{1,0:T(8,128)(2,1)}, bf16[80,5120]{1,0:T(8,128)(2,1)S(1)}, u32[]{:S(2)}, u32[]{:S(2)}) %collective-permute-start.26) | collective-permute-done | bytes 819232 | tf_op jit(solution)/shard_map/ppermute | solution.py:26
  115.0 13.8 %collective-permute-start.28 = (bf16[80,5120]{1,0:T(8,128)(2,1)S(1)}, bf16[80,5120]{1,0:T(8,128)(2,1)S(1)}, u32[]{:S(2)}, u32[]{:S(2)}) collective-permute-start(bf16[80,5120]{1,0:T(8,128)(2,1)S(1)} %collective-permute-done.26.refs_12_), channel_id=1, source_target_pairs={{0,2},{2,64},{64,66},{66,128},{128,130},{130,192},{192,194},{194,0... | collective-permute-start | bytes 2457608 | tf_op jit(solution)/shard_map/ppermute | solution.py:26
  128.8 9.7 %collective-permute-start.29 = (bf16[80,5120]{1,0:T(8,128)(2,1)}, bf16[80,5120]{1,0:T(8,128)(2,1)}, u32[]{:S(2)}, u32[]{:S(2)}) collective-permute-start(bf16[80,5120]{1,0:T(8,128)(2,1)} %collective-permute-done.27.refs_13_), channel_id=1, source_target_pairs={{0,194},{2,0},{64,2},{66,64},{128,66},{130,128},{192,130},{194,192... | collective-permute-start | bytes 2457608 | tf_op jit(solution)/shard_map/ppermute | solution.py:26
  138.6 3.8 %collective-permute-start.15 = (bf16[320,768]{1,0:T(8,128)(2,1)}, bf16[320,768]{1,0:T(8,128)(2,1)S(1)}, u32[]{:S(2)}, u32[]{:S(2)}) collective-permute-start(bf16[320,768]{1,0:T(8,128)(2,1)} %attention.1.refs_0_), channel_id=1, source_target_pairs={{0,12},{4,0},{8,4},{12,8},{1,13},{5,1},{9,5},{13,9},{2,14},{6,2},{... | collective-permute-start | bytes 1474568 | tf_op jit(solution)/shard_map/ppermute | solution.py:26
  144.2 9.1 %collective-permute-done.15.refs_1_ = bf16[320,768]{1,0:T(8,128)(2,1)S(1)} collective-permute-done((bf16[320,768]{1,0:T(8,128)(2,1)}, bf16[320,768]{1,0:T(8,128)(2,1)S(1)}, u32[]{:S(2)}, u32[]{:S(2)}) %collective-permute-start.15) | collective-permute-done | bytes 491552 | tf_op jit(solution)/shard_map/ppermute | solution.py:26
  154.2 4.4 %collective-permute-done.29.refs_15_ = bf16[80,5120]{1,0:T(8,128)(2,1)} collective-permute-done((bf16[80,5120]{1,0:T(8,128)(2,1)}, bf16[80,5120]{1,0:T(8,128)(2,1)}, u32[]{:S(2)}, u32[]{:S(2)}) %collective-permute-start.29) | collective-permute-done | bytes 819232 | tf_op jit(solution)/shard_map/ppermute | solution.py:26
  162.2 11.1 %collective-permute-done.16.refs_2_ = bf16[320,768]{1,0:T(8,128)(2,1)S(1)} collective-permute-done((bf16[320,768]{1,0:T(8,128)(2,1)}, bf16[320,768]{1,0:T(8,128)(2,1)S(1)}, u32[]{:S(2)}, u32[]{:S(2)}) %collective-permute-start.16) | collective-permute-done | bytes 491552 | tf_op jit(solution)/shard_map/ppermute | solution.py:26
  173.9 5.0 %collective-permute-done.30.refs_16_ = bf16[80,5120]{1,0:T(8,128)(2,1)} collective-permute-done((bf16[80,5120]{1,0:T(8,128)(2,1)S(1)}, bf16[80,5120]{1,0:T(8,128)(2,1)}, u32[]{:S(2)}, u32[]{:S(2)}) %collective-permute-start.30) | collective-permute-done | bytes 819232 | tf_op jit(solution)/shard_map/ppermute | solution.py:26
  182.3 22.3 %layer.1 = (bf16[4,320,768]{2,1,0:T(8,128)(2,1)}, f32[320,768]{1,0:T(8,128)}) custom-call(s32[4]{0:T(128)} %pad_add_fusion.place_ref, bf16[320,768]{1,0:T(8,128)(2,1)} %attention.1.refs_0_, bf16[320,768]{1,0:T(8,128)(2,1)} %copy-done.30, bf16[320,768]{1,0:T(8,128)(2,1)} %copy-done.31, bf16[320,768]{1,0:T(8,128)(2,1)} %collective-permute-done.17.refs_3_, ...), custom_call_target="tpu_custom_call" | custom-call | flops 10000000000 | bytes 20000000 | tf_op jit(solution)/shard_map/layer/pallas_call | solution.py:316
  204.6 3.6 %all-to-all-start = ((bf16[4,320,768]{2,1,0:T(8,128)(2,1)}), bf16[4,320,768]{2,1,0:T(8,128)(2,1)S(1)}, u32[]{:S(2)}, u32[]{:S(2)}) async-start(bf16[4,320,768]{2,1,0:T(8,128)(2,1)} %get-tuple-element.44), calls=%async_computation | async-start | bytes 3932160 | tf_op jit(solution)/shard_map/all_to_all | solution.py:413
  208.6 25.5 %all-to-all-done = bf16[4,320,768]{2,1,0:T(8,128)(2,1)S(1)} async-done(((bf16[4,320,768]{2,1,0:T(8,128)(2,1)}), bf16[4,320,768]{2,1,0:T(8,128)(2,1)S(1)}, u32[]{:S(2)}, u32[]{:S(2)}) %all-to-all-start) | async-done | bytes 1966112 | tf_op jit(solution)/shard_map/all_to_all | solution.py:413
  238.8 2.7 %collective-permute-done.40 = f32[4,768]{1,0:T(4,128)S(1)} collective-permute-done((f32[4,768]{1,0:T(4,128)S(1)}, f32[4,768]{1,0:T(4,128)S(1)}, u32[]{:S(2)}, u32[]{:S(2)}) %collective-permute-start.40) | collective-permute-done | bytes 12320 | tf_op jit(solution)/shard_map/ppermute | solution.py:26
  (175 shorter events, 54.9 us)
Async XLA Ops:
  1.1 10.6 %collective-permute-start.3 = (bf16[20,960]{1,0:T(8,128)(2,1)S(1)}, bf16[20,960]{1,0:T(8,128)(2,1)S(1)}, u32[]{:S(2)}, u32[]{:S(2)}) collective-permute-start(bf16[20,960]{1,0:T(8,128)(2,1)S(1)} %reshape.58.refs_0_), channel_id=1, source_target_pairs={{0,48},{16,0},{32,16},{48,32},{1,49},{17,1},{33,17},{49,33},{2,50}... | collective-permute-start | bytes 115208 | tf_op jit(solution)/shard_map/ppermute | solution.py:26
  1.6 11.8 %collective-permute-start.4 = (bf16[20,960]{1,0:T(8,128)(2,1)S(1)}, bf16[20,960]{1,0:T(8,128)(2,1)S(1)}, u32[]{:S(2)}, u32[]{:S(2)}) collective-permute-start(bf16[20,960]{1,0:T(8,128)(2,1)S(1)} %reshape.58.refs_0_), channel_id=1, source_target_pairs={{0,32},{16,48},{32,0},{48,16},{1,33},{17,49},{33,1},{49,17},{2,34}... | collective-permute-start | bytes 115208 | tf_op jit(solution)/shard_map/ppermute | solution.py:26
  4.5 8.9 %collective-permute-start.5 = (bf16[20,960]{1,0:T(8,128)(2,1)S(1)}, bf16[20,960]{1,0:T(8,128)(2,1)S(1)}, u32[]{:S(2)}, u32[]{:S(2)}) collective-permute-start(bf16[20,960]{1,0:T(8,128)(2,1)S(1)} %reshape.58.refs_0_), channel_id=1, source_target_pairs={{0,16},{16,32},{32,48},{48,0},{1,17},{17,33},{33,49},{49,1},{2,18}... | collective-permute-start | bytes 115208 | tf_op jit(solution)/shard_map/ppermute | solution.py:26
  7.2 22.0 %collective-permute-start = (bf16[320,768]{1,0:T(8,128)(2,1)S(1)}, bf16[320,768]{1,0:T(8,128)(2,1)S(1)}, u32[]{:S(2)}, u32[]{:S(2)}) collective-permute-start(bf16[320,768]{1,0:T(8,128)(2,1)S(1)} %reshape.57.refs_0_), channel_id=1, source_target_pairs={{0,12},{4,0},{8,4},{12,8},{1,13},{5,1},{9,5},{13,9},{2,14},{6,2},{... | collective-permute-start | bytes 1474568 | tf_op jit(solution)/shard_map/ppermute | solution.py:26
  8.7 23.9 %collective-permute-start.2 = (bf16[320,768]{1,0:T(8,128)(2,1)S(1)}, bf16[320,768]{1,0:T(8,128)(2,1)S(1)}, u32[]{:S(2)}, u32[]{:S(2)}) collective-permute-start(bf16[320,768]{1,0:T(8,128)(2,1)S(1)} %reshape.57.refs_0_), channel_id=1, source_target_pairs={{0,4},{4,8},{8,12},{12,0},{1,5},{5,9},{9,13},{13,1},{2,6},{6,10},{... | collective-permute-start | bytes 1474568 | tf_op jit(solution)/shard_map/ppermute | solution.py:26
  11.7 27.0 %collective-permute-start.1 = (bf16[320,768]{1,0:T(8,128)(2,1)S(1)}, bf16[320,768]{1,0:T(8,128)(2,1)S(1)}, u32[]{:S(2)}, u32[]{:S(2)}) collective-permute-start(bf16[320,768]{1,0:T(8,128)(2,1)S(1)} %reshape.57.refs_0_), channel_id=1, source_target_pairs={{0,8},{4,12},{8,0},{12,4},{1,9},{5,13},{9,1},{13,5},{2,10},{6,14},... | collective-permute-start | bytes 1474568 | tf_op jit(solution)/shard_map/ppermute | solution.py:26
  18.8 13.9 %collective-permute-start.7 = (bf16[160,960]{1,0:T(8,128)(2,1)S(1)}, bf16[160,960]{1,0:T(8,128)(2,1)S(1)}, u32[]{:S(2)}, u32[]{:S(2)}) collective-permute-start(bf16[160,960]{1,0:T(8,128)(2,1)S(1)} %pad_maximum_fusion.refs_4_), channel_id=1, source_target_pairs={{0,2},{2,64},{64,66},{66,128},{128,130},{130,192},{192,194},{194,0... | collective-permute-start | bytes 921608 | tf_op jit(solution)/shard_map/ppermute | solution.py:26
  20.8 12.0 %collective-permute-start.8 = (bf16[160,960]{1,0:T(8,128)(2,1)S(1)}, bf16[160,960]{1,0:T(8,128)(2,1)S(1)}, u32[]{:S(2)}, u32[]{:S(2)}) collective-permute-start(bf16[160,960]{1,0:T(8,128)(2,1)S(1)} %pad_maximum_fusion.refs_4_), channel_id=1, source_target_pairs={{0,194},{2,0},{64,2},{66,64},{128,66},{130,128},{192,130},{194,192... | collective-permute-start | bytes 921608 | tf_op jit(solution)/shard_map/ppermute | solution.py:26
  32.8 10.3 %collective-permute-start.10 = (bf16[160,960]{1,0:T(8,128)(2,1)S(1)}, bf16[160,960]{1,0:T(8,128)(2,1)}, u32[]{:S(2)}, u32[]{:S(2)}) collective-permute-start(bf16[160,960]{1,0:T(8,128)(2,1)S(1)} %collective-permute-done.8.refs_6_), channel_id=1, source_target_pairs={{0,194},{2,0},{64,2},{66,64},{128,66},{130,128},{192,130},{194,192... | collective-permute-start | bytes 921608 | tf_op jit(solution)/shard_map/ppermute | solution.py:26
  38.5 9.0 %collective-permute-start.9 = (bf16[160,960]{1,0:T(8,128)(2,1)S(1)}, bf16[160,960]{1,0:T(8,128)(2,1)}, u32[]{:S(2)}, u32[]{:S(2)}) collective-permute-start(bf16[160,960]{1,0:T(8,128)(2,1)S(1)} %collective-permute-done.7.refs_5_), channel_id=1, source_target_pairs={{0,2},{2,64},{64,66},{66,128},{128,130},{130,192},{192,194},{194,0... | collective-permute-start | bytes 921608 | tf_op jit(solution)/shard_map/ppermute | solution.py:26
  47.4 9.5 %collective-permute-start.11 = (bf16[160,960]{1,0:T(8,128)(2,1)}, bf16[160,960]{1,0:T(8,128)(2,1)}, u32[]{:S(2)}, u32[]{:S(2)}) collective-permute-start(bf16[160,960]{1,0:T(8,128)(2,1)} %collective-permute-done.9.refs_7_), channel_id=1, source_target_pairs={{0,2},{2,64},{64,66},{66,128},{128,130},{130,192},{192,194},{194,0... | collective-permute-start | bytes 921608 | tf_op jit(solution)/shard_map/ppermute | solution.py:26
  47.4 9.5 %collective-permute-start.12 = (bf16[160,960]{1,0:T(8,128)(2,1)}, bf16[160,960]{1,0:T(8,128)(2,1)S(1)}, u32[]{:S(2)}, u32[]{:S(2)}) collective-permute-start(bf16[160,960]{1,0:T(8,128)(2,1)} %collective-permute-done.10.refs_8_), channel_id=1, source_target_pairs={{0,194},{2,0},{64,2},{66,64},{128,66},{130,128},{192,130},{194,192... | collective-permute-start | bytes 921608 | tf_op jit(solution)/shard_map/ppermute | solution.py:26
  50.7 9.0 %collective-permute-start.18 = (bf16[20,320]{1,0:T(8,128)(2,1)S(1)}, bf16[20,320]{1,0:T(8,128)(2,1)S(1)}, u32[]{:S(2)}, u32[]{:S(2)}) collective-permute-start(bf16[20,320]{1,0:T(8,128)(2,1)S(1)} %convert_bitcast_fusion.1), channel_id=1, source_target_pairs={{0,12},{4,0},{8,4},{12,8},{1,13},{5,1},{9,5},{13,9},{2,14},{6,2},{... | collective-permute-start | bytes 38408 | tf_op jit(solution)/shard_map/ppermute | solution.py:26
  50.8 9.0 %collective-permute-start.19 = (bf16[20,320]{1,0:T(8,128)(2,1)S(1)}, bf16[20,320]{1,0:T(8,128)(2,1)S(1)}, u32[]{:S(2)}, u32[]{:S(2)}) collective-permute-start(bf16[20,320]{1,0:T(8,128)(2,1)S(1)} %convert_bitcast_fusion.1), channel_id=1, source_target_pairs={{0,8},{4,12},{8,0},{12,4},{1,9},{5,13},{9,1},{13,5},{2,10},{6,14},... | collective-permute-start | bytes 38408 | tf_op jit(solution)/shard_map/ppermute | solution.py:26
  57.7 16.9 %collective-permute-start.13 = (bf16[160,960]{1,0:T(8,128)(2,1)}, bf16[160,960]{1,0:T(8,128)(2,1)}, u32[]{:S(2)}, u32[]{:S(2)}) collective-permute-start(bf16[160,960]{1,0:T(8,128)(2,1)} %collective-permute-done.11.refs_9_), channel_id=1, source_target_pairs={{0,2},{2,64},{64,66},{66,128},{128,130},{130,192},{192,194},{194,0... | collective-permute-start | bytes 921608 | tf_op jit(solution)/shard_map/ppermute | solution.py:26
  61.5 8.1 %collective-permute-start.22 = (bf16[20,5120]{1,0:T(8,128)(2,1)}, bf16[20,5120]{1,0:T(8,128)(2,1)}, u32[]{:S(2)}, u32[]{:S(2)}) collective-permute-start(bf16[20,5120]{1,0:T(8,128)(2,1)} %concatenate.14.refs_0_), channel_id=1, source_target_pairs={{0,32},{16,48},{32,0},{48,16},{1,33},{17,49},{33,1},{49,17},{2,34}... | collective-permute-start | bytes 614408 | tf_op jit(solution)/shard_map/ppermute | solution.py:26
  63.3 8.8 %collective-permute-start.23 = (bf16[20,5120]{1,0:T(8,128)(2,1)}, bf16[20,5120]{1,0:T(8,128)(2,1)}, u32[]{:S(2)}, u32[]{:S(2)}) collective-permute-start(bf16[20,5120]{1,0:T(8,128)(2,1)} %concatenate.14.refs_0_), channel_id=1, source_target_pairs={{0,16},{16,32},{32,48},{48,0},{1,17},{17,33},{33,49},{49,1},{2,18}... | collective-permute-start | bytes 614408 | tf_op jit(solution)/shard_map/ppermute | solution.py:26
  74.6 17.6 %collective-permute-start.24 = (bf16[80,5120]{1,0:T(8,128)(2,1)}, bf16[80,5120]{1,0:T(8,128)(2,1)}, u32[]{:S(2)}, u32[]{:S(2)}) collective-permute-start(bf16[80,5120]{1,0:T(8,128)(2,1)} %in_order.3.refs_9_), channel_id=1, source_target_pairs={{0,2},{2,64},{64,66},{66,128},{128,130},{130,192},{192,194},{194,0... | collective-permute-start | bytes 2457608 | tf_op jit(solution)/shard_map/ppermute | solution.py:26
  76.4 18.0 %collective-permute-start.25 = (bf16[80,5120]{1,0:T(8,128)(2,1)}, bf16[80,5120]{1,0:T(8,128)(2,1)}, u32[]{:S(2)}, u32[]{:S(2)}) collective-permute-start(bf16[80,5120]{1,0:T(8,128)(2,1)} %in_order.3.refs_9_), channel_id=1, source_target_pairs={{0,194},{2,0},{64,2},{66,64},{128,66},{130,128},{192,130},{194,192... | collective-permute-start | bytes 2457608 | tf_op jit(solution)/shard_map/ppermute | solution.py:26
  94.4 20.6 %collective-permute-start.26 = (bf16[80,5120]{1,0:T(8,128)(2,1)}, bf16[80,5120]{1,0:T(8,128)(2,1)S(1)}, u32[]{:S(2)}, u32[]{:S(2)}) collective-permute-start(bf16[80,5120]{1,0:T(8,128)(2,1)} %collective-permute-done.24.refs_10_), channel_id=1, source_target_pairs={{0,2},{2,64},{64,66},{66,128},{128,130},{130,192},{192,194},{194,0... | collective-permute-start | bytes 2457608 | tf_op jit(solution)/shard_map/ppermute | solution.py:26
  96.0 19.0 %collective-permute-start.27 = (bf16[80,5120]{1,0:T(8,128)(2,1)}, bf16[80,5120]{1,0:T(8,128)(2,1)}, u32[]{:S(2)}, u32[]{:S(2)}) collective-permute-start(bf16[80,5120]{1,0:T(8,128)(2,1)} %collective-permute-done.25.refs_11_), channel_id=1, source_target_pairs={{0,194},{2,0},{64,2},{66,64},{128,66},{130,128},{192,130},{194,192... | collective-permute-start | bytes 2457608 | tf_op jit(solution)/shard_map/ppermute | solution.py:26
  115.0 39.2 %collective-permute-start.28 = (bf16[80,5120]{1,0:T(8,128)(2,1)S(1)}, bf16[80,5120]{1,0:T(8,128)(2,1)S(1)}, u32[]{:S(2)}, u32[]{:S(2)}) collective-permute-start(bf16[80,5120]{1,0:T(8,128)(2,1)S(1)} %collective-permute-done.26.refs_12_), channel_id=1, source_target_pairs={{0,2},{2,64},{64,66},{66,128},{128,130},{130,192},{192,194},{194,0... | collective-permute-start | bytes 2457608 | tf_op jit(solution)/shard_map/ppermute | solution.py:26
  128.8 29.8 %collective-permute-start.29 = (bf16[80,5120]{1,0:T(8,128)(2,1)}, bf16[80,5120]{1,0:T(8,128)(2,1)}, u32[]{:S(2)}, u32[]{:S(2)}) collective-permute-start(bf16[80,5120]{1,0:T(8,128)(2,1)} %collective-permute-done.27.refs_13_), channel_id=1, source_target_pairs={{0,194},{2,0},{64,2},{66,64},{128,66},{130,128},{192,130},{194,192... | collective-permute-start | bytes 2457608 | tf_op jit(solution)/shard_map/ppermute | solution.py:26
  138.6 14.7 %collective-permute-start.15 = (bf16[320,768]{1,0:T(8,128)(2,1)}, bf16[320,768]{1,0:T(8,128)(2,1)S(1)}, u32[]{:S(2)}, u32[]{:S(2)}) collective-permute-start(bf16[320,768]{1,0:T(8,128)(2,1)} %attention.1.refs_0_), channel_id=1, source_target_pairs={{0,12},{4,0},{8,4},{12,8},{1,13},{5,1},{9,5},{13,9},{2,14},{6,2},{... | collective-permute-start | bytes 1474568 | tf_op jit(solution)/shard_map/ppermute | solution.py:26
  142.4 11.9 %collective-permute-start.17 = (bf16[320,768]{1,0:T(8,128)(2,1)}, bf16[320,768]{1,0:T(8,128)(2,1)}, u32[]{:S(2)}, u32[]{:S(2)}) collective-permute-start(bf16[320,768]{1,0:T(8,128)(2,1)} %attention.1.refs_0_), channel_id=1, source_target_pairs={{0,4},{4,8},{8,12},{12,0},{1,5},{5,9},{9,13},{13,1},{2,6},{6,10},{... | collective-permute-start | bytes 1474568 | tf_op jit(solution)/shard_map/ppermute | solution.py:26
  144.2 17.9 %collective-permute-start.31 = (bf16[80,5120]{1,0:T(8,128)(2,1)S(1)}, bf16[80,5120]{1,0:T(8,128)(2,1)S(1)}, u32[]{:S(2)}, u32[]{:S(2)}) collective-permute-start(bf16[80,5120]{1,0:T(8,128)(2,1)S(1)} %copy-done.12), channel_id=1, source_target_pairs={{0,1},{1,0},{2,3},{3,2},{4,5},{5,4},{6,7},{7,6},{8,9},{9,8},{10,11... | collective-permute-start | bytes 2457608 | tf_op jit(solution)/shard_map/ppermute | solution.py:30
  153.3 20.0 %collective-permute-start.32 = (bf16[80,5120]{1,0:T(8,128)(2,1)}, bf16[80,5120]{1,0:T(8,128)(2,1)S(1)}, u32[]{:S(2)}, u32[]{:S(2)}) collective-permute-start(bf16[80,5120]{1,0:T(8,128)(2,1)} %collective-permute-done.24.refs_10_), channel_id=1, source_target_pairs={{0,1},{1,0},{2,3},{3,2},{4,5},{5,4},{6,7},{7,6},{8,9},{9,8},{10,11... | collective-permute-start | bytes 2457608 | tf_op jit(solution)/shard_map/ppermute | solution.py:30
  154.2 19.6 %collective-permute-start.33 = (bf16[80,5120]{1,0:T(8,128)(2,1)}, bf16[80,5120]{1,0:T(8,128)(2,1)S(1)}, u32[]{:S(2)}, u32[]{:S(2)}) collective-permute-start(bf16[80,5120]{1,0:T(8,128)(2,1)} %collective-permute-done.25.refs_11_), channel_id=1, source_target_pairs={{0,1},{1,0},{2,3},{3,2},{4,5},{5,4},{6,7},{7,6},{8,9},{9,8},{10,11... | collective-permute-start | bytes 2457608 | tf_op jit(solution)/shard_map/ppermute | solution.py:30
  158.6 20.3 %collective-permute-start.30 = (bf16[80,5120]{1,0:T(8,128)(2,1)S(1)}, bf16[80,5120]{1,0:T(8,128)(2,1)}, u32[]{:S(2)}, u32[]{:S(2)}) collective-permute-start(bf16[80,5120]{1,0:T(8,128)(2,1)S(1)} %collective-permute-done.28.refs_14_), channel_id=1, source_target_pairs={{0,2},{2,64},{64,66},{66,128},{128,130},{130,192},{192,194},{194,0... | collective-permute-start | bytes 2457608 | tf_op jit(solution)/shard_map/ppermute | solution.py:26
  160.4 12.9 %collective-permute-start.16 = (bf16[320,768]{1,0:T(8,128)(2,1)}, bf16[320,768]{1,0:T(8,128)(2,1)S(1)}, u32[]{:S(2)}, u32[]{:S(2)}) collective-permute-start(bf16[320,768]{1,0:T(8,128)(2,1)} %attention.1.refs_0_), channel_id=1, source_target_pairs={{0,8},{4,12},{8,0},{12,4},{1,9},{5,13},{9,1},{13,5},{2,10},{6,14},... | collective-permute-start | bytes 1474568 | tf_op jit(solution)/shard_map/ppermute | solution.py:26
  162.1 19.3 %collective-permute-start.34 = (bf16[80,5120]{1,0:T(8,128)(2,1)S(1)}, bf16[80,5120]{1,0:T(8,128)(2,1)S(1)}, u32[]{:S(2)}, u32[]{:S(2)}) collective-permute-start(bf16[80,5120]{1,0:T(8,128)(2,1)S(1)} %collective-permute-done.26.refs_12_), channel_id=1, source_target_pairs={{0,1},{1,0},{2,3},{3,2},{4,5},{5,4},{6,7},{7,6},{8,9},{9,8},{10,11... | collective-permute-start | bytes 2457608 | tf_op jit(solution)/shard_map/ppermute | solution.py:30
  204.6 29.4 %all-to-all-start = ((bf16[4,320,768]{2,1,0:T(8,128)(2,1)}), bf16[4,320,768]{2,1,0:T(8,128)(2,1)S(1)}, u32[]{:S(2)}, u32[]{:S(2)}) async-start(bf16[4,320,768]{2,1,0:T(8,128)(2,1)} %get-tuple-element.44), calls=%async_computation | async-start | bytes 3932160 | tf_op jit(solution)/shard_map/all_to_all | solution.py:413
  (43 other events, 710.0 us)

commit v2 on v1

--- a/solution.py
+++ b/solution.py
@@ -31,6 +31,8 @@
 
 
 SHARD = 20
+PADDED = 24
+WIDE = 64 * PADDED
 RING_ORDER = (0, 7, 1, 6, 2, 5, 3, 4)
 SMALL = pl.BlockSpec(memory_space=pltpu.SMEM)
 NEAR = pl.BlockSpec(memory_space=pltpu.VMEM)
@@ -68,15 +70,14 @@
     )(spot, *blocks)
 
 
-def ring_z(start, waits):
-    ahead = behind = start
+def ring_z(start, ahead, behind, waits):
     blocks = [start]
-    for step in range(1, 5):
+    for step in range(1, 4):
+        ahead, behind = after([ahead, behind], *waits.get(step, ()))
+        blocks += [ahead, behind]
         ahead = shift(ahead, Z, 8, 1)
-        if step < 4:
+        if step < 3:
             behind = shift(behind, Z, 8, -1)
-            ahead, behind = after([ahead, behind], *waits.get(step, ()))
-            blocks += [ahead, behind]
     return blocks + [ahead]
 
 
@@ -153,25 +154,31 @@
 
 
 def project_kernel(place_ref, *refs):
-    x_refs, w_refs, gain_ref, cos_ref, sin_ref = refs[:4], refs[4:12], *refs[12:15]
-    query_ref, own_ref, features_ref, size_ref, weight, result = refs[15:]
-    tp, ring = place_ref[0], place_ref[2]
+    x_refs, near_refs, far_refs, gain_ref, cos_ref, sin_ref = refs[:4], refs[4:8], refs[8], *refs[9:12]
+    query_ref, own_ref, features_ref, size_ref, held, weight, result = refs[12:]
+    tp, core, spot_y = place_ref[0], place_ref[1], place_ref[3]
     local, rows = query_ref.shape
+    held[...] = jnp.zeros_like(held)
     for away, ref in enumerate(x_refs):
         block = (tp + away) % 4
         features_ref[pl.ds(pl.multiple_of(block * local, local), local), :] = ref[...]
-    for away, ref in zip(RING_ORDER, w_refs):
-        weight[(ring + away) % 8] = ref[...]
+        for shard in range(16):
+            held[block, shard, :SHARD] = ref[shard * SHARD : (shard + 1) * SHARD]
+    for away, ref in enumerate(near_refs):
+        y = (spot_y + away) % 4
+        for z in range(8):
+            weight[z, core, y] = ref[z]
+            weight[z, 1 - core, y] = far_refs[away, z]
     size = lax.rsqrt(
         chunk_squares(lambda i: features_ref[pl.ds(pl.multiple_of(i * 128, 128), 128), :], D // 128, rows) + EPS
     )
     size_ref[...] = size
     for kind in range(3):
-        part = weight[..., kind * local : (kind + 1) * local].reshape(D, local)
+        part = weight[..., kind * local : (kind + 1) * local].reshape(WIDE, local)
         turned = jnp.transpose(part)
         wide = turned.astype(F32)
         length = lax.rsqrt(jnp.sum(wide * wide, axis=1, keepdims=True) + EPS)
-        raw = jnp.dot(turned, features_ref[...], preferred_element_type=F32)
+        raw = jnp.dot(turned, held[...].reshape(WIDE, rows), preferred_element_type=F32)
         result[kind * local : (kind + 1) * local] = raw * length * size
     half = HD // 2
     cosine, sine = cos_ref[...], sin_ref[...]
@@ -193,7 +200,7 @@
     lax.fori_loop(0, local // HD, one_head, 0)
 
 
-def project(spot, blocks, weights, gain, cosine, sine):
+def project(spot, blocks, near, far, gain, cosine, sine):
     local, rows = blocks[0].shape
     return pl.pallas_call(
         project_kernel,
@@ -203,16 +210,17 @@
             jax.ShapeDtypeStruct((D, rows), BF16),
             jax.ShapeDtypeStruct((1, rows), F32),
         ],
-        in_specs=[SMALL] + [NEAR] * 15,
+        in_specs=[SMALL] + [NEAR] * 12,
         out_specs=[NEAR] * 4,
         scratch_shapes=[
-            pltpu.VMEM((8, 160, 3 * local), BF16),
+            pltpu.VMEM((4, 16, PADDED, rows), BF16),
+            pltpu.VMEM((8, 2, 4, PADDED, 3 * local), BF16),
             pltpu.VMEM((3 * local, rows), F32),
         ],
         compiler_params=pltpu.CompilerParams(vmem_limit_bytes=40 * 2**20),
         cost_estimate=pl.CostEstimate(flops=1_900_000_000, bytes_accessed=12_000_000, transcendentals=0),
         name="project",
-    )(spot, *blocks, *weights, gain, cosine, sine)
+    )(spot, *blocks, *near, far, gain, cosine, sine)
 
 
 def layer_kernel(place_ref, *refs):
@@ -370,14 +378,10 @@
     spot_z = lax.axis_index("zh") * 2 + lax.axis_index("zl")
     spot = jnp.stack([tp, core, spot_z, spot_y]).astype(jnp.int32)
 
-    qkv = qkv_weight.astype(BF16).reshape(SHARD, 3 * local)
-    qkv_y = in_order(spot, 3, four_blocks(qkv, "y"), (0, 1, 2, 3))
+    qkv = jnp.pad(qkv_weight.astype(BF16).reshape(SHARD, 3 * local), ((0, PADDED - SHARD), (0, 0)))
+    everywhere = jnp.broadcast_to(qkv[None], (8,) + qkv.shape)
+    qkv_z = lax.all_to_all(everywhere, Z, 0, 0, tiled=True)
     blocks = four_blocks(kernel_order(tokens[0].T), "tp")
-    qkv_far = swap_core(qkv_y)
-    first = core == 0
-    qkv_both = jnp.concatenate(
-        [jnp.where(first, qkv_y, qkv_far), jnp.where(first, qkv_far, qkv_y)], axis=0
-    )
 
     starts = stream_starts(segment_ids[0])
     own_first = piece * rows
@@ -395,17 +399,18 @@
     out_rows = four_blocks(out_weight.T.astype(BF16), "tp")
     wide = gate_up_weight.astype(BF16).reshape(SHARD, 2 * hidden)
     rest = jnp.concatenate(out_rows + [wide, down_weight.T.astype(BF16)], axis=1)
-    (rest,) = after([rest], qkv_y)
     rest_y = in_order(spot, 3, four_blocks(rest, "y"), (0, 1, 2, 3))
 
-    waits = {1: (blocks[1], blocks[3], cosine, sine, key_start, gain), 2: (blocks[2], attn_step, step_block)}
-    qkv_blocks = ring_z(qkv_both, waits)
-    (rest_y,) = after([rest_y], *qkv_blocks)
-    query, own, features, size = project(spot, blocks, qkv_blocks, gain, cosine, sine)
+    (qkv_z,) = after([qkv_z], rest_y, cosine, sine, key_start, gain, attn_step, step_block, *blocks)
+    qkv_near = four_blocks(qkv_z, "y")
+    ahead, behind = shift(rest_y, Z, 8, 1), shift(rest_y, Z, 8, -1)
+    (qkv_stack,) = after([jnp.stack(qkv_near)], ahead, behind)
+    qkv_far = swap_core(qkv_stack)
+    query, own, features, size = project(spot, blocks, qkv_near, qkv_far, gain, cosine, sine)
     before = lax.ppermute(own[:, rows - window :], ("zl", "co"), [(i, i + 1) for i in range(3)])
     attended = attention(key_start, query, before, own)
     everyone = four_blocks(attended, "tp")
-    near = ring_z(rest_y, {1: (query,), 2: (attended,), 3: (everyone[1], everyone[3])})
+    near = ring_z(rest_y, ahead, behind, {1: (qkv_far,), 2: (attended,), 3: (everyone[1], everyone[3])})
     far = [swap_core(block) for block in near]
     parts, mixed = layer(
         spot, everyone, features, size, attn_step, up_scale[None], gate_scale[None], near, far

time: 249 us -> 216 us (0.87)
  waiting for transfers between devices: 102 us -> 85.2 us
  starting transfers between devices: 77.7 us -> 64.2 us
    ppermute x32 -> x25, starting transfers between devices: 71 us -> 49.2 us  [shift(): return lax.ppermute(block, axis, ring(count, step))]
    ppermute x32 -> x25, waiting for transfers between devices: 74 us -> 54.3 us  [shift(): return lax.ppermute(block, axis, ring(count, step))]
    all_to_all x0 -> x1, starting transfers between devices: none -> 8.47 us  [body(): qkv_z = lax.all_to_all(everywhere, Z, 0, 0, tiled=True)]
    ppermute x9, waiting for transfers between devices: 1.18 us -> 3.93 us  [swap_core(): return lax.ppermute(block, 'co', [(0, 1), (1, 0)])]
    unnamed x66 -> x72, local copies, waits for them, and re-layouts: 8.35 us -> 8.9 us
  transfers between devices with their start and end apart: 43 -> 37, of which waited for: 24 -> 18; matrix products, arithmetic and copies ran while one was open for 5% -> 5% of each run, Pallas kernels for 8% -> 8%
where the time goes in v2:
time: 216 us; the launch traced here: 212 us
  waiting for transfers between devices  85.2 us (39%)
  starting transfers between devices  64.2 us (30%)
  Pallas kernels  40.2 us (19%)
  local copies, waits for them, and re-layouts  16.6 us (8%)
  other arithmetic  5.7 us (3%)
    ppermute x25, waiting for transfers between devices, shift(): return lax.ppermute(block, axis, ring(count, step))  54.3 us
    ppermute x25, starting transfers between devices, shift(): return lax.ppermute(block, axis, ring(count, step))  49.2 us
    all_to_all x1, waiting for transfers between devices, body(): landed = lax.all_to_all(parts, 'tp', 0, 0, tiled=True).astype(F32)  25.2 us
    pallas_call x1, Pallas kernels, layer(): pl.pallas_call(layer_kernel, out_shape=[jax.ShapeDtypeStruct((4, local, r...  22.3 us
    pallas_call x1, Pallas kernels, attention(): pl.pallas_call(attention_kernel, out_shape=jax.ShapeDtypeStruct(query.sha...  9.51 us
    unnamed x72, local copies, waits for them, and re-layouts  8.9 us
    all_to_all x1, starting transfers between devices, body(): qkv_z = lax.all_to_all(everywhere, Z, 0, 0, tiled=True)  8.47 us
    pallas_call x1, Pallas kernels, project(): pl.pallas_call(project_kernel, out_shape=[jax.ShapeDtypeStruct((local, ro...  5.84 us
  transfers between devices with their start and end apart: 37, of which 18 were waited for; matrix products, arithmetic and copies ran while one was open for 5% of the time, Pallas kernels for 8%

profile of v2, /device:TPU:16, one launch (start us, length us, event | category | flops | bytes accessed | tf_op | source)
XLA Modules:
  0.0 212.4 jit_solution(4200947310765296407)
XLA Ops:
  0.8 2.8 %collective-permute-start.3 = (bf16[20,320]{1,0:T(8,128)(2,1)S(1)}, bf16[20,320]{1,0:T(8,128)(2,1)S(1)}, u32[]{:S(2)}, u32[]{:S(2)}) collective-permute-start(bf16[20,320]{1,0:T(8,128)(2,1)S(1)} %convert_bitcast_fusion.1), channel_id=1, source_target_pairs={{0,12},{4,0},{8,4},{12,8},{1,13},{5,1},{9,5},{13,9},{2,14},{6,2},{... | collective-permute-start | bytes 38408 | tf_op jit(solution)/shard_map/ppermute | solution.py:26
  6.6 2.4 %collective-permute-start = (bf16[320,768]{1,0:T(8,128)(2,1)S(1)}, bf16[320,768]{1,0:T(8,128)(2,1)S(1)}, u32[]{:S(2)}, u32[]{:S(2)}) collective-permute-start(bf16[320,768]{1,0:T(8,128)(2,1)S(1)} %reshape.58.refs_0_), channel_id=1, source_target_pairs={{0,12},{4,0},{8,4},{12,8},{1,13},{5,1},{9,5},{13,9},{2,14},{6,2},{... | collective-permute-start | bytes 1474568 | tf_op jit(solution)/shard_map/ppermute | solution.py:26
  11.5 8.5 %all-to-all-start = ((bf16[8,24,960]{2,1,0:T(8,128)(2,1)}), bf16[8,24,960]{2,1,0:T(8,128)(2,1)S(1)}, u32[]{:S(2)}, u32[]{:S(2)}) async-start(bf16[8,24,960]{2,1,0:T(8,128)(2,1)} %broadcast_in_dim.31), calls=%async_computation | async-start | bytes 786432 | tf_op jit(solution)/shard_map/all_to_all | solution.py:383
  22.8 2.9 %collective-permute-start.7 = (bf16[20,5120]{1,0:T(8,128)(2,1)S(1)}, bf16[20,5120]{1,0:T(8,128)(2,1)S(1)}, u32[]{:S(2)}, u32[]{:S(2)}) collective-permute-start(bf16[20,5120]{1,0:T(8,128)(2,1)S(1)} %concatenate.10.refs_0_), channel_id=1, source_target_pairs={{0,32},{16,48},{32,0},{48,16},{1,33},{17,49},{33,1},{49,17},{2,34}... | collective-permute-start | bytes 614408 | tf_op jit(solution)/shard_map/ppermute | solution.py:26
  25.7 5.2 %collective-permute-done.6.refs_1_ = bf16[20,5120]{1,0:T(8,128)(2,1)S(1)} collective-permute-done((bf16[20,5120]{1,0:T(8,128)(2,1)S(1)}, bf16[20,5120]{1,0:T(8,128)(2,1)S(1)}, u32[]{:S(2)}, u32[]{:S(2)}) %collective-permute-start.6) | collective-permute-done | bytes 204832 | tf_op jit(solution)/shard_map/ppermute | solution.py:26
  30.9 5.1 %collective-permute-start.8 = (bf16[20,5120]{1,0:T(8,128)(2,1)S(1)}, bf16[20,5120]{1,0:T(8,128)(2,1)S(1)}, u32[]{:S(2)}, u32[]{:S(2)}) collective-permute-start(bf16[20,5120]{1,0:T(8,128)(2,1)S(1)} %concatenate.10.refs_0_), channel_id=1, source_target_pairs={{0,16},{16,32},{32,48},{48,0},{1,17},{17,33},{33,49},{49,1},{2,18}... | collective-permute-start | bytes 614408 | tf_op jit(solution)/shard_map/ppermute | solution.py:26
  37.6 2.2 %collective-permute-done.8.refs_3_ = bf16[20,5120]{1,0:T(8,128)(2,1)S(1)} collective-permute-done((bf16[20,5120]{1,0:T(8,128)(2,1)S(1)}, bf16[20,5120]{1,0:T(8,128)(2,1)S(1)}, u32[]{:S(2)}, u32[]{:S(2)}) %collective-permute-start.8) | collective-permute-done | bytes 204832 | tf_op jit(solution)/shard_map/ppermute | solution.py:26
  40.5 2.5 %in_order.1.refs_9_ = bf16[80,5120]{1,0:T(8,128)(2,1)} custom-call(s32[4]{0:T(128)} %pad_add_fusion.place_ref, bf16[20,5120]{1,0:T(8,128)(2,1)} %copy-done.12, bf16[20,5120]{1,0:T(8,128)(2,1)} %copy-done.14, bf16[20,5120]{1,0:T(8,128)(2,1)} %copy-done.15, bf16[20,5120]{1,0:T(8,128)(2,1)} %copy-done.16), custom_call_target="tpu_custom_call" | custom-call | bytes 1638400 | tf_op jit(solution)/shard_map/in_order/pallas_call | solution.py:62
  43.0 1.7 collective-permute-start.12
  47.6 4.5 %collective-permute-start.10 = (bf16[8,24,960]{2,1,0:T(8,128)(2,1)S(1)}, bf16[8,24,960]{2,1,0:T(8,128)(2,1)S(1)}, u32[]{:S(2)}, u32[]{:S(2)}) collective-permute-start(bf16[8,24,960]{2,1,0:T(8,128)(2,1)S(1)} %all-to-all-done.refs_4_), channel_id=1, source_target_pairs={{0,32},{16,48},{32,0},{48,16},{1,33},{17,49},{33,1},{49,17},{2,34}... | collective-permute-start | bytes 1105928 | tf_op jit(solution)/shard_map/ppermute | solution.py:26
  52.7 5.0 %collective-permute-done.9.refs_5_ = bf16[8,24,960]{2,1,0:T(8,128)(2,1)S(1)} collective-permute-done((bf16[8,24,960]{2,1,0:T(8,128)(2,1)S(1)}, bf16[8,24,960]{2,1,0:T(8,128)(2,1)S(1)}, u32[]{:S(2)}, u32[]{:S(2)}) %collective-permute-start.9) | collective-permute-done | bytes 368672 | tf_op jit(solution)/shard_map/ppermute | solution.py:26
  57.7 1.9 collective-permute-done.10.refs_6_
  59.6 4.1 %collective-permute-done.11.refs_7_ = bf16[8,24,960]{2,1,0:T(8,128)(2,1)S(1)} collective-permute-done((bf16[8,24,960]{2,1,0:T(8,128)(2,1)S(1)}, bf16[8,24,960]{2,1,0:T(8,128)(2,1)S(1)}, u32[]{:S(2)}, u32[]{:S(2)}) %collective-permute-start.11) | collective-permute-done | bytes 368672 | tf_op jit(solution)/shard_map/ppermute | solution.py:26
  65.3 3.6 %collective-permute-done.14.refs_8_ = bf16[4,8,24,960]{3,2,1,0:T(8,128)(2,1)} collective-permute-done((bf16[4,8,24,960]{3,2,1,0:T(8,128)(2,1)}, bf16[4,8,24,960]{3,2,1,0:T(8,128)(2,1)}, u32[]{:S(2)}, u32[]{:S(2)}) %collective-permute-start.14) | collective-permute-done | bytes 1474592 | tf_op jit(solution)/shard_map/ppermute | solution.py:30
  69.2 3.0 %collective-permute-start.20 = (bf16[80,5120]{1,0:T(8,128)(2,1)}, bf16[80,5120]{1,0:T(8,128)(2,1)}, u32[]{:S(2)}, u32[]{:S(2)}) collective-permute-start(bf16[80,5120]{1,0:T(8,128)(2,1)} %collective-permute-done.13.refs_11_), channel_id=1, source_target_pairs={{0,194},{2,0},{64,2},{66,64},{128,66},{130,128},{192,130},{194,192... | collective-permute-start | bytes 2457608 | tf_op jit(solution)/shard_map/ppermute | solution.py:26
  75.2 5.8 %project.1 = (bf16[320,768]{1,0:T(8,128)(2,1)S(1)}, bf16[640,768]{1,0:T(8,128)(2,1)S(1)}, bf16[1280,768]{1,0:T(8,128)(2,1)S(1)}, f32[1,768]{1,0:T(1,128)S(1)}) custom-call(s32[4]{0:T(128)S(1)} %copy-done.1, bf16[320,768]{1,0:T(8,128)(2,1)S(1)} %reshape.58.refs_0_, bf16[320,768]{1,0:T(8,128)(2,1)S(1)} %copy-done.3, bf16[320,768]{1,0:T(8,128)(2,1)S(1)} %copy-done.5, ...), custom_call_target="tpu_custom_call" | custom-call | flops 1900000000 | bytes 12000000 | tf_op jit(solution)/shard_map/project/pallas_call | solution.py:205
  85.4 1.7 collective-permute-done.15.before_ref
  87.9 9.5 %attention.1.refs_0_ = bf16[320,768]{1,0:T(8,128)(2,1)} custom-call(s32[1,768]{1,0:T(1,128)} %broadcast_in_dim.30.start_ref, bf16[320,768]{1,0:T(8,128)(2,1)} %copy-done.9, bf16[640,512]{1,0:T(8,128)(2,1)} %copy-done.32, bf16[640,768]{1,0:T(8,128)(2,1)} %copy-done), custom_call_target="tpu_custom_call" | custom-call | flops 800000000 | bytes 4000000 | tf_op jit(solution)/shard_map/attention/pallas_call | solution.py:140
  97.4 9.8 %collective-permute-start.21 = (bf16[80,5120]{1,0:T(8,128)(2,1)}, bf16[80,5120]{1,0:T(8,128)(2,1)S(1)}, u32[]{:S(2)}, u32[]{:S(2)}) collective-permute-start(bf16[80,5120]{1,0:T(8,128)(2,1)} %collective-permute-done.19.refs_12_), channel_id=1, source_target_pairs={{0,2},{2,64},{64,66},{66,128},{128,130},{130,192},{192,194},{194,0... | collective-permute-start | bytes 2457608 | tf_op jit(solution)/shard_map/ppermute | solution.py:26
  107.2 1.6 collective-permute-start.22
  108.7 2.6 %collective-permute-start.16 = (bf16[320,768]{1,0:T(8,128)(2,1)}, bf16[320,768]{1,0:T(8,128)(2,1)S(1)}, u32[]{:S(2)}, u32[]{:S(2)}) collective-permute-start(bf16[320,768]{1,0:T(8,128)(2,1)} %attention.1.refs_0_), channel_id=1, source_target_pairs={{0,12},{4,0},{8,4},{12,8},{1,13},{5,1},{9,5},{13,9},{2,14},{6,2},{... | collective-permute-start | bytes 1474568 | tf_op jit(solution)/shard_map/ppermute | solution.py:26
  111.4 10.0 %collective-permute-done.16.refs_1_ = bf16[320,768]{1,0:T(8,128)(2,1)S(1)} collective-permute-done((bf16[320,768]{1,0:T(8,128)(2,1)}, bf16[320,768]{1,0:T(8,128)(2,1)S(1)}, u32[]{:S(2)}, u32[]{:S(2)}) %collective-permute-start.16) | collective-permute-done | bytes 491552 | tf_op jit(solution)/shard_map/ppermute | solution.py:26
  121.3 3.4 %collective-permute-done.18.refs_3_ = bf16[320,768]{1,0:T(8,128)(2,1)} collective-permute-done((bf16[320,768]{1,0:T(8,128)(2,1)}, bf16[320,768]{1,0:T(8,128)(2,1)}, u32[]{:S(2)}, u32[]{:S(2)}) %collective-permute-start.18) | collective-permute-done | bytes 491552 | tf_op jit(solution)/shard_map/ppermute | solution.py:26
  124.7 1.6 collective-permute-done.21.refs_14_
  126.9 1.7 collective-permute-start.23
  128.7 2.1 %collective-permute-start.17 = (bf16[320,768]{1,0:T(8,128)(2,1)}, bf16[320,768]{1,0:T(8,128)(2,1)S(1)}, u32[]{:S(2)}, u32[]{:S(2)}) collective-permute-start(bf16[320,768]{1,0:T(8,128)(2,1)} %attention.1.refs_0_), channel_id=1, source_target_pairs={{0,8},{4,12},{8,0},{12,4},{1,9},{5,13},{9,1},{13,5},{2,10},{6,14},... | collective-permute-start | bytes 1474568 | tf_op jit(solution)/shard_map/ppermute | solution.py:26
  131.6 10.2 %collective-permute-done.17.refs_2_ = bf16[320,768]{1,0:T(8,128)(2,1)S(1)} collective-permute-done((bf16[320,768]{1,0:T(8,128)(2,1)}, bf16[320,768]{1,0:T(8,128)(2,1)S(1)}, u32[]{:S(2)}, u32[]{:S(2)}) %collective-permute-start.17) | collective-permute-done | bytes 491552 | tf_op jit(solution)/shard_map/ppermute | solution.py:26
  141.7 5.3 %collective-permute-done.23.refs_16_ = bf16[80,5120]{1,0:T(8,128)(2,1)} collective-permute-done((bf16[80,5120]{1,0:T(8,128)(2,1)S(1)}, bf16[80,5120]{1,0:T(8,128)(2,1)}, u32[]{:S(2)}, u32[]{:S(2)}) %collective-permute-start.23) | collective-permute-done | bytes 819232 | tf_op jit(solution)/shard_map/ppermute | solution.py:26
  150.3 22.3 %layer.1 = (bf16[4,320,768]{2,1,0:T(8,128)(2,1)}, f32[320,768]{1,0:T(8,128)}) custom-call(s32[4]{0:T(128)} %pad_add_fusion.place_ref, bf16[320,768]{1,0:T(8,128)(2,1)} %attention.1.refs_0_, bf16[320,768]{1,0:T(8,128)(2,1)} %copy-done.33, bf16[320,768]{1,0:T(8,128)(2,1)} %copy-done.34, bf16[320,768]{1,0:T(8,128)(2,1)} %collective-permute-done.18.refs_3_, ...), custom_call_target="tpu_custom_call" | custom-call | flops 10000000000 | bytes 20000000 | tf_op jit(solution)/shard_map/layer/pallas_call | solution.py:324
  172.7 4.1 %all-to-all-start.1 = ((bf16[4,320,768]{2,1,0:T(8,128)(2,1)}), bf16[4,320,768]{2,1,0:T(8,128)(2,1)S(1)}, u32[]{:S(2)}, u32[]{:S(2)}) async-start(bf16[4,320,768]{2,1,0:T(8,128)(2,1)} %get-tuple-element.32), calls=%async_computation.1 | async-start | bytes 3932160 | tf_op jit(solution)/shard_map/all_to_all | solution.py:418
  177.2 25.2 %all-to-all-done.1 = bf16[4,320,768]{2,1,0:T(8,128)(2,1)S(1)} async-done(((bf16[4,320,768]{2,1,0:T(8,128)(2,1)}), bf16[4,320,768]{2,1,0:T(8,128)(2,1)S(1)}, u32[]{:S(2)}, u32[]{:S(2)}) %all-to-all-start.1) | async-done | bytes 1966112 | tf_op jit(solution)/shard_map/all_to_all | solution.py:418
  207.2 2.7 %collective-permute-done.33 = f32[4,768]{1,0:T(4,128)S(1)} collective-permute-done((f32[4,768]{1,0:T(4,128)S(1)}, f32[4,768]{1,0:T(4,128)S(1)}, u32[]{:S(2)}, u32[]{:S(2)}) %collective-permute-start.33) | collective-permute-done | bytes 12320 | tf_op jit(solution)/shard_map/ppermute | solution.py:26
  (169 shorter events, 36.7 us)
Async XLA Ops:
  0.8 21.2 %collective-permute-start.3 = (bf16[20,320]{1,0:T(8,128)(2,1)S(1)}, bf16[20,320]{1,0:T(8,128)(2,1)S(1)}, u32[]{:S(2)}, u32[]{:S(2)}) collective-permute-start(bf16[20,320]{1,0:T(8,128)(2,1)S(1)} %convert_bitcast_fusion.1), channel_id=1, source_target_pairs={{0,12},{4,0},{8,4},{12,8},{1,13},{5,1},{9,5},{13,9},{2,14},{6,2},{... | collective-permute-start | bytes 38408 | tf_op jit(solution)/shard_map/ppermute | solution.py:26
  3.5 18.5 %collective-permute-start.4 = (bf16[20,320]{1,0:T(8,128)(2,1)S(1)}, bf16[20,320]{1,0:T(8,128)(2,1)S(1)}, u32[]{:S(2)}, u32[]{:S(2)}) collective-permute-start(bf16[20,320]{1,0:T(8,128)(2,1)S(1)} %convert_bitcast_fusion.1), channel_id=1, source_target_pairs={{0,8},{4,12},{8,0},{12,4},{1,9},{5,13},{9,1},{13,5},{2,10},{6,14},... | collective-permute-start | bytes 38408 | tf_op jit(solution)/shard_map/ppermute | solution.py:26
  4.3 17.7 %collective-permute-start.5 = (bf16[20,320]{1,0:T(8,128)(2,1)S(1)}, bf16[20,320]{1,0:T(8,128)(2,1)S(1)}, u32[]{:S(2)}, u32[]{:S(2)}) collective-permute-start(bf16[20,320]{1,0:T(8,128)(2,1)S(1)} %convert_bitcast_fusion.1), channel_id=1, source_target_pairs={{0,4},{4,8},{8,12},{12,0},{1,5},{5,9},{9,13},{13,1},{2,6},{6,10},{... | collective-permute-start | bytes 38408 | tf_op jit(solution)/shard_map/ppermute | solution.py:26
  6.6 40.1 %collective-permute-start = (bf16[320,768]{1,0:T(8,128)(2,1)S(1)}, bf16[320,768]{1,0:T(8,128)(2,1)S(1)}, u32[]{:S(2)}, u32[]{:S(2)}) collective-permute-start(bf16[320,768]{1,0:T(8,128)(2,1)S(1)} %reshape.58.refs_0_), channel_id=1, source_target_pairs={{0,12},{4,0},{8,4},{12,8},{1,13},{5,1},{9,5},{13,9},{2,14},{6,2},{... | collective-permute-start | bytes 1474568 | tf_op jit(solution)/shard_map/ppermute | solution.py:26
  9.0 37.7 %collective-permute-start.1 = (bf16[320,768]{1,0:T(8,128)(2,1)S(1)}, bf16[320,768]{1,0:T(8,128)(2,1)S(1)}, u32[]{:S(2)}, u32[]{:S(2)}) collective-permute-start(bf16[320,768]{1,0:T(8,128)(2,1)S(1)} %reshape.58.refs_0_), channel_id=1, source_target_pairs={{0,8},{4,12},{8,0},{12,4},{1,9},{5,13},{9,1},{13,5},{2,10},{6,14},... | collective-permute-start | bytes 1474568 | tf_op jit(solution)/shard_map/ppermute | solution.py:26
  11.5 36.1 %all-to-all-start = ((bf16[8,24,960]{2,1,0:T(8,128)(2,1)}), bf16[8,24,960]{2,1,0:T(8,128)(2,1)S(1)}, u32[]{:S(2)}, u32[]{:S(2)}) async-start(bf16[8,24,960]{2,1,0:T(8,128)(2,1)} %broadcast_in_dim.31), calls=%async_computation | async-start | bytes 786432 | tf_op jit(solution)/shard_map/all_to_all | solution.py:383
  22.0 24.7 %collective-permute-start.2 = (bf16[320,768]{1,0:T(8,128)(2,1)S(1)}, bf16[320,768]{1,0:T(8,128)(2,1)S(1)}, u32[]{:S(2)}, u32[]{:S(2)}) collective-permute-start(bf16[320,768]{1,0:T(8,128)(2,1)S(1)} %reshape.58.refs_0_), channel_id=1, source_target_pairs={{0,4},{4,8},{8,12},{12,0},{1,5},{5,9},{9,13},{13,1},{2,6},{6,10},{... | collective-permute-start | bytes 1474568 | tf_op jit(solution)/shard_map/ppermute | solution.py:26
  22.2 8.7 %collective-permute-start.6 = (bf16[20,5120]{1,0:T(8,128)(2,1)S(1)}, bf16[20,5120]{1,0:T(8,128)(2,1)S(1)}, u32[]{:S(2)}, u32[]{:S(2)}) collective-permute-start(bf16[20,5120]{1,0:T(8,128)(2,1)S(1)} %concatenate.10.refs_0_), channel_id=1, source_target_pairs={{0,48},{16,0},{32,16},{48,32},{1,49},{17,1},{33,17},{49,33},{2,50}... | collective-permute-start | bytes 614408 | tf_op jit(solution)/shard_map/ppermute | solution.py:26
  22.8 14.8 %collective-permute-start.7 = (bf16[20,5120]{1,0:T(8,128)(2,1)S(1)}, bf16[20,5120]{1,0:T(8,128)(2,1)S(1)}, u32[]{:S(2)}, u32[]{:S(2)}) collective-permute-start(bf16[20,5120]{1,0:T(8,128)(2,1)S(1)} %concatenate.10.refs_0_), channel_id=1, source_target_pairs={{0,32},{16,48},{32,0},{48,16},{1,33},{17,49},{33,1},{49,17},{2,34}... | collective-permute-start | bytes 614408 | tf_op jit(solution)/shard_map/ppermute | solution.py:26
  30.9 8.8 %collective-permute-start.8 = (bf16[20,5120]{1,0:T(8,128)(2,1)S(1)}, bf16[20,5120]{1,0:T(8,128)(2,1)S(1)}, u32[]{:S(2)}, u32[]{:S(2)}) collective-permute-start(bf16[20,5120]{1,0:T(8,128)(2,1)S(1)} %concatenate.10.refs_0_), channel_id=1, source_target_pairs={{0,16},{16,32},{32,48},{48,0},{1,17},{17,33},{33,49},{49,1},{2,18}... | collective-permute-start | bytes 614408 | tf_op jit(solution)/shard_map/ppermute | solution.py:26
  43.0 22.1 %collective-permute-start.12 = (bf16[80,5120]{1,0:T(8,128)(2,1)}, bf16[80,5120]{1,0:T(8,128)(2,1)}, u32[]{:S(2)}, u32[]{:S(2)}) collective-permute-start(bf16[80,5120]{1,0:T(8,128)(2,1)} %in_order.1.refs_9_), channel_id=1, source_target_pairs={{0,2},{2,64},{64,66},{66,128},{128,130},{130,192},{192,194},{194,0... | collective-permute-start | bytes 2457608 | tf_op jit(solution)/shard_map/ppermute | solution.py:26
  44.7 20.4 %collective-permute-start.13 = (bf16[80,5120]{1,0:T(8,128)(2,1)}, bf16[80,5120]{1,0:T(8,128)(2,1)}, u32[]{:S(2)}, u32[]{:S(2)}) collective-permute-start(bf16[80,5120]{1,0:T(8,128)(2,1)} %in_order.1.refs_9_), channel_id=1, source_target_pairs={{0,194},{2,0},{64,2},{66,64},{128,66},{130,128},{192,130},{194,192... | collective-permute-start | bytes 2457608 | tf_op jit(solution)/shard_map/ppermute | solution.py:26
  47.6 10.2 %collective-permute-start.9 = (bf16[8,24,960]{2,1,0:T(8,128)(2,1)S(1)}, bf16[8,24,960]{2,1,0:T(8,128)(2,1)S(1)}, u32[]{:S(2)}, u32[]{:S(2)}) collective-permute-start(bf16[8,24,960]{2,1,0:T(8,128)(2,1)S(1)} %all-to-all-done.refs_4_), channel_id=1, source_target_pairs={{0,48},{16,0},{32,16},{48,32},{1,49},{17,1},{33,17},{49,33},{2,50}... | collective-permute-start | bytes 1105928 | tf_op jit(solution)/shard_map/ppermute | solution.py:26
  47.6 12.1 %collective-permute-start.10 = (bf16[8,24,960]{2,1,0:T(8,128)(2,1)S(1)}, bf16[8,24,960]{2,1,0:T(8,128)(2,1)S(1)}, u32[]{:S(2)}, u32[]{:S(2)}) collective-permute-start(bf16[8,24,960]{2,1,0:T(8,128)(2,1)S(1)} %all-to-all-done.refs_4_), channel_id=1, source_target_pairs={{0,32},{16,48},{32,0},{48,16},{1,33},{17,49},{33,1},{49,17},{2,34}... | collective-permute-start | bytes 1105928 | tf_op jit(solution)/shard_map/ppermute | solution.py:26
  52.1 11.6 %collective-permute-start.11 = (bf16[8,24,960]{2,1,0:T(8,128)(2,1)S(1)}, bf16[8,24,960]{2,1,0:T(8,128)(2,1)S(1)}, u32[]{:S(2)}, u32[]{:S(2)}) collective-permute-start(bf16[8,24,960]{2,1,0:T(8,128)(2,1)S(1)} %all-to-all-done.refs_4_), channel_id=1, source_target_pairs={{0,16},{16,32},{32,48},{48,0},{1,17},{17,33},{33,49},{49,1},{2,18}... | collective-permute-start | bytes 1105928 | tf_op jit(solution)/shard_map/ppermute | solution.py:26
  68.9 28.5 %collective-permute-start.19 = (bf16[80,5120]{1,0:T(8,128)(2,1)}, bf16[80,5120]{1,0:T(8,128)(2,1)}, u32[]{:S(2)}, u32[]{:S(2)}) collective-permute-start(bf16[80,5120]{1,0:T(8,128)(2,1)} %collective-permute-done.12.refs_10_), channel_id=1, source_target_pairs={{0,2},{2,64},{64,66},{66,128},{128,130},{130,192},{192,194},{194,0... | collective-permute-start | bytes 2457608 | tf_op jit(solution)/shard_map/ppermute | solution.py:26
  69.2 28.2 %collective-permute-start.20 = (bf16[80,5120]{1,0:T(8,128)(2,1)}, bf16[80,5120]{1,0:T(8,128)(2,1)}, u32[]{:S(2)}, u32[]{:S(2)}) collective-permute-start(bf16[80,5120]{1,0:T(8,128)(2,1)} %collective-permute-done.13.refs_11_), channel_id=1, source_target_pairs={{0,194},{2,0},{64,2},{66,64},{128,66},{130,128},{192,130},{194,192... | collective-permute-start | bytes 2457608 | tf_op jit(solution)/shard_map/ppermute | solution.py:26
  97.4 29.0 %collective-permute-start.21 = (bf16[80,5120]{1,0:T(8,128)(2,1)}, bf16[80,5120]{1,0:T(8,128)(2,1)S(1)}, u32[]{:S(2)}, u32[]{:S(2)}) collective-permute-start(bf16[80,5120]{1,0:T(8,128)(2,1)} %collective-permute-done.19.refs_12_), channel_id=1, source_target_pairs={{0,2},{2,64},{64,66},{66,128},{128,130},{130,192},{192,194},{194,0... | collective-permute-start | bytes 2457608 | tf_op jit(solution)/shard_map/ppermute | solution.py:26
  107.2 19.8 %collective-permute-start.22 = (bf16[80,5120]{1,0:T(8,128)(2,1)}, bf16[80,5120]{1,0:T(8,128)(2,1)S(1)}, u32[]{:S(2)}, u32[]{:S(2)}) collective-permute-start(bf16[80,5120]{1,0:T(8,128)(2,1)} %collective-permute-done.20.refs_13_), channel_id=1, source_target_pairs={{0,194},{2,0},{64,2},{66,64},{128,66},{130,128},{192,130},{194,192... | collective-permute-start | bytes 2457608 | tf_op jit(solution)/shard_map/ppermute | solution.py:26
  108.7 12.6 %collective-permute-start.16 = (bf16[320,768]{1,0:T(8,128)(2,1)}, bf16[320,768]{1,0:T(8,128)(2,1)S(1)}, u32[]{:S(2)}, u32[]{:S(2)}) collective-permute-start(bf16[320,768]{1,0:T(8,128)(2,1)} %attention.1.refs_0_), channel_id=1, source_target_pairs={{0,12},{4,0},{8,4},{12,8},{1,13},{5,1},{9,5},{13,9},{2,14},{6,2},{... | collective-permute-start | bytes 1474568 | tf_op jit(solution)/shard_map/ppermute | solution.py:26
  111.3 13.4 %collective-permute-start.18 = (bf16[320,768]{1,0:T(8,128)(2,1)}, bf16[320,768]{1,0:T(8,128)(2,1)}, u32[]{:S(2)}, u32[]{:S(2)}) collective-permute-start(bf16[320,768]{1,0:T(8,128)(2,1)} %attention.1.refs_0_), channel_id=1, source_target_pairs={{0,4},{4,8},{8,12},{12,0},{1,5},{5,9},{9,13},{13,1},{2,6},{6,10},{... | collective-permute-start | bytes 1474568 | tf_op jit(solution)/shard_map/ppermute | solution.py:26
  111.3 19.5 %collective-permute-start.24 = (bf16[80,5120]{1,0:T(8,128)(2,1)S(1)}, bf16[80,5120]{1,0:T(8,128)(2,1)S(1)}, u32[]{:S(2)}, u32[]{:S(2)}) collective-permute-start(bf16[80,5120]{1,0:T(8,128)(2,1)S(1)} %copy-done.13), channel_id=1, source_target_pairs={{0,1},{1,0},{2,3},{3,2},{4,5},{5,4},{6,7},{7,6},{8,9},{9,8},{10,11... | collective-permute-start | bytes 2457608 | tf_op jit(solution)/shard_map/ppermute | solution.py:30
  121.3 9.6 %collective-permute-start.25 = (bf16[80,5120]{1,0:T(8,128)(2,1)}, bf16[80,5120]{1,0:T(8,128)(2,1)S(1)}, u32[]{:S(2)}, u32[]{:S(2)}) collective-permute-start(bf16[80,5120]{1,0:T(8,128)(2,1)} %collective-permute-done.12.refs_10_), channel_id=1, source_target_pairs={{0,1},{1,0},{2,3},{3,2},{4,5},{5,4},{6,7},{7,6},{8,9},{9,8},{10,11... | collective-permute-start | bytes 2457608 | tf_op jit(solution)/shard_map/ppermute | solution.py:30
  124.7 6.7 %collective-permute-start.26 = (bf16[80,5120]{1,0:T(8,128)(2,1)}, bf16[80,5120]{1,0:T(8,128)(2,1)S(1)}, u32[]{:S(2)}, u32[]{:S(2)}) collective-permute-start(bf16[80,5120]{1,0:T(8,128)(2,1)} %collective-permute-done.13.refs_11_), channel_id=1, source_target_pairs={{0,1},{1,0},{2,3},{3,2},{4,5},{5,4},{6,7},{7,6},{8,9},{9,8},{10,11... | collective-permute-start | bytes 2457608 | tf_op jit(solution)/shard_map/ppermute | solution.py:30
  126.9 20.1 %collective-permute-start.23 = (bf16[80,5120]{1,0:T(8,128)(2,1)S(1)}, bf16[80,5120]{1,0:T(8,128)(2,1)}, u32[]{:S(2)}, u32[]{:S(2)}) collective-permute-start(bf16[80,5120]{1,0:T(8,128)(2,1)S(1)} %collective-permute-done.21.refs_14_), channel_id=1, source_target_pairs={{0,2},{2,64},{64,66},{66,128},{128,130},{130,192},{192,194},{194,0... | collective-permute-start | bytes 2457608 | tf_op jit(solution)/shard_map/ppermute | solution.py:26
  128.7 13.0 %collective-permute-start.17 = (bf16[320,768]{1,0:T(8,128)(2,1)}, bf16[320,768]{1,0:T(8,128)(2,1)S(1)}, u32[]{:S(2)}, u32[]{:S(2)}) collective-permute-start(bf16[320,768]{1,0:T(8,128)(2,1)} %attention.1.refs_0_), channel_id=1, source_target_pairs={{0,8},{4,12},{8,0},{12,4},{1,9},{5,13},{9,1},{13,5},{2,10},{6,14},... | collective-permute-start | bytes 1474568 | tf_op jit(solution)/shard_map/ppermute | solution.py:26
  130.8 18.6 %collective-permute-start.27 = (bf16[80,5120]{1,0:T(8,128)(2,1)}, bf16[80,5120]{1,0:T(8,128)(2,1)S(1)}, u32[]{:S(2)}, u32[]{:S(2)}) collective-permute-start(bf16[80,5120]{1,0:T(8,128)(2,1)} %collective-permute-done.19.refs_12_), channel_id=1, source_target_pairs={{0,1},{1,0},{2,3},{3,2},{4,5},{5,4},{6,7},{7,6},{8,9},{9,8},{10,11... | collective-permute-start | bytes 2457608 | tf_op jit(solution)/shard_map/ppermute | solution.py:30
  131.0 18.5 %collective-permute-start.28 = (bf16[80,5120]{1,0:T(8,128)(2,1)}, bf16[80,5120]{1,0:T(8,128)(2,1)}, u32[]{:S(2)}, u32[]{:S(2)}) collective-permute-start(bf16[80,5120]{1,0:T(8,128)(2,1)} %collective-permute-done.20.refs_13_), channel_id=1, source_target_pairs={{0,1},{1,0},{2,3},{3,2},{4,5},{5,4},{6,7},{7,6},{8,9},{9,8},{10,11... | collective-permute-start | bytes 2457608 | tf_op jit(solution)/shard_map/ppermute | solution.py:30
  131.4 18.0 %collective-permute-start.29 = (bf16[80,5120]{1,0:T(8,128)(2,1)S(1)}, bf16[80,5120]{1,0:T(8,128)(2,1)}, u32[]{:S(2)}, u32[]{:S(2)}) collective-permute-start(bf16[80,5120]{1,0:T(8,128)(2,1)S(1)} %collective-permute-done.21.refs_14_), channel_id=1, source_target_pairs={{0,1},{1,0},{2,3},{3,2},{4,5},{5,4},{6,7},{7,6},{8,9},{9,8},{10,11... | collective-permute-start | bytes 2457608 | tf_op jit(solution)/shard_map/ppermute | solution.py:30
  141.7 7.8 %collective-permute-start.30 = (bf16[80,5120]{1,0:T(8,128)(2,1)S(1)}, bf16[80,5120]{1,0:T(8,128)(2,1)}, u32[]{:S(2)}, u32[]{:S(2)}) collective-permute-start(bf16[80,5120]{1,0:T(8,128)(2,1)S(1)} %collective-permute-done.22.refs_15_), channel_id=1, source_target_pairs={{0,1},{1,0},{2,3},{3,2},{4,5},{5,4},{6,7},{7,6},{8,9},{9,8},{10,11... | collective-permute-start | bytes 2457608 | tf_op jit(solution)/shard_map/ppermute | solution.py:30
  172.7 29.7 %all-to-all-start.1 = ((bf16[4,320,768]{2,1,0:T(8,128)(2,1)}), bf16[4,320,768]{2,1,0:T(8,128)(2,1)S(1)}, u32[]{:S(2)}, u32[]{:S(2)}) async-start(bf16[4,320,768]{2,1,0:T(8,128)(2,1)} %get-tuple-element.32), calls=%async_computation.1 | async-start | bytes 3932160 | tf_op jit(solution)/shard_map/all_to_all | solution.py:418
  204.6 5.2 %collective-permute-start.33 = (f32[4,768]{1,0:T(4,128)S(1)}, f32[4,768]{1,0:T(4,128)S(1)}, u32[]{:S(2)}, u32[]{:S(2)}) collective-permute-start(f32[4,768]{1,0:T(4,128)S(1)} %pad_maximum_fusion.1), channel_id=1, source_target_pairs={{0,8},{4,12},{8,0},{12,4},{1,9},{5,13},{9,1},{13,5},{2,10},{6,14},... | collective-permute-start | bytes 36872 | tf_op jit(solution)/shard_map/ppermute | solution.py:26
  (40 other events, 488.4 us)

commit v3 on v2

--- a/solution.py
+++ b/solution.py
@@ -378,10 +378,12 @@
     spot_z = lax.axis_index("zh") * 2 + lax.axis_index("zl")
     spot = jnp.stack([tp, core, spot_z, spot_y]).astype(jnp.int32)
 
-    qkv = jnp.pad(qkv_weight.astype(BF16).reshape(SHARD, 3 * local), ((0, PADDED - SHARD), (0, 0)))
+    out_rows = four_blocks(out_weight.T.astype(BF16), "tp")
+    shard, own_tokens = after([qkv_weight.astype(BF16), tokens[0].T], *out_rows)
+    qkv = jnp.pad(shard.reshape(SHARD, 3 * local), ((0, PADDED - SHARD), (0, 0)))
     everywhere = jnp.broadcast_to(qkv[None], (8,) + qkv.shape)
     qkv_z = lax.all_to_all(everywhere, Z, 0, 0, tiled=True)
-    blocks = four_blocks(kernel_order(tokens[0].T), "tp")
+    blocks = four_blocks(kernel_order(own_tokens), "tp")
 
     starts = stream_starts(segment_ids[0])
     own_first = piece * rows
@@ -396,7 +398,6 @@
     attn_step = kernel_order(attn_rate)[:, None]
     step_block = lax.dynamic_slice_in_dim(kernel_order(mlp_rate), tp * local, local)[:, None]
 
-    out_rows = four_blocks(out_weight.T.astype(BF16), "tp")
     wide = gate_up_weight.astype(BF16).reshape(SHARD, 2 * hidden)
     rest = jnp.concatenate(out_rows + [wide, down_weight.T.astype(BF16)], axis=1)
     rest_y = in_order(spot, 3, four_blocks(rest, "y"), (0, 1, 2, 3))
@@ -410,7 +411,7 @@
     before = lax.ppermute(own[:, rows - window :], ("zl", "co"), [(i, i + 1) for i in range(3)])
     attended = attention(key_start, query, before, own)
     everyone = four_blocks(attended, "tp")
-    near = ring_z(rest_y, ahead, behind, {1: (qkv_far,), 2: (attended,), 3: (everyone[1], everyone[3])})
+    near = ring_z(rest_y, ahead, behind, {1: (qkv_far,), 2: (before,), 3: (everyone[1], everyone[3])})
     far = [swap_core(block) for block in near]
     parts, mixed = layer(
         spot, everyone, features, size, attn_step, up_scale[None], gate_scale[None], near, far

time: 216 us -> 222 us (1.028)
  waiting for transfers between devices: 85.2 us -> 103 us
  starting transfers between devices: 64.2 us -> 52.1 us
  other arithmetic: 5.7 us -> 9.31 us
    ppermute x25, waiting for transfers between devices: 54.3 us -> 71.5 us  [shift(): return lax.ppermute(block, axis, ring(count, step))]
    ppermute x25, starting transfers between devices: 49.2 us -> 37.7 us  [shift(): return lax.ppermute(block, axis, ring(count, step))]
    unnamed x72 -> x64, local copies, waits for them, and re-layouts: 8.9 us -> 7.96 us
  transfers between devices with their start and end apart: 37 -> 37, of which waited for: 18 -> 20; matrix products, arithmetic and copies ran while one was open for 5% -> 6% of each run, Pallas kernels for 8% -> 8%
where the time goes in v3:
time: 222 us; the launch traced here: 221 us
  waiting for transfers between devices  103 us (46%)
  starting transfers between devices  52.1 us (23%)
  Pallas kernels  40.2 us (18%)
  local copies, waits for them, and re-layouts  15.2 us (7%)
  other arithmetic  9.31 us (4%)
    ppermute x25, waiting for transfers between devices, shift(): return lax.ppermute(block, axis, ring(count, step))  71.5 us
    ppermute x25, starting transfers between devices, shift(): return lax.ppermute(block, axis, ring(count, step))  37.7 us
    all_to_all x1, waiting for transfers between devices, body(): landed = lax.all_to_all(parts, 'tp', 0, 0, tiled=True).astype(F32)  25.4 us
    pallas_call x1, Pallas kernels, layer(): pl.pallas_call(layer_kernel, out_shape=[jax.ShapeDtypeStruct((4, local, r...  22.3 us
    pallas_call x1, Pallas kernels, attention(): pl.pallas_call(attention_kernel, out_shape=jax.ShapeDtypeStruct(query.sha...  9.52 us
    all_to_all x1, starting transfers between devices, body(): qkv_z = lax.all_to_all(everywhere, Z, 0, 0, tiled=True)  8.47 us
    unnamed x64, local copies, waits for them, and re-layouts  7.96 us
    pallas_call x1, Pallas kernels, project(): pl.pallas_call(project_kernel, out_shape=[jax.ShapeDtypeStruct((local, ro...  5.85 us
  transfers between devices with their start and end apart: 37, of which 20 were waited for; matrix products, arithmetic and copies ran while one was open for 6% of the time, Pallas kernels for 8%

profile of v3, /device:TPU:16, one launch (start us, length us, event | category | flops | bytes accessed | tf_op | source)
XLA Modules:
  0.0 220.6 jit_solution(3981114327576698538)
XLA Ops:
  0.8 2.8 %collective-permute-start = (bf16[20,320]{1,0:T(8,128)(2,1)S(1)}, bf16[20,320]{1,0:T(8,128)(2,1)S(1)}, u32[]{:S(2)}, u32[]{:S(2)}) collective-permute-start(bf16[20,320]{1,0:T(8,128)(2,1)S(1)} %convert_bitcast_fusion.1), channel_id=1, source_target_pairs={{0,12},{4,0},{8,4},{12,8},{1,13},{5,1},{9,5},{13,9},{2,14},{6,2},{... | collective-permute-start | bytes 38408 | tf_op jit(solution)/shard_map/ppermute | solution.py:26
  13.0 8.5 %all-to-all-start = ((bf16[8,24,960]{2,1,0:T(8,128)(2,1)}), bf16[8,24,960]{2,1,0:T(8,128)(2,1)S(1)}, u32[]{:S(2)}, u32[]{:S(2)}) async-start(bf16[8,24,960]{2,1,0:T(8,128)(2,1)} %broadcast_in_dim.31), calls=%async_computation | async-start | bytes 786432 | tf_op jit(solution)/shard_map/all_to_all | solution.py:385
  21.5 3.0 %collective-permute-start.7 = (bf16[20,5120]{1,0:T(8,128)(2,1)S(1)}, bf16[20,5120]{1,0:T(8,128)(2,1)S(1)}, u32[]{:S(2)}, u32[]{:S(2)}) collective-permute-start(bf16[20,5120]{1,0:T(8,128)(2,1)S(1)} %concatenate.10.refs_0_), channel_id=1, source_target_pairs={{0,32},{16,48},{32,0},{48,16},{1,33},{17,49},{33,1},{49,17},{2,34}... | collective-permute-start | bytes 614408 | tf_op jit(solution)/shard_map/ppermute | solution.py:26
  24.8 2.4 %collective-permute-start.3 = (bf16[320,768]{1,0:T(8,128)(2,1)S(1)}, bf16[320,768]{1,0:T(8,128)(2,1)S(1)}, u32[]{:S(2)}, u32[]{:S(2)}) collective-permute-start(bf16[320,768]{1,0:T(8,128)(2,1)S(1)} %reshape.58.refs_0_), channel_id=1, source_target_pairs={{0,12},{4,0},{8,4},{12,8},{1,13},{5,1},{9,5},{13,9},{2,14},{6,2},{... | collective-permute-start | bytes 1474568 | tf_op jit(solution)/shard_map/ppermute | solution.py:26
  27.2 1.5 collective-permute-start.4
  30.3 1.6 collective-permute-done.7.refs_2_
  32.0 2.7 %collective-permute-done.8.refs_3_ = bf16[20,5120]{1,0:T(8,128)(2,1)S(1)} collective-permute-done((bf16[20,5120]{1,0:T(8,128)(2,1)S(1)}, bf16[20,5120]{1,0:T(8,128)(2,1)S(1)}, u32[]{:S(2)}, u32[]{:S(2)}) %collective-permute-start.8) | collective-permute-done | bytes 204832 | tf_op jit(solution)/shard_map/ppermute | solution.py:26
  35.4 2.5 %in_order.1.refs_9_ = bf16[80,5120]{1,0:T(8,128)(2,1)} custom-call(s32[4]{0:T(128)} %pad_add_fusion.place_ref, bf16[20,5120]{1,0:T(8,128)(2,1)} %copy-done.12, bf16[20,5120]{1,0:T(8,128)(2,1)} %copy-done.15, bf16[20,5120]{1,0:T(8,128)(2,1)} %copy-done.16, bf16[20,5120]{1,0:T(8,128)(2,1)} %copy-done.17), custom_call_target="tpu_custom_call" | custom-call | bytes 1638400 | tf_op jit(solution)/shard_map/in_order/pallas_call | solution.py:62
  37.8 1.7 collective-permute-start.12
  41.5 5.0 %collective-permute-done.3.refs_1_ = bf16[320,768]{1,0:T(8,128)(2,1)S(1)} collective-permute-done((bf16[320,768]{1,0:T(8,128)(2,1)S(1)}, bf16[320,768]{1,0:T(8,128)(2,1)S(1)}, u32[]{:S(2)}, u32[]{:S(2)}) %collective-permute-start.3) | collective-permute-done | bytes 491552 | tf_op jit(solution)/shard_map/ppermute | solution.py:26
  46.6 3.7 %collective-permute-done.5.refs_3_ = bf16[320,768]{1,0:T(8,128)(2,1)S(1)} collective-permute-done((bf16[320,768]{1,0:T(8,128)(2,1)S(1)}, bf16[320,768]{1,0:T(8,128)(2,1)S(1)}, u32[]{:S(2)}, u32[]{:S(2)}) %collective-permute-start.5) | collective-permute-done | bytes 491552 | tf_op jit(solution)/shard_map/ppermute | solution.py:26
  51.0 1.7 collective-permute-start.9
  52.8 1.8 collective-permute-start.10
  55.0 14.9 %collective-permute-done.9.refs_5_ = bf16[8,24,960]{2,1,0:T(8,128)(2,1)S(1)} collective-permute-done((bf16[8,24,960]{2,1,0:T(8,128)(2,1)S(1)}, bf16[8,24,960]{2,1,0:T(8,128)(2,1)S(1)}, u32[]{:S(2)}, u32[]{:S(2)}) %collective-permute-start.9) | collective-permute-done | bytes 368672 | tf_op jit(solution)/shard_map/ppermute | solution.py:26
  69.9 3.7 %collective-permute-done.11.refs_7_ = bf16[8,24,960]{2,1,0:T(8,128)(2,1)S(1)} collective-permute-done((bf16[8,24,960]{2,1,0:T(8,128)(2,1)S(1)}, bf16[8,24,960]{2,1,0:T(8,128)(2,1)S(1)}, u32[]{:S(2)}, u32[]{:S(2)}) %collective-permute-start.11) | collective-permute-done | bytes 368672 | tf_op jit(solution)/shard_map/ppermute | solution.py:26
  75.2 3.6 %collective-permute-done.14.refs_8_ = bf16[4,8,24,960]{3,2,1,0:T(8,128)(2,1)} collective-permute-done((bf16[4,8,24,960]{3,2,1,0:T(8,128)(2,1)}, bf16[4,8,24,960]{3,2,1,0:T(8,128)(2,1)}, u32[]{:S(2)}, u32[]{:S(2)}) %collective-permute-start.14) | collective-permute-done | bytes 1474592 | tf_op jit(solution)/shard_map/ppermute | solution.py:30
  78.8 1.6 collective-permute-start.19
  80.4 1.6 collective-permute-start.20
  85.1 5.9 %project.1 = (bf16[320,768]{1,0:T(8,128)(2,1)S(1)}, bf16[640,768]{1,0:T(8,128)(2,1)S(1)}, bf16[1280,768]{1,0:T(8,128)(2,1)S(1)}, f32[1,768]{1,0:T(1,128)S(1)}) custom-call(s32[4]{0:T(128)S(1)} %copy-done.1, bf16[320,768]{1,0:T(8,128)(2,1)S(1)} %reshape.58.refs_0_, bf16[320,768]{1,0:T(8,128)(2,1)S(1)} %copy-done.3, bf16[320,768]{1,0:T(8,128)(2,1)S(1)} %copy-done.5, ...), custom_call_target="tpu_custom_call" | custom-call | flops 1900000000 | bytes 12000000 | tf_op jit(solution)/shard_map/project/pallas_call | solution.py:205
  93.7 1.5 collective-permute-start.15
  95.2 1.7 collective-permute-done.15.before_ref
  96.9 3.7 %collective-permute-done.19.refs_12_ = bf16[80,5120]{1,0:T(8,128)(2,1)} collective-permute-done((bf16[80,5120]{1,0:T(8,128)(2,1)}, bf16[80,5120]{1,0:T(8,128)(2,1)}, u32[]{:S(2)}, u32[]{:S(2)}) %collective-permute-start.19) | collective-permute-done | bytes 819232 | tf_op jit(solution)/shard_map/ppermute | solution.py:26
  100.7 8.0 %collective-permute-start.21 = (bf16[80,5120]{1,0:T(8,128)(2,1)}, bf16[80,5120]{1,0:T(8,128)(2,1)S(1)}, u32[]{:S(2)}, u32[]{:S(2)}) collective-permute-start(bf16[80,5120]{1,0:T(8,128)(2,1)} %collective-permute-done.19.refs_12_), channel_id=1, source_target_pairs={{0,2},{2,64},{64,66},{66,128},{128,130},{130,192},{192,194},{194,0... | collective-permute-start | bytes 2457608 | tf_op jit(solution)/shard_map/ppermute | solution.py:26
  110.1 9.5 %attention.1.refs_0_ = bf16[320,768]{1,0:T(8,128)(2,1)} custom-call(s32[1,768]{1,0:T(1,128)} %broadcast_in_dim.30.start_ref, bf16[320,768]{1,0:T(8,128)(2,1)} %copy-done.9, bf16[640,512]{1,0:T(8,128)(2,1)} %copy-done.28, bf16[640,768]{1,0:T(8,128)(2,1)} %copy-done), custom_call_target="tpu_custom_call" | custom-call | flops 800000000 | bytes 4000000 | tf_op jit(solution)/shard_map/attention/pallas_call | solution.py:140
  119.6 2.0 collective-permute-start.18
  121.7 10.3 %collective-permute-done.16.refs_1_ = bf16[320,768]{1,0:T(8,128)(2,1)S(1)} collective-permute-done((bf16[320,768]{1,0:T(8,128)(2,1)}, bf16[320,768]{1,0:T(8,128)(2,1)S(1)}, u32[]{:S(2)}, u32[]{:S(2)}) %collective-permute-start.16) | collective-permute-done | bytes 491552 | tf_op jit(solution)/shard_map/ppermute | solution.py:26
  135.9 13.1 %collective-permute-done.17.refs_2_ = bf16[320,768]{1,0:T(8,128)(2,1)S(1)} collective-permute-done((bf16[320,768]{1,0:T(8,128)(2,1)}, bf16[320,768]{1,0:T(8,128)(2,1)S(1)}, u32[]{:S(2)}, u32[]{:S(2)}) %collective-permute-start.17) | collective-permute-done | bytes 491552 | tf_op jit(solution)/shard_map/ppermute | solution.py:26
  149.0 6.5 %collective-permute-done.23.refs_16_ = bf16[80,5120]{1,0:T(8,128)(2,1)} collective-permute-done((bf16[80,5120]{1,0:T(8,128)(2,1)S(1)}, bf16[80,5120]{1,0:T(8,128)(2,1)}, u32[]{:S(2)}, u32[]{:S(2)}) %collective-permute-start.23) | collective-permute-done | bytes 819232 | tf_op jit(solution)/shard_map/ppermute | solution.py:26
  158.9 22.3 %layer.1 = (bf16[4,320,768]{2,1,0:T(8,128)(2,1)}, f32[320,768]{1,0:T(8,128)}) custom-call(s32[4]{0:T(128)} %pad_add_fusion.place_ref, bf16[320,768]{1,0:T(8,128)(2,1)} %attention.1.refs_0_, bf16[320,768]{1,0:T(8,128)(2,1)} %copy-done.29, bf16[320,768]{1,0:T(8,128)(2,1)} %copy-done.30, bf16[320,768]{1,0:T(8,128)(2,1)} %collective-permute-done.18.refs_3_, ...), custom_call_target="tpu_custom_call" | custom-call | flops 10000000000 | bytes 20000000 | tf_op jit(solution)/shard_map/layer/pallas_call | solution.py:324
  181.2 3.6 %all-to-all-start.1 = ((bf16[4,320,768]{2,1,0:T(8,128)(2,1)}), bf16[4,320,768]{2,1,0:T(8,128)(2,1)S(1)}, u32[]{:S(2)}, u32[]{:S(2)}) async-start(bf16[4,320,768]{2,1,0:T(8,128)(2,1)} %get-tuple-element.36), calls=%async_computation.1 | async-start | bytes 3932160 | tf_op jit(solution)/shard_map/all_to_all | solution.py:419
  185.2 25.4 %all-to-all-done.1 = bf16[4,320,768]{2,1,0:T(8,128)(2,1)S(1)} async-done(((bf16[4,320,768]{2,1,0:T(8,128)(2,1)}), bf16[4,320,768]{2,1,0:T(8,128)(2,1)S(1)}, u32[]{:S(2)}, u32[]{:S(2)}) %all-to-all-start.1) | async-done | bytes 1966112 | tf_op jit(solution)/shard_map/all_to_all | solution.py:419
  215.4 2.7 %collective-permute-done.33 = f32[4,768]{1,0:T(4,128)S(1)} collective-permute-done((f32[4,768]{1,0:T(4,128)S(1)}, f32[4,768]{1,0:T(4,128)S(1)}, u32[]{:S(2)}, u32[]{:S(2)}) %collective-permute-start.33) | collective-permute-done | bytes 12320 | tf_op jit(solution)/shard_map/ppermute | solution.py:26
  (161 shorter events, 39.6 us)
Async XLA Ops:
  0.8 10.6 %collective-permute-start = (bf16[20,320]{1,0:T(8,128)(2,1)S(1)}, bf16[20,320]{1,0:T(8,128)(2,1)S(1)}, u32[]{:S(2)}, u32[]{:S(2)}) collective-permute-start(bf16[20,320]{1,0:T(8,128)(2,1)S(1)} %convert_bitcast_fusion.1), channel_id=1, source_target_pairs={{0,12},{4,0},{8,4},{12,8},{1,13},{5,1},{9,5},{13,9},{2,14},{6,2},{... | collective-permute-start | bytes 38408 | tf_op jit(solution)/shard_map/ppermute | solution.py:26
  3.5 7.8 %collective-permute-start.1 = (bf16[20,320]{1,0:T(8,128)(2,1)S(1)}, bf16[20,320]{1,0:T(8,128)(2,1)S(1)}, u32[]{:S(2)}, u32[]{:S(2)}) collective-permute-start(bf16[20,320]{1,0:T(8,128)(2,1)S(1)} %convert_bitcast_fusion.1), channel_id=1, source_target_pairs={{0,8},{4,12},{8,0},{12,4},{1,9},{5,13},{9,1},{13,5},{2,10},{6,14},... | collective-permute-start | bytes 38408 | tf_op jit(solution)/shard_map/ppermute | solution.py:26
  4.3 7.0 %collective-permute-start.2 = (bf16[20,320]{1,0:T(8,128)(2,1)S(1)}, bf16[20,320]{1,0:T(8,128)(2,1)S(1)}, u32[]{:S(2)}, u32[]{:S(2)}) collective-permute-start(bf16[20,320]{1,0:T(8,128)(2,1)S(1)} %convert_bitcast_fusion.1), channel_id=1, source_target_pairs={{0,4},{4,8},{8,12},{12,0},{1,5},{5,9},{9,13},{13,1},{2,6},{6,10},{... | collective-permute-start | bytes 38408 | tf_op jit(solution)/shard_map/ppermute | solution.py:26
  11.5 17.2 %collective-permute-start.6 = (bf16[20,5120]{1,0:T(8,128)(2,1)S(1)}, bf16[20,5120]{1,0:T(8,128)(2,1)S(1)}, u32[]{:S(2)}, u32[]{:S(2)}) collective-permute-start(bf16[20,5120]{1,0:T(8,128)(2,1)S(1)} %concatenate.10.refs_0_), channel_id=1, source_target_pairs={{0,48},{16,0},{32,16},{48,32},{1,49},{17,1},{33,17},{49,33},{2,50}... | collective-permute-start | bytes 614408 | tf_op jit(solution)/shard_map/ppermute | solution.py:26
  13.0 38.0 %all-to-all-start = ((bf16[8,24,960]{2,1,0:T(8,128)(2,1)}), bf16[8,24,960]{2,1,0:T(8,128)(2,1)S(1)}, u32[]{:S(2)}, u32[]{:S(2)}) async-start(bf16[8,24,960]{2,1,0:T(8,128)(2,1)} %broadcast_in_dim.31), calls=%async_computation | async-start | bytes 786432 | tf_op jit(solution)/shard_map/all_to_all | solution.py:385
  21.5 10.5 %collective-permute-start.7 = (bf16[20,5120]{1,0:T(8,128)(2,1)S(1)}, bf16[20,5120]{1,0:T(8,128)(2,1)S(1)}, u32[]{:S(2)}, u32[]{:S(2)}) collective-permute-start(bf16[20,5120]{1,0:T(8,128)(2,1)S(1)} %concatenate.10.refs_0_), channel_id=1, source_target_pairs={{0,32},{16,48},{32,0},{48,16},{1,33},{17,49},{33,1},{49,17},{2,34}... | collective-permute-start | bytes 614408 | tf_op jit(solution)/shard_map/ppermute | solution.py:26
  24.5 10.2 %collective-permute-start.8 = (bf16[20,5120]{1,0:T(8,128)(2,1)S(1)}, bf16[20,5120]{1,0:T(8,128)(2,1)S(1)}, u32[]{:S(2)}, u32[]{:S(2)}) collective-permute-start(bf16[20,5120]{1,0:T(8,128)(2,1)S(1)} %concatenate.10.refs_0_), channel_id=1, source_target_pairs={{0,16},{16,32},{32,48},{48,0},{1,17},{17,33},{33,49},{49,1},{2,18}... | collective-permute-start | bytes 614408 | tf_op jit(solution)/shard_map/ppermute | solution.py:26
  24.8 21.8 %collective-permute-start.3 = (bf16[320,768]{1,0:T(8,128)(2,1)S(1)}, bf16[320,768]{1,0:T(8,128)(2,1)S(1)}, u32[]{:S(2)}, u32[]{:S(2)}) collective-permute-start(bf16[320,768]{1,0:T(8,128)(2,1)S(1)} %reshape.58.refs_0_), channel_id=1, source_target_pairs={{0,12},{4,0},{8,4},{12,8},{1,13},{5,1},{9,5},{13,9},{2,14},{6,2},{... | collective-permute-start | bytes 1474568 | tf_op jit(solution)/shard_map/ppermute | solution.py:26
  27.2 19.4 %collective-permute-start.4 = (bf16[320,768]{1,0:T(8,128)(2,1)S(1)}, bf16[320,768]{1,0:T(8,128)(2,1)S(1)}, u32[]{:S(2)}, u32[]{:S(2)}) collective-permute-start(bf16[320,768]{1,0:T(8,128)(2,1)S(1)} %reshape.58.refs_0_), channel_id=1, source_target_pairs={{0,8},{4,12},{8,0},{12,4},{1,9},{5,13},{9,1},{13,5},{2,10},{6,14},... | collective-permute-start | bytes 1474568 | tf_op jit(solution)/shard_map/ppermute | solution.py:26
  28.7 21.5 %collective-permute-start.5 = (bf16[320,768]{1,0:T(8,128)(2,1)S(1)}, bf16[320,768]{1,0:T(8,128)(2,1)S(1)}, u32[]{:S(2)}, u32[]{:S(2)}) collective-permute-start(bf16[320,768]{1,0:T(8,128)(2,1)S(1)} %reshape.58.refs_0_), channel_id=1, source_target_pairs={{0,4},{4,8},{8,12},{12,0},{1,5},{5,9},{9,13},{13,1},{2,6},{6,10},{... | collective-permute-start | bytes 1474568 | tf_op jit(solution)/shard_map/ppermute | solution.py:26
  37.8 37.1 %collective-permute-start.12 = (bf16[80,5120]{1,0:T(8,128)(2,1)}, bf16[80,5120]{1,0:T(8,128)(2,1)}, u32[]{:S(2)}, u32[]{:S(2)}) collective-permute-start(bf16[80,5120]{1,0:T(8,128)(2,1)} %in_order.1.refs_9_), channel_id=1, source_target_pairs={{0,2},{2,64},{64,66},{66,128},{128,130},{130,192},{192,194},{194,0... | collective-permute-start | bytes 2457608 | tf_op jit(solution)/shard_map/ppermute | solution.py:26
  39.6 35.3 %collective-permute-start.13 = (bf16[80,5120]{1,0:T(8,128)(2,1)}, bf16[80,5120]{1,0:T(8,128)(2,1)}, u32[]{:S(2)}, u32[]{:S(2)}) collective-permute-start(bf16[80,5120]{1,0:T(8,128)(2,1)} %in_order.1.refs_9_), channel_id=1, source_target_pairs={{0,194},{2,0},{64,2},{66,64},{128,66},{130,128},{192,130},{194,192... | collective-permute-start | bytes 2457608 | tf_op jit(solution)/shard_map/ppermute | solution.py:26
  51.0 18.9 %collective-permute-start.9 = (bf16[8,24,960]{2,1,0:T(8,128)(2,1)S(1)}, bf16[8,24,960]{2,1,0:T(8,128)(2,1)S(1)}, u32[]{:S(2)}, u32[]{:S(2)}) collective-permute-start(bf16[8,24,960]{2,1,0:T(8,128)(2,1)S(1)} %all-to-all-done.refs_4_), channel_id=1, source_target_pairs={{0,48},{16,0},{32,16},{48,32},{1,49},{17,1},{33,17},{49,33},{2,50}... | collective-permute-start | bytes 1105928 | tf_op jit(solution)/shard_map/ppermute | solution.py:26
  52.8 17.1 %collective-permute-start.10 = (bf16[8,24,960]{2,1,0:T(8,128)(2,1)S(1)}, bf16[8,24,960]{2,1,0:T(8,128)(2,1)S(1)}, u32[]{:S(2)}, u32[]{:S(2)}) collective-permute-start(bf16[8,24,960]{2,1,0:T(8,128)(2,1)S(1)} %all-to-all-done.refs_4_), channel_id=1, source_target_pairs={{0,32},{16,48},{32,0},{48,16},{1,33},{17,49},{33,1},{49,17},{2,34}... | collective-permute-start | bytes 1105928 | tf_op jit(solution)/shard_map/ppermute | solution.py:26
  54.6 19.0 %collective-permute-start.11 = (bf16[8,24,960]{2,1,0:T(8,128)(2,1)S(1)}, bf16[8,24,960]{2,1,0:T(8,128)(2,1)S(1)}, u32[]{:S(2)}, u32[]{:S(2)}) collective-permute-start(bf16[8,24,960]{2,1,0:T(8,128)(2,1)S(1)} %all-to-all-done.refs_4_), channel_id=1, source_target_pairs={{0,16},{16,32},{32,48},{48,0},{1,17},{17,33},{33,49},{49,1},{2,18}... | collective-permute-start | bytes 1105928 | tf_op jit(solution)/shard_map/ppermute | solution.py:26
  74.9 3.8 %collective-permute-start.14 = (bf16[4,8,24,960]{3,2,1,0:T(8,128)(2,1)}, bf16[4,8,24,960]{3,2,1,0:T(8,128)(2,1)}, u32[]{:S(2)}, u32[]{:S(2)}) collective-permute-start(bf16[4,8,24,960]{3,2,1,0:T(8,128)(2,1)} %pad_maximum_fusion), channel_id=1, source_target_pairs={{0,1},{1,0},{2,3},{3,2},{4,5},{5,4},{6,7},{7,6},{8,9},{9,8},{10,11... | collective-permute-start | bytes 4423688 | tf_op jit(solution)/shard_map/ppermute | solution.py:30
  78.8 21.8 %collective-permute-start.19 = (bf16[80,5120]{1,0:T(8,128)(2,1)}, bf16[80,5120]{1,0:T(8,128)(2,1)}, u32[]{:S(2)}, u32[]{:S(2)}) collective-permute-start(bf16[80,5120]{1,0:T(8,128)(2,1)} %collective-permute-done.12.refs_10_), channel_id=1, source_target_pairs={{0,2},{2,64},{64,66},{66,128},{128,130},{130,192},{192,194},{194,0... | collective-permute-start | bytes 2457608 | tf_op jit(solution)/shard_map/ppermute | solution.py:26
  80.4 20.3 %collective-permute-start.20 = (bf16[80,5120]{1,0:T(8,128)(2,1)}, bf16[80,5120]{1,0:T(8,128)(2,1)}, u32[]{:S(2)}, u32[]{:S(2)}) collective-permute-start(bf16[80,5120]{1,0:T(8,128)(2,1)} %collective-permute-done.13.refs_11_), channel_id=1, source_target_pairs={{0,194},{2,0},{64,2},{66,64},{128,66},{130,128},{192,130},{194,192... | collective-permute-start | bytes 2457608 | tf_op jit(solution)/shard_map/ppermute | solution.py:26
  100.7 32.5 %collective-permute-start.21 = (bf16[80,5120]{1,0:T(8,128)(2,1)}, bf16[80,5120]{1,0:T(8,128)(2,1)S(1)}, u32[]{:S(2)}, u32[]{:S(2)}) collective-permute-start(bf16[80,5120]{1,0:T(8,128)(2,1)} %collective-permute-done.19.refs_12_), channel_id=1, source_target_pairs={{0,2},{2,64},{64,66},{66,128},{128,130},{130,192},{192,194},{194,0... | collective-permute-start | bytes 2457608 | tf_op jit(solution)/shard_map/ppermute | solution.py:26
  108.8 24.5 %collective-permute-start.22 = (bf16[80,5120]{1,0:T(8,128)(2,1)}, bf16[80,5120]{1,0:T(8,128)(2,1)}, u32[]{:S(2)}, u32[]{:S(2)}) collective-permute-start(bf16[80,5120]{1,0:T(8,128)(2,1)} %collective-permute-done.20.refs_13_), channel_id=1, source_target_pairs={{0,194},{2,0},{64,2},{66,64},{128,66},{130,128},{192,130},{194,192... | collective-permute-start | bytes 2457608 | tf_op jit(solution)/shard_map/ppermute | solution.py:26
  119.6 12.3 %collective-permute-start.16 = (bf16[320,768]{1,0:T(8,128)(2,1)}, bf16[320,768]{1,0:T(8,128)(2,1)S(1)}, u32[]{:S(2)}, u32[]{:S(2)}) collective-permute-start(bf16[320,768]{1,0:T(8,128)(2,1)} %attention.1.refs_0_), channel_id=1, source_target_pairs={{0,12},{4,0},{8,4},{12,8},{1,13},{5,1},{9,5},{13,9},{2,14},{6,2},{... | collective-permute-start | bytes 1474568 | tf_op jit(solution)/shard_map/ppermute | solution.py:26
  119.6 13.6 %collective-permute-start.18 = (bf16[320,768]{1,0:T(8,128)(2,1)}, bf16[320,768]{1,0:T(8,128)(2,1)}, u32[]{:S(2)}, u32[]{:S(2)}) collective-permute-start(bf16[320,768]{1,0:T(8,128)(2,1)} %attention.1.refs_0_), channel_id=1, source_target_pairs={{0,4},{4,8},{8,12},{12,0},{1,5},{5,9},{9,13},{13,1},{2,6},{6,10},{... | collective-permute-start | bytes 1474568 | tf_op jit(solution)/shard_map/ppermute | solution.py:26
  121.7 12.9 %collective-permute-start.24 = (bf16[80,5120]{1,0:T(8,128)(2,1)S(1)}, bf16[80,5120]{1,0:T(8,128)(2,1)S(1)}, u32[]{:S(2)}, u32[]{:S(2)}) collective-permute-start(bf16[80,5120]{1,0:T(8,128)(2,1)S(1)} %copy-done.13), channel_id=1, source_target_pairs={{0,1},{1,0},{2,3},{3,2},{4,5},{5,4},{6,7},{7,6},{8,9},{9,8},{10,11... | collective-permute-start | bytes 2457608 | tf_op jit(solution)/shard_map/ppermute | solution.py:30
  133.3 22.3 %collective-permute-start.23 = (bf16[80,5120]{1,0:T(8,128)(2,1)S(1)}, bf16[80,5120]{1,0:T(8,128)(2,1)}, u32[]{:S(2)}, u32[]{:S(2)}) collective-permute-start(bf16[80,5120]{1,0:T(8,128)(2,1)S(1)} %collective-permute-done.21.refs_14_), channel_id=1, source_target_pairs={{0,2},{2,64},{64,66},{66,128},{128,130},{130,192},{192,194},{194,0... | collective-permute-start | bytes 2457608 | tf_op jit(solution)/shard_map/ppermute | solution.py:26
  133.7 15.4 %collective-permute-start.17 = (bf16[320,768]{1,0:T(8,128)(2,1)}, bf16[320,768]{1,0:T(8,128)(2,1)S(1)}, u32[]{:S(2)}, u32[]{:S(2)}) collective-permute-start(bf16[320,768]{1,0:T(8,128)(2,1)} %attention.1.refs_0_), channel_id=1, source_target_pairs={{0,8},{4,12},{8,0},{12,4},{1,9},{5,13},{9,1},{13,5},{2,10},{6,14},... | collective-permute-start | bytes 1474568 | tf_op jit(solution)/shard_map/ppermute | solution.py:26
  134.6 23.4 %collective-permute-start.27 = (bf16[80,5120]{1,0:T(8,128)(2,1)}, bf16[80,5120]{1,0:T(8,128)(2,1)S(1)}, u32[]{:S(2)}, u32[]{:S(2)}) collective-permute-start(bf16[80,5120]{1,0:T(8,128)(2,1)} %collective-permute-done.19.refs_12_), channel_id=1, source_target_pairs={{0,1},{1,0},{2,3},{3,2},{4,5},{5,4},{6,7},{7,6},{8,9},{9,8},{10,11... | collective-permute-start | bytes 2457608 | tf_op jit(solution)/shard_map/ppermute | solution.py:30
  134.8 23.2 %collective-permute-start.28 = (bf16[80,5120]{1,0:T(8,128)(2,1)}, bf16[80,5120]{1,0:T(8,128)(2,1)}, u32[]{:S(2)}, u32[]{:S(2)}) collective-permute-start(bf16[80,5120]{1,0:T(8,128)(2,1)} %collective-permute-done.20.refs_13_), channel_id=1, source_target_pairs={{0,1},{1,0},{2,3},{3,2},{4,5},{5,4},{6,7},{7,6},{8,9},{9,8},{10,11... | collective-permute-start | bytes 2457608 | tf_op jit(solution)/shard_map/ppermute | solution.py:30
  135.8 22.2 %collective-permute-start.29 = (bf16[80,5120]{1,0:T(8,128)(2,1)S(1)}, bf16[80,5120]{1,0:T(8,128)(2,1)}, u32[]{:S(2)}, u32[]{:S(2)}) collective-permute-start(bf16[80,5120]{1,0:T(8,128)(2,1)S(1)} %collective-permute-done.21.refs_14_), channel_id=1, source_target_pairs={{0,1},{1,0},{2,3},{3,2},{4,5},{5,4},{6,7},{7,6},{8,9},{9,8},{10,11... | collective-permute-start | bytes 2457608 | tf_op jit(solution)/shard_map/ppermute | solution.py:30
  149.0 8.9 %collective-permute-start.30 = (bf16[80,5120]{1,0:T(8,128)(2,1)}, bf16[80,5120]{1,0:T(8,128)(2,1)}, u32[]{:S(2)}, u32[]{:S(2)}) collective-permute-start(bf16[80,5120]{1,0:T(8,128)(2,1)} %collective-permute-done.22.refs_15_), channel_id=1, source_target_pairs={{0,1},{1,0},{2,3},{3,2},{4,5},{5,4},{6,7},{7,6},{8,9},{9,8},{10,11... | collective-permute-start | bytes 2457608 | tf_op jit(solution)/shard_map/ppermute | solution.py:30
  181.2 29.4 %all-to-all-start.1 = ((bf16[4,320,768]{2,1,0:T(8,128)(2,1)}), bf16[4,320,768]{2,1,0:T(8,128)(2,1)S(1)}, u32[]{:S(2)}, u32[]{:S(2)}) async-start(bf16[4,320,768]{2,1,0:T(8,128)(2,1)} %get-tuple-element.36), calls=%async_computation.1 | async-start | bytes 3932160 | tf_op jit(solution)/shard_map/all_to_all | solution.py:419
  212.8 5.2 %collective-permute-start.33 = (f32[4,768]{1,0:T(4,128)S(1)}, f32[4,768]{1,0:T(4,128)S(1)}, u32[]{:S(2)}, u32[]{:S(2)}) collective-permute-start(f32[4,768]{1,0:T(4,128)S(1)} %pad_maximum_fusion.1), channel_id=1, source_target_pairs={{0,8},{4,12},{8,0},{12,4},{1,9},{5,13},{9,1},{13,5},{2,10},{6,14},... | collective-permute-start | bytes 36872 | tf_op jit(solution)/shard_map/ppermute | solution.py:26
  214.3 4.9 %collective-permute-start.34 = (f32[4,768]{1,0:T(4,128)S(1)}, f32[4,768]{1,0:T(4,128)S(1)}, u32[]{:S(2)}, u32[]{:S(2)}) collective-permute-start(f32[4,768]{1,0:T(4,128)S(1)} %pad_maximum_fusion.1), channel_id=1, source_target_pairs={{0,4},{4,8},{8,12},{12,0},{1,5},{5,9},{9,13},{13,1},{2,6},{6,10},{... | collective-permute-start | bytes 36872 | tf_op jit(solution)/shard_map/ppermute | solution.py:26
  (36 other events, 419.2 us)

commit v4 on v2

--- a/solution.py
+++ b/solution.py
@@ -89,62 +89,88 @@
     return jnp.sum(lax.fori_loop(0, count, step, jnp.zeros((8, width), F32)), axis=0, keepdims=True)
 
 
-def attention_kernel(start_ref, q_ref, before_ref, own_ref, o_ref):
-    heads = q_ref.shape[0] // HD
-
-    def window(kind, head, block):
-        rows = pl.ds(pl.multiple_of((kind * heads + head) * HD, HD), HD)
-        ref, block = (before_ref, block) if block < 2 else (own_ref, block - 2)
-        return ref[rows, block * BLOCK : (block + 1) * BLOCK]
-
+def attend(head, heads, part, start_ref, q_ref, window, o_ref, cols):
     key_row = lax.broadcasted_iota(jnp.int32, (BLOCK, BLOCK), 0)
     query_col = lax.broadcasted_iota(jnp.int32, (BLOCK, BLOCK), 1)
-    causal = key_row <= query_col
+    span = pl.ds(pl.multiple_of(head * HD, HD), HD)
+    own = slice(part * BLOCK, (part + 1) * BLOCK)
+    query = q_ref[span, own]
+    start = start_ref[:, own]
+    scores = []
+    for step in range(3):
+        base = (part + step) * BLOCK
+        score = lax.dot_general(
+            window(head, part + step), query, (((0,), (0,)), ((), ())), preferred_element_type=F32
+        )
+        allowed = key_row >= start - base
+        if step == 2:
+            allowed = allowed & (key_row <= query_col)
+        scores.append(jnp.where(allowed, score, -1e30))
+    top = jnp.maximum(jnp.maximum(scores[0], scores[1]), scores[2])
+    top = jnp.max(top, axis=0, keepdims=True)
+    total = jnp.zeros((1, BLOCK), F32)
+    mixed = jnp.zeros((HD, BLOCK), F32)
+    for step in range(3):
+        weight = jnp.exp2((scores[step] - top) * (math.sqrt(HD) * LOG2E))
+        total = total + jnp.sum(weight, axis=0, keepdims=True)
+        mixed = mixed + jnp.dot(
+            window(heads + head, part + step), weight.astype(BF16), preferred_element_type=F32
+        )
+    o_ref[span, cols] = (mixed / total).astype(BF16)
+
+
+def window_of(own_ref, before_ref):
+    def window(row, block):
+        span = pl.ds(pl.multiple_of(row * HD, HD), HD)
+        ref, block = (before_ref, block) if block < 2 else (own_ref, block - 2)
+        return ref[span, block * BLOCK : (block + 1) * BLOCK]
+
+    return window
+
+
+def recent_kernel(start_ref, q_ref, own_ref, o_ref):
+    heads = q_ref.shape[0] // HD
 
     def one_head(head, carry):
-        rows = pl.ds(pl.multiple_of(head * HD, HD), HD)
-        for part in range(q_ref.shape[1] // BLOCK):
+        attend(head, heads, 2, start_ref, q_ref, window_of(own_ref, None), o_ref, slice(0, BLOCK))
+        return carry
+
+    lax.fori_loop(0, heads, one_head, 0)
+
+
+def attention_kernel(start_ref, q_ref, before_ref, own_ref, recent_ref, o_ref):
+    heads = q_ref.shape[0] // HD
+    o_ref[:, 2 * BLOCK :] = recent_ref[...]
+
+    def one_head(head, carry):
+        for part in range(2):
             cols = slice(part * BLOCK, (part + 1) * BLOCK)
-            query = q_ref[rows, cols]
-            start = start_ref[:, cols]
-            scores = []
-            for step in range(3):
-                base = (part + step) * BLOCK
-                keys = window(0, head, part + step)
-                score = lax.dot_general(
-                    keys, query, (((0,), (0,)), ((), ())), preferred_element_type=F32
-                )
-                allowed = key_row >= start - base
-                if step == 2:
-                    allowed = allowed & causal
-                scores.append(jnp.where(allowed, score, -1e30))
-            top = jnp.maximum(jnp.maximum(scores[0], scores[1]), scores[2])
-            top = jnp.max(top, axis=0, keepdims=True)
-            total = jnp.zeros((1, BLOCK), F32)
-            mixed = jnp.zeros((HD, BLOCK), F32)
-            for step in range(3):
-                weight = jnp.exp2((scores[step] - top) * (math.sqrt(HD) * LOG2E))
-                total = total + jnp.sum(weight, axis=0, keepdims=True)
-                mixed = mixed + jnp.dot(
-                    window(1, head, part + step),
-                    weight.astype(BF16),
-                    preferred_element_type=F32,
-                )
-            o_ref[rows, cols] = (mixed / total).astype(BF16)
+            attend(head, heads, part, start_ref, q_ref, window_of(own_ref, before_ref), o_ref, cols)
         return carry
 
     lax.fori_loop(0, heads, one_head, 0)
 
 
-def attention(start, query, before, own):
+def attention_recent(start, query, own):
+    return pl.pallas_call(
+        recent_kernel,
+        out_shape=jax.ShapeDtypeStruct((query.shape[0], BLOCK), BF16),
+        in_specs=[NEAR] * 3,
+        out_specs=NEAR,
+        cost_estimate=pl.CostEstimate(flops=260_000_000, bytes_accessed=2_000_000, transcendentals=1_000_000),
+        name="attention_recent",
+    )(start, query, own)
+
+
+def attention(start, query, before, own, recent):
     return pl.pallas_call(
         attention_kernel,
         out_shape=jax.ShapeDtypeStruct(query.shape, BF16),
-        in_specs=[pl.BlockSpec(memory_space=pltpu.VMEM)] * 4,
-        out_specs=pl.BlockSpec(memory_space=pltpu.VMEM),
-        cost_estimate=pl.CostEstimate(flops=800_000_000, bytes_accessed=4_000_000, transcendentals=3_000_000),
+        in_specs=[NEAR] * 5,
+        out_specs=NEAR,
+        cost_estimate=pl.CostEstimate(flops=520_000_000, bytes_accessed=4_000_000, transcendentals=2_000_000),
         name="attention",
-    )(start, query, before, own)
+    )(start, query, before, own, recent)
 
 
 def stream_starts(segment):
@@ -155,24 +181,28 @@
 
 def project_kernel(place_ref, *refs):
     x_refs, near_refs, far_refs, gain_ref, cos_ref, sin_ref = refs[:4], refs[4:8], refs[8], *refs[9:12]
-    query_ref, own_ref, features_ref, size_ref, held, weight, result = refs[12:]
+    query_ref, own_ref, features_ref, size_ref, held, weight, result, sems = refs[12:]
     tp, core, spot_y = place_ref[0], place_ref[1], place_ref[3]
     local, rows = query_ref.shape
+    copies = []
+    for away, ref in enumerate(near_refs):
+        y = (spot_y + away) % 4
+        copies.append(pltpu.make_async_copy(ref, weight.at[:, core, y], sems.at[away]))
+        copies.append(pltpu.make_async_copy(far_refs.at[away], weight.at[:, 1 - core, y], sems.at[4 + away]))
+    for copy in copies:
+        copy.start()
     held[...] = jnp.zeros_like(held)
     for away, ref in enumerate(x_refs):
         block = (tp + away) % 4
         features_ref[pl.ds(pl.multiple_of(block * local, local), local), :] = ref[...]
         for shard in range(16):
             held[block, shard, :SHARD] = ref[shard * SHARD : (shard + 1) * SHARD]
-    for away, ref in enumerate(near_refs):
-        y = (spot_y + away) % 4
-        for z in range(8):
-            weight[z, core, y] = ref[z]
-            weight[z, 1 - core, y] = far_refs[away, z]
     size = lax.rsqrt(
         chunk_squares(lambda i: features_ref[pl.ds(pl.multiple_of(i * 128, 128), 128), :], D // 128, rows) + EPS
     )
     size_ref[...] = size
+    for copy in copies:
+        copy.wait()
     for kind in range(3):
         part = weight[..., kind * local : (kind + 1) * local].reshape(WIDE, local)
         turned = jnp.transpose(part)
@@ -210,12 +240,13 @@
             jax.ShapeDtypeStruct((D, rows), BF16),
             jax.ShapeDtypeStruct((1, rows), F32),
         ],
-        in_specs=[SMALL] + [NEAR] * 12,
+        in_specs=[SMALL] + [NEAR] * 4 + [FAR] * 5 + [NEAR] * 3,
         out_specs=[NEAR] * 4,
         scratch_shapes=[
             pltpu.VMEM((4, 16, PADDED, rows), BF16),
             pltpu.VMEM((8, 2, 4, PADDED, 3 * local), BF16),
             pltpu.VMEM((3 * local, rows), F32),
+            pltpu.SemaphoreType.DMA((8,)),
         ],
         compiler_params=pltpu.CompilerParams(vmem_limit_bytes=40 * 2**20),
         cost_estimate=pl.CostEstimate(flops=1_900_000_000, bytes_accessed=12_000_000, transcendentals=0),
@@ -378,9 +409,7 @@
     spot_z = lax.axis_index("zh") * 2 + lax.axis_index("zl")
     spot = jnp.stack([tp, core, spot_z, spot_y]).astype(jnp.int32)
 
-    qkv = jnp.pad(qkv_weight.astype(BF16).reshape(SHARD, 3 * local), ((0, PADDED - SHARD), (0, 0)))
-    everywhere = jnp.broadcast_to(qkv[None], (8,) + qkv.shape)
-    qkv_z = lax.all_to_all(everywhere, Z, 0, 0, tiled=True)
+    out_rows = four_blocks(out_weight.T.astype(BF16), "tp")
     blocks = four_blocks(kernel_order(tokens[0].T), "tp")
 
     starts = stream_starts(segment_ids[0])
@@ -396,9 +425,12 @@
     attn_step = kernel_order(attn_rate)[:, None]
     step_block = lax.dynamic_slice_in_dim(kernel_order(mlp_rate), tp * local, local)[:, None]
 
-    out_rows = four_blocks(out_weight.T.astype(BF16), "tp")
     wide = gate_up_weight.astype(BF16).reshape(SHARD, 2 * hidden)
     rest = jnp.concatenate(out_rows + [wide, down_weight.T.astype(BF16)], axis=1)
+    (shard,) = after([qkv_weight.astype(BF16)], rest)
+    qkv = jnp.pad(shard.reshape(SHARD, 3 * local), ((0, PADDED - SHARD), (0, 0)))
+    everywhere = jnp.broadcast_to(qkv[None], (8,) + qkv.shape)
+    qkv_z = lax.all_to_all(everywhere, Z, 0, 0, tiled=True)
     rest_y = in_order(spot, 3, four_blocks(rest, "y"), (0, 1, 2, 3))
 
     (qkv_z,) = after([qkv_z], rest_y, cosine, sine, key_start, gain, attn_step, step_block, *blocks)
@@ -408,9 +440,11 @@
     qkv_far = swap_core(qkv_stack)
     query, own, features, size = project(spot, blocks, qkv_near, qkv_far, gain, cosine, sine)
     before = lax.ppermute(own[:, rows - window :], ("zl", "co"), [(i, i + 1) for i in range(3)])
-    attended = attention(key_start, query, before, own)
+    recent = attention_recent(key_start, query, own)
+    (before,) = after([before], recent)
+    attended = attention(key_start, query, before, own, recent)
     everyone = four_blocks(attended, "tp")
-    near = ring_z(rest_y, ahead, behind, {1: (qkv_far,), 2: (attended,), 3: (everyone[1], everyone[3])})
+    near = ring_z(rest_y, ahead, behind, {2: (before, recent), 3: (everyone[1], everyone[3])})
     far = [swap_core(block) for block in near]
     parts, mixed = layer(
         spot, everyone, features, size, attn_step, up_scale[None], gate_scale[None], near, far

time: 216 us -> 207 us (0.958)
  starting transfers between devices: 64.2 us -> 52.6 us
  Pallas kernels: 40.2 us -> 43.4 us
    ppermute x25, starting transfers between devices: 49.2 us -> 37.5 us  [shift(): return lax.ppermute(block, axis, ring(count, step))]
    ppermute x25, waiting for transfers between devices: 54.3 us -> 59.8 us  [shift(): return lax.ppermute(block, axis, ring(count, step))]
    pallas_call x0 -> x1, Pallas kernels: none -> 5.23 us  [attention_recent(): pl.pallas_call(recent_kernel, out_shape=jax.ShapeDtypeStruct((query.shape...]
    ppermute x9, waiting for transfers between devices: 3.93 us -> 1.34 us  [swap_core(): return lax.ppermute(block, 'co', [(0, 1), (1, 0)])]
    unnamed x72 -> x70, local copies, waits for them, and re-layouts: 8.9 us -> 8.06 us
  transfers between devices with their start and end apart: 37 -> 37, of which waited for: 18 -> 16; matrix products, arithmetic and copies ran while one was open for 5% -> 5% of each run, Pallas kernels for 8% -> 10%
where the time goes in v4:
time: 207 us; the launch traced here: 205 us
  waiting for transfers between devices  86.7 us (42%)
  starting transfers between devices  52.6 us (25%)
  Pallas kernels  43.4 us (21%)
  local copies, waits for them, and re-layouts  15.8 us (8%)
  other arithmetic  5.73 us (3%)
    ppermute x25, waiting for transfers between devices, shift(): return lax.ppermute(block, axis, ring(count, step))  59.8 us
    ppermute x25, starting transfers between devices, shift(): return lax.ppermute(block, axis, ring(count, step))  37.5 us
    all_to_all x1, waiting for transfers between devices, body(): landed = lax.all_to_all(parts, 'tp', 0, 0, tiled=True).astype(F32)  25.5 us
    pallas_call x1, Pallas kernels, layer(): pl.pallas_call(layer_kernel, out_shape=[jax.ShapeDtypeStruct((4, local, r...  22.3 us
    all_to_all x1, starting transfers between devices, body(): qkv_z = lax.all_to_all(everywhere, Z, 0, 0, tiled=True)  8.47 us
    unnamed x70, local copies, waits for them, and re-layouts  8.06 us
    pallas_call x1, Pallas kernels, attention(): pl.pallas_call(attention_kernel, out_shape=jax.ShapeDtypeStruct(query.sha...  7.54 us
    pallas_call x1, Pallas kernels, project(): pl.pallas_call(project_kernel, out_shape=[jax.ShapeDtypeStruct((local, ro...  5.85 us
  transfers between devices with their start and end apart: 37, of which 16 were waited for; matrix products, arithmetic and copies ran while one was open for 5% of the time, Pallas kernels for 10%

profile of v4, /device:TPU:16, one launch (start us, length us, event | category | flops | bytes accessed | tf_op | source)
XLA Modules:
  0.0 204.8 jit_solution(1176656747235222890)
XLA Ops:
  0.8 2.8 %collective-permute-start.3 = (bf16[20,320]{1,0:T(8,128)(2,1)S(1)}, bf16[20,320]{1,0:T(8,128)(2,1)S(1)}, u32[]{:S(2)}, u32[]{:S(2)}) collective-permute-start(bf16[20,320]{1,0:T(8,128)(2,1)S(1)} %convert_bitcast_fusion.1), channel_id=1, source_target_pairs={{0,12},{4,0},{8,4},{12,8},{1,13},{5,1},{9,5},{13,9},{2,14},{6,2},{... | collective-permute-start | bytes 38408 | tf_op jit(solution)/shard_map/ppermute | solution.py:26
  6.6 2.4 %collective-permute-start = (bf16[320,768]{1,0:T(8,128)(2,1)S(1)}, bf16[320,768]{1,0:T(8,128)(2,1)S(1)}, u32[]{:S(2)}, u32[]{:S(2)}) collective-permute-start(bf16[320,768]{1,0:T(8,128)(2,1)S(1)} %reshape.58.refs_0_), channel_id=1, source_target_pairs={{0,12},{4,0},{8,4},{12,8},{1,13},{5,1},{9,5},{13,9},{2,14},{6,2},{... | collective-permute-start | bytes 1474568 | tf_op jit(solution)/shard_map/ppermute | solution.py:26
  9.0 1.5 collective-permute-start.1
  14.2 8.5 %all-to-all-start = ((bf16[8,24,960]{2,1,0:T(8,128)(2,1)}), bf16[8,24,960]{2,1,0:T(8,128)(2,1)S(1)}, u32[]{:S(2)}, u32[]{:S(2)}) async-start(bf16[8,24,960]{2,1,0:T(8,128)(2,1)} %broadcast_in_dim.31), calls=%async_computation | async-start | bytes 786432 | tf_op jit(solution)/shard_map/all_to_all | solution.py:433
  22.8 2.9 %collective-permute-start.7 = (bf16[20,5120]{1,0:T(8,128)(2,1)S(1)}, bf16[20,5120]{1,0:T(8,128)(2,1)S(1)}, u32[]{:S(2)}, u32[]{:S(2)}) collective-permute-start(bf16[20,5120]{1,0:T(8,128)(2,1)S(1)} %concatenate.10.refs_0_), channel_id=1, source_target_pairs={{0,32},{16,48},{32,0},{48,16},{1,33},{17,49},{33,1},{49,17},{2,34}... | collective-permute-start | bytes 614408 | tf_op jit(solution)/shard_map/ppermute | solution.py:26
  27.3 5.4 %collective-permute-done.7.refs_2_ = bf16[20,5120]{1,0:T(8,128)(2,1)S(1)} collective-permute-done((bf16[20,5120]{1,0:T(8,128)(2,1)S(1)}, bf16[20,5120]{1,0:T(8,128)(2,1)S(1)}, u32[]{:S(2)}, u32[]{:S(2)}) %collective-permute-start.7) | collective-permute-done | bytes 204832 | tf_op jit(solution)/shard_map/ppermute | solution.py:26
  32.8 2.6 %collective-permute-done.8.refs_3_ = bf16[20,5120]{1,0:T(8,128)(2,1)S(1)} collective-permute-done((bf16[20,5120]{1,0:T(8,128)(2,1)S(1)}, bf16[20,5120]{1,0:T(8,128)(2,1)S(1)}, u32[]{:S(2)}, u32[]{:S(2)}) %collective-permute-start.8) | collective-permute-done | bytes 204832 | tf_op jit(solution)/shard_map/ppermute | solution.py:26
  36.0 2.5 %in_order.1.refs_9_ = bf16[80,5120]{1,0:T(8,128)(2,1)} custom-call(s32[4]{0:T(128)} %pad_add_fusion.place_ref, bf16[20,5120]{1,0:T(8,128)(2,1)} %copy-done.12, bf16[20,5120]{1,0:T(8,128)(2,1)} %copy-done.14, bf16[20,5120]{1,0:T(8,128)(2,1)} %copy-done.15, bf16[20,5120]{1,0:T(8,128)(2,1)} %copy-done.16), custom_call_target="tpu_custom_call" | custom-call | bytes 1638400 | tf_op jit(solution)/shard_map/in_order/pallas_call | solution.py:62
  38.5 1.7 collective-permute-start.12
  40.3 1.5 collective-permute-start.13
  43.7 2.9 %collective-permute-start.10 = (bf16[8,24,960]{2,1,0:T(8,128)(2,1)S(1)}, bf16[8,24,960]{2,1,0:T(8,128)(2,1)S(1)}, u32[]{:S(2)}, u32[]{:S(2)}) collective-permute-start(bf16[8,24,960]{2,1,0:T(8,128)(2,1)S(1)} %all-to-all-done.refs_4_), channel_id=1, source_target_pairs={{0,32},{16,48},{32,0},{48,16},{1,33},{17,49},{33,1},{49,17},{2,34}... | collective-permute-start | bytes 1105928 | tf_op jit(solution)/shard_map/ppermute | solution.py:26
  46.6 2.0 collective-permute-start.11
  48.7 6.5 %collective-permute-done.9.refs_5_ = bf16[8,24,960]{2,1,0:T(8,128)(2,1)S(1)} collective-permute-done((bf16[8,24,960]{2,1,0:T(8,128)(2,1)S(1)}, bf16[8,24,960]{2,1,0:T(8,128)(2,1)S(1)}, u32[]{:S(2)}, u32[]{:S(2)}) %collective-permute-start.9) | collective-permute-done | bytes 368672 | tf_op jit(solution)/shard_map/ppermute | solution.py:26
  55.2 2.1 %collective-permute-done.10.refs_6_ = bf16[8,24,960]{2,1,0:T(8,128)(2,1)S(1)} collective-permute-done((bf16[8,24,960]{2,1,0:T(8,128)(2,1)S(1)}, bf16[8,24,960]{2,1,0:T(8,128)(2,1)S(1)}, u32[]{:S(2)}, u32[]{:S(2)}) %collective-permute-start.10) | collective-permute-done | bytes 368672 | tf_op jit(solution)/shard_map/ppermute | solution.py:26
  57.3 5.3 %collective-permute-done.11.refs_7_ = bf16[8,24,960]{2,1,0:T(8,128)(2,1)S(1)} collective-permute-done((bf16[8,24,960]{2,1,0:T(8,128)(2,1)S(1)}, bf16[8,24,960]{2,1,0:T(8,128)(2,1)S(1)}, u32[]{:S(2)}, u32[]{:S(2)}) %collective-permute-start.11) | collective-permute-done | bytes 368672 | tf_op jit(solution)/shard_map/ppermute | solution.py:26
  62.6 1.3 pad_maximum_fusion
  64.5 3.0 %collective-permute-start.20 = (bf16[80,5120]{1,0:T(8,128)(2,1)}, bf16[80,5120]{1,0:T(8,128)(2,1)}, u32[]{:S(2)}, u32[]{:S(2)}) collective-permute-start(bf16[80,5120]{1,0:T(8,128)(2,1)} %collective-permute-done.13.refs_11_), channel_id=1, source_target_pairs={{0,194},{2,0},{64,2},{66,64},{128,66},{130,128},{192,130},{194,192... | collective-permute-start | bytes 2457608 | tf_op jit(solution)/shard_map/ppermute | solution.py:26
  70.9 5.8 %project.1 = (bf16[320,768]{1,0:T(8,128)(2,1)S(1)}, bf16[640,768]{1,0:T(8,128)(2,1)S(1)}, bf16[1280,768]{1,0:T(8,128)(2,1)S(1)}, f32[1,768]{1,0:T(1,128)S(1)}) custom-call(s32[4]{0:T(128)S(1)} %copy-done.1, bf16[320,768]{1,0:T(8,128)(2,1)S(1)} %reshape.58.refs_0_, bf16[320,768]{1,0:T(8,128)(2,1)S(1)} %copy-done.3, bf16[320,768]{1,0:T(8,128)(2,1)S(1)} %copy-done.5, ...), custom_call_target="tpu_custom_call" | custom-call | flops 1900000000 | bytes 12000000 | tf_op jit(solution)/shard_map/project/pallas_call | solution.py:235
  79.5 2.1 %collective-permute-start.15 = (bf16[640,512]{1,0:T(8,128)(2,1)S(1)}, bf16[640,512]{1,0:T(8,128)(2,1)S(1)}, u32[]{:S(2)}, u32[]{:S(2)}) collective-permute-start(bf16[640,512]{1,0:T(8,128)(2,1)S(1)} %slice.52), channel_id=1, source_target_pairs={{0,1},{1,2},{2,3},{4,5},{5,6},{6,7},{8,9},{9,10},{10,11},{12,13},{... | collective-permute-start | bytes 1966088 | tf_op jit(solution)/shard_map/ppermute | solution.py:442
  81.6 5.2 %attention_recent.1.recent_ref = bf16[320,256]{1,0:T(8,128)(2,1)} custom-call(s32[1,768]{1,0:T(1,128)} %broadcast_in_dim.30.start_ref, bf16[320,768]{1,0:T(8,128)(2,1)} %copy-done.8, bf16[640,768]{1,0:T(8,128)(2,1)} %copy-done), custom_call_target="tpu_custom_call" | custom-call | flops 260000000 | bytes 2000000 | tf_op jit(solution)/shard_map/attention_recent/pallas_call | solution.py:155
  86.8 5.7 %collective-permute-start.21 = (bf16[80,5120]{1,0:T(8,128)(2,1)}, bf16[80,5120]{1,0:T(8,128)(2,1)S(1)}, u32[]{:S(2)}, u32[]{:S(2)}) collective-permute-start(bf16[80,5120]{1,0:T(8,128)(2,1)} %collective-permute-done.19.refs_12_), channel_id=1, source_target_pairs={{0,2},{2,64},{64,66},{66,128},{128,130},{130,192},{192,194},{194,0... | collective-permute-start | bytes 2457608 | tf_op jit(solution)/shard_map/ppermute | solution.py:26
  93.8 7.5 %attention.1.refs_0_ = bf16[320,768]{1,0:T(8,128)(2,1)} custom-call(s32[1,768]{1,0:T(1,128)} %broadcast_in_dim.30.start_ref, bf16[320,768]{1,0:T(8,128)(2,1)} %copy-done.8, bf16[640,512]{1,0:T(8,128)(2,1)} %copy-done.32, bf16[640,768]{1,0:T(8,128)(2,1)} %copy-done, bf16[320,256]{1,0:T(8,128)(2,1)} %attention_recent.1.recent_ref), custom_call_target="tpu_custom_call" | custom-call | flops 520000000 | bytes 4000000 | tf_op jit(solution)/shard_map/attention/pallas_call | solution.py:166
  101.3 2.6 %collective-permute-start.16 = (bf16[320,768]{1,0:T(8,128)(2,1)}, bf16[320,768]{1,0:T(8,128)(2,1)}, u32[]{:S(2)}, u32[]{:S(2)}) collective-permute-start(bf16[320,768]{1,0:T(8,128)(2,1)} %attention.1.refs_0_), channel_id=1, source_target_pairs={{0,12},{4,0},{8,4},{12,8},{1,13},{5,1},{9,5},{13,9},{2,14},{6,2},{... | collective-permute-start | bytes 1474568 | tf_op jit(solution)/shard_map/ppermute | solution.py:26
  104.0 10.0 %collective-permute-done.16.refs_1_ = bf16[320,768]{1,0:T(8,128)(2,1)} collective-permute-done((bf16[320,768]{1,0:T(8,128)(2,1)}, bf16[320,768]{1,0:T(8,128)(2,1)}, u32[]{:S(2)}, u32[]{:S(2)}) %collective-permute-start.16) | collective-permute-done | bytes 491552 | tf_op jit(solution)/shard_map/ppermute | solution.py:26
  114.0 3.4 %collective-permute-done.18.refs_3_ = bf16[320,768]{1,0:T(8,128)(2,1)} collective-permute-done((bf16[320,768]{1,0:T(8,128)(2,1)}, bf16[320,768]{1,0:T(8,128)(2,1)}, u32[]{:S(2)}, u32[]{:S(2)}) %collective-permute-start.18) | collective-permute-done | bytes 491552 | tf_op jit(solution)/shard_map/ppermute | solution.py:26
  120.1 13.6 %collective-permute-done.17.refs_2_ = bf16[320,768]{1,0:T(8,128)(2,1)S(1)} collective-permute-done((bf16[320,768]{1,0:T(8,128)(2,1)}, bf16[320,768]{1,0:T(8,128)(2,1)S(1)}, u32[]{:S(2)}, u32[]{:S(2)}) %collective-permute-start.17) | collective-permute-done | bytes 491552 | tf_op jit(solution)/shard_map/ppermute | solution.py:26
  133.6 6.0 %collective-permute-done.23.refs_16_ = bf16[80,5120]{1,0:T(8,128)(2,1)} collective-permute-done((bf16[80,5120]{1,0:T(8,128)(2,1)S(1)}, bf16[80,5120]{1,0:T(8,128)(2,1)}, u32[]{:S(2)}, u32[]{:S(2)}) %collective-permute-start.23) | collective-permute-done | bytes 819232 | tf_op jit(solution)/shard_map/ppermute | solution.py:26
  143.0 22.3 %layer.1 = (bf16[4,320,768]{2,1,0:T(8,128)(2,1)}, f32[320,768]{1,0:T(8,128)}) custom-call(s32[4]{0:T(128)} %pad_add_fusion.place_ref, bf16[320,768]{1,0:T(8,128)(2,1)} %attention.1.refs_0_, bf16[320,768]{1,0:T(8,128)(2,1)} %collective-permute-done.16.refs_1_, bf16[320,768]{1,0:T(8,128)(2,1)} %copy-done.33, bf16[320,768]{1,0:T(8,128)(2,1)} %collective-permute-done.18.refs_3_, ...), custom_call_target="tpu_custom_call" | custom-call | flops 10000000000 | bytes 20000000 | tf_op jit(solution)/shard_map/layer/pallas_call | solution.py:355
  165.3 3.6 %all-to-all-start.1 = ((bf16[4,320,768]{2,1,0:T(8,128)(2,1)}), bf16[4,320,768]{2,1,0:T(8,128)(2,1)S(1)}, u32[]{:S(2)}, u32[]{:S(2)}) async-start(bf16[4,320,768]{2,1,0:T(8,128)(2,1)} %get-tuple-element.36), calls=%async_computation.1 | async-start | bytes 3932160 | tf_op jit(solution)/shard_map/all_to_all | solution.py:452
  169.3 25.5 %all-to-all-done.1 = bf16[4,320,768]{2,1,0:T(8,128)(2,1)S(1)} async-done(((bf16[4,320,768]{2,1,0:T(8,128)(2,1)}), bf16[4,320,768]{2,1,0:T(8,128)(2,1)S(1)}, u32[]{:S(2)}, u32[]{:S(2)}) %all-to-all-start.1) | async-done | bytes 1966112 | tf_op jit(solution)/shard_map/all_to_all | solution.py:452
  197.0 1.5 collective-permute-start.33
  199.5 2.7 %collective-permute-done.33 = f32[4,768]{1,0:T(4,128)S(1)} collective-permute-done((f32[4,768]{1,0:T(4,128)S(1)}, f32[4,768]{1,0:T(4,128)S(1)}, u32[]{:S(2)}, u32[]{:S(2)}) %collective-permute-start.33) | collective-permute-done | bytes 12320 | tf_op jit(solution)/shard_map/ppermute | solution.py:26
  (168 shorter events, 31.6 us)
Async XLA Ops:
  0.8 11.8 %collective-permute-start.3 = (bf16[20,320]{1,0:T(8,128)(2,1)S(1)}, bf16[20,320]{1,0:T(8,128)(2,1)S(1)}, u32[]{:S(2)}, u32[]{:S(2)}) collective-permute-start(bf16[20,320]{1,0:T(8,128)(2,1)S(1)} %convert_bitcast_fusion.1), channel_id=1, source_target_pairs={{0,12},{4,0},{8,4},{12,8},{1,13},{5,1},{9,5},{13,9},{2,14},{6,2},{... | collective-permute-start | bytes 38408 | tf_op jit(solution)/shard_map/ppermute | solution.py:26
  3.5 9.1 %collective-permute-start.4 = (bf16[20,320]{1,0:T(8,128)(2,1)S(1)}, bf16[20,320]{1,0:T(8,128)(2,1)S(1)}, u32[]{:S(2)}, u32[]{:S(2)}) collective-permute-start(bf16[20,320]{1,0:T(8,128)(2,1)S(1)} %convert_bitcast_fusion.1), channel_id=1, source_target_pairs={{0,8},{4,12},{8,0},{12,4},{1,9},{5,13},{9,1},{13,5},{2,10},{6,14},... | collective-permute-start | bytes 38408 | tf_op jit(solution)/shard_map/ppermute | solution.py:26
  4.3 8.3 %collective-permute-start.5 = (bf16[20,320]{1,0:T(8,128)(2,1)S(1)}, bf16[20,320]{1,0:T(8,128)(2,1)S(1)}, u32[]{:S(2)}, u32[]{:S(2)}) collective-permute-start(bf16[20,320]{1,0:T(8,128)(2,1)S(1)} %convert_bitcast_fusion.1), channel_id=1, source_target_pairs={{0,4},{4,8},{8,12},{12,0},{1,5},{5,9},{9,13},{13,1},{2,6},{6,10},{... | collective-permute-start | bytes 38408 | tf_op jit(solution)/shard_map/ppermute | solution.py:26
  6.6 35.6 %collective-permute-start = (bf16[320,768]{1,0:T(8,128)(2,1)S(1)}, bf16[320,768]{1,0:T(8,128)(2,1)S(1)}, u32[]{:S(2)}, u32[]{:S(2)}) collective-permute-start(bf16[320,768]{1,0:T(8,128)(2,1)S(1)} %reshape.58.refs_0_), channel_id=1, source_target_pairs={{0,12},{4,0},{8,4},{12,8},{1,13},{5,1},{9,5},{13,9},{2,14},{6,2},{... | collective-permute-start | bytes 1474568 | tf_op jit(solution)/shard_map/ppermute | solution.py:26
  9.0 33.2 %collective-permute-start.1 = (bf16[320,768]{1,0:T(8,128)(2,1)S(1)}, bf16[320,768]{1,0:T(8,128)(2,1)S(1)}, u32[]{:S(2)}, u32[]{:S(2)}) collective-permute-start(bf16[320,768]{1,0:T(8,128)(2,1)S(1)} %reshape.58.refs_0_), channel_id=1, source_target_pairs={{0,8},{4,12},{8,0},{12,4},{1,9},{5,13},{9,1},{13,5},{2,10},{6,14},... | collective-permute-start | bytes 1474568 | tf_op jit(solution)/shard_map/ppermute | solution.py:26
  12.6 29.7 %collective-permute-start.2 = (bf16[320,768]{1,0:T(8,128)(2,1)S(1)}, bf16[320,768]{1,0:T(8,128)(2,1)S(1)}, u32[]{:S(2)}, u32[]{:S(2)}) collective-permute-start(bf16[320,768]{1,0:T(8,128)(2,1)S(1)} %reshape.58.refs_0_), channel_id=1, source_target_pairs={{0,4},{4,8},{8,12},{12,0},{1,5},{5,9},{9,13},{13,1},{2,6},{6,10},{... | collective-permute-start | bytes 1474568 | tf_op jit(solution)/shard_map/ppermute | solution.py:26
  12.8 12.9 %collective-permute-start.6 = (bf16[20,5120]{1,0:T(8,128)(2,1)S(1)}, bf16[20,5120]{1,0:T(8,128)(2,1)S(1)}, u32[]{:S(2)}, u32[]{:S(2)}) collective-permute-start(bf16[20,5120]{1,0:T(8,128)(2,1)S(1)} %concatenate.10.refs_0_), channel_id=1, source_target_pairs={{0,48},{16,0},{32,16},{48,32},{1,49},{17,1},{33,17},{49,33},{2,50}... | collective-permute-start | bytes 614408 | tf_op jit(solution)/shard_map/ppermute | solution.py:26
  14.2 28.9 %all-to-all-start = ((bf16[8,24,960]{2,1,0:T(8,128)(2,1)}), bf16[8,24,960]{2,1,0:T(8,128)(2,1)S(1)}, u32[]{:S(2)}, u32[]{:S(2)}) async-start(bf16[8,24,960]{2,1,0:T(8,128)(2,1)} %broadcast_in_dim.31), calls=%async_computation | async-start | bytes 786432 | tf_op jit(solution)/shard_map/all_to_all | solution.py:433
  22.8 10.0 %collective-permute-start.7 = (bf16[20,5120]{1,0:T(8,128)(2,1)S(1)}, bf16[20,5120]{1,0:T(8,128)(2,1)S(1)}, u32[]{:S(2)}, u32[]{:S(2)}) collective-permute-start(bf16[20,5120]{1,0:T(8,128)(2,1)S(1)} %concatenate.10.refs_0_), channel_id=1, source_target_pairs={{0,32},{16,48},{32,0},{48,16},{1,33},{17,49},{33,1},{49,17},{2,34}... | collective-permute-start | bytes 614408 | tf_op jit(solution)/shard_map/ppermute | solution.py:26
  25.7 9.6 %collective-permute-start.8 = (bf16[20,5120]{1,0:T(8,128)(2,1)S(1)}, bf16[20,5120]{1,0:T(8,128)(2,1)S(1)}, u32[]{:S(2)}, u32[]{:S(2)}) collective-permute-start(bf16[20,5120]{1,0:T(8,128)(2,1)S(1)} %concatenate.10.refs_0_), channel_id=1, source_target_pairs={{0,16},{16,32},{32,48},{48,0},{1,17},{17,33},{33,49},{49,1},{2,18}... | collective-permute-start | bytes 614408 | tf_op jit(solution)/shard_map/ppermute | solution.py:26
  38.5 25.4 %collective-permute-start.12 = (bf16[80,5120]{1,0:T(8,128)(2,1)}, bf16[80,5120]{1,0:T(8,128)(2,1)}, u32[]{:S(2)}, u32[]{:S(2)}) collective-permute-start(bf16[80,5120]{1,0:T(8,128)(2,1)} %in_order.1.refs_9_), channel_id=1, source_target_pairs={{0,2},{2,64},{64,66},{66,128},{128,130},{130,192},{192,194},{194,0... | collective-permute-start | bytes 2457608 | tf_op jit(solution)/shard_map/ppermute | solution.py:26
  40.3 23.7 %collective-permute-start.13 = (bf16[80,5120]{1,0:T(8,128)(2,1)}, bf16[80,5120]{1,0:T(8,128)(2,1)}, u32[]{:S(2)}, u32[]{:S(2)}) collective-permute-start(bf16[80,5120]{1,0:T(8,128)(2,1)} %in_order.1.refs_9_), channel_id=1, source_target_pairs={{0,194},{2,0},{64,2},{66,64},{128,66},{130,128},{192,130},{194,192... | collective-permute-start | bytes 2457608 | tf_op jit(solution)/shard_map/ppermute | solution.py:26
  43.1 12.1 %collective-permute-start.9 = (bf16[8,24,960]{2,1,0:T(8,128)(2,1)S(1)}, bf16[8,24,960]{2,1,0:T(8,128)(2,1)S(1)}, u32[]{:S(2)}, u32[]{:S(2)}) collective-permute-start(bf16[8,24,960]{2,1,0:T(8,128)(2,1)S(1)} %all-to-all-done.refs_4_), channel_id=1, source_target_pairs={{0,48},{16,0},{32,16},{48,32},{1,49},{17,1},{33,17},{49,33},{2,50}... | collective-permute-start | bytes 1105928 | tf_op jit(solution)/shard_map/ppermute | solution.py:26
  43.7 13.6 %collective-permute-start.10 = (bf16[8,24,960]{2,1,0:T(8,128)(2,1)S(1)}, bf16[8,24,960]{2,1,0:T(8,128)(2,1)S(1)}, u32[]{:S(2)}, u32[]{:S(2)}) collective-permute-start(bf16[8,24,960]{2,1,0:T(8,128)(2,1)S(1)} %all-to-all-done.refs_4_), channel_id=1, source_target_pairs={{0,32},{16,48},{32,0},{48,16},{1,33},{17,49},{33,1},{49,17},{2,34}... | collective-permute-start | bytes 1105928 | tf_op jit(solution)/shard_map/ppermute | solution.py:26
  46.6 15.9 %collective-permute-start.11 = (bf16[8,24,960]{2,1,0:T(8,128)(2,1)S(1)}, bf16[8,24,960]{2,1,0:T(8,128)(2,1)S(1)}, u32[]{:S(2)}, u32[]{:S(2)}) collective-permute-start(bf16[8,24,960]{2,1,0:T(8,128)(2,1)S(1)} %all-to-all-done.refs_4_), channel_id=1, source_target_pairs={{0,16},{16,32},{32,48},{48,0},{1,17},{17,33},{33,49},{49,1},{2,18}... | collective-permute-start | bytes 1105928 | tf_op jit(solution)/shard_map/ppermute | solution.py:26
  64.2 22.6 %collective-permute-start.19 = (bf16[80,5120]{1,0:T(8,128)(2,1)}, bf16[80,5120]{1,0:T(8,128)(2,1)}, u32[]{:S(2)}, u32[]{:S(2)}) collective-permute-start(bf16[80,5120]{1,0:T(8,128)(2,1)} %collective-permute-done.12.refs_10_), channel_id=1, source_target_pairs={{0,2},{2,64},{64,66},{66,128},{128,130},{130,192},{192,194},{194,0... | collective-permute-start | bytes 2457608 | tf_op jit(solution)/shard_map/ppermute | solution.py:26
  64.5 22.3 %collective-permute-start.20 = (bf16[80,5120]{1,0:T(8,128)(2,1)}, bf16[80,5120]{1,0:T(8,128)(2,1)}, u32[]{:S(2)}, u32[]{:S(2)}) collective-permute-start(bf16[80,5120]{1,0:T(8,128)(2,1)} %collective-permute-done.13.refs_11_), channel_id=1, source_target_pairs={{0,194},{2,0},{64,2},{66,64},{128,66},{130,128},{192,130},{194,192... | collective-permute-start | bytes 2457608 | tf_op jit(solution)/shard_map/ppermute | solution.py:26
  79.5 7.3 %collective-permute-start.15 = (bf16[640,512]{1,0:T(8,128)(2,1)S(1)}, bf16[640,512]{1,0:T(8,128)(2,1)S(1)}, u32[]{:S(2)}, u32[]{:S(2)}) collective-permute-start(bf16[640,512]{1,0:T(8,128)(2,1)S(1)} %slice.52), channel_id=1, source_target_pairs={{0,1},{1,2},{2,3},{4,5},{5,6},{6,7},{8,9},{9,10},{10,11},{12,13},{... | collective-permute-start | bytes 1966088 | tf_op jit(solution)/shard_map/ppermute | solution.py:442
  86.8 30.5 %collective-permute-start.21 = (bf16[80,5120]{1,0:T(8,128)(2,1)}, bf16[80,5120]{1,0:T(8,128)(2,1)S(1)}, u32[]{:S(2)}, u32[]{:S(2)}) collective-permute-start(bf16[80,5120]{1,0:T(8,128)(2,1)} %collective-permute-done.19.refs_12_), channel_id=1, source_target_pairs={{0,2},{2,64},{64,66},{66,128},{128,130},{130,192},{192,194},{194,0... | collective-permute-start | bytes 2457608 | tf_op jit(solution)/shard_map/ppermute | solution.py:26
  92.5 24.9 %collective-permute-start.22 = (bf16[80,5120]{1,0:T(8,128)(2,1)}, bf16[80,5120]{1,0:T(8,128)(2,1)S(1)}, u32[]{:S(2)}, u32[]{:S(2)}) collective-permute-start(bf16[80,5120]{1,0:T(8,128)(2,1)} %collective-permute-done.20.refs_13_), channel_id=1, source_target_pairs={{0,194},{2,0},{64,2},{66,64},{128,66},{130,128},{192,130},{194,192... | collective-permute-start | bytes 2457608 | tf_op jit(solution)/shard_map/ppermute | solution.py:26
  101.3 12.6 %collective-permute-start.16 = (bf16[320,768]{1,0:T(8,128)(2,1)}, bf16[320,768]{1,0:T(8,128)(2,1)}, u32[]{:S(2)}, u32[]{:S(2)}) collective-permute-start(bf16[320,768]{1,0:T(8,128)(2,1)} %attention.1.refs_0_), channel_id=1, source_target_pairs={{0,12},{4,0},{8,4},{12,8},{1,13},{5,1},{9,5},{13,9},{2,14},{6,2},{... | collective-permute-start | bytes 1474568 | tf_op jit(solution)/shard_map/ppermute | solution.py:26
  104.0 13.4 %collective-permute-start.18 = (bf16[320,768]{1,0:T(8,128)(2,1)}, bf16[320,768]{1,0:T(8,128)(2,1)}, u32[]{:S(2)}, u32[]{:S(2)}) collective-permute-start(bf16[320,768]{1,0:T(8,128)(2,1)} %attention.1.refs_0_), channel_id=1, source_target_pairs={{0,4},{4,8},{8,12},{12,0},{1,5},{5,9},{9,13},{13,1},{2,6},{6,10},{... | collective-permute-start | bytes 1474568 | tf_op jit(solution)/shard_map/ppermute | solution.py:26
  104.0 14.6 %collective-permute-start.24 = (bf16[80,5120]{1,0:T(8,128)(2,1)S(1)}, bf16[80,5120]{1,0:T(8,128)(2,1)S(1)}, u32[]{:S(2)}, u32[]{:S(2)}) collective-permute-start(bf16[80,5120]{1,0:T(8,128)(2,1)S(1)} %copy-done.13), channel_id=1, source_target_pairs={{0,1},{1,0},{2,3},{3,2},{4,5},{5,4},{6,7},{7,6},{8,9},{9,8},{10,11... | collective-permute-start | bytes 2457608 | tf_op jit(solution)/shard_map/ppermute | solution.py:30
  114.0 4.9 %collective-permute-start.25 = (bf16[80,5120]{1,0:T(8,128)(2,1)}, bf16[80,5120]{1,0:T(8,128)(2,1)S(1)}, u32[]{:S(2)}, u32[]{:S(2)}) collective-permute-start(bf16[80,5120]{1,0:T(8,128)(2,1)} %collective-permute-done.12.refs_10_), channel_id=1, source_target_pairs={{0,1},{1,0},{2,3},{3,2},{4,5},{5,4},{6,7},{7,6},{8,9},{9,8},{10,11... | collective-permute-start | bytes 2457608 | tf_op jit(solution)/shard_map/ppermute | solution.py:30
  117.4 22.3 %collective-permute-start.23 = (bf16[80,5120]{1,0:T(8,128)(2,1)S(1)}, bf16[80,5120]{1,0:T(8,128)(2,1)}, u32[]{:S(2)}, u32[]{:S(2)}) collective-permute-start(bf16[80,5120]{1,0:T(8,128)(2,1)S(1)} %collective-permute-done.21.refs_14_), channel_id=1, source_target_pairs={{0,2},{2,64},{64,66},{66,128},{128,130},{130,192},{192,194},{194,0... | collective-permute-start | bytes 2457608 | tf_op jit(solution)/shard_map/ppermute | solution.py:26
  118.6 15.1 %collective-permute-start.17 = (bf16[320,768]{1,0:T(8,128)(2,1)}, bf16[320,768]{1,0:T(8,128)(2,1)S(1)}, u32[]{:S(2)}, u32[]{:S(2)}) collective-permute-start(bf16[320,768]{1,0:T(8,128)(2,1)} %attention.1.refs_0_), channel_id=1, source_target_pairs={{0,8},{4,12},{8,0},{12,4},{1,9},{5,13},{9,1},{13,5},{2,10},{6,14},... | collective-permute-start | bytes 1474568 | tf_op jit(solution)/shard_map/ppermute | solution.py:26
  118.6 23.5 %collective-permute-start.27 = (bf16[80,5120]{1,0:T(8,128)(2,1)}, bf16[80,5120]{1,0:T(8,128)(2,1)S(1)}, u32[]{:S(2)}, u32[]{:S(2)}) collective-permute-start(bf16[80,5120]{1,0:T(8,128)(2,1)} %collective-permute-done.19.refs_12_), channel_id=1, source_target_pairs={{0,1},{1,0},{2,3},{3,2},{4,5},{5,4},{6,7},{7,6},{8,9},{9,8},{10,11... | collective-permute-start | bytes 2457608 | tf_op jit(solution)/shard_map/ppermute | solution.py:30
  118.9 23.2 %collective-permute-start.28 = (bf16[80,5120]{1,0:T(8,128)(2,1)}, bf16[80,5120]{1,0:T(8,128)(2,1)}, u32[]{:S(2)}, u32[]{:S(2)}) collective-permute-start(bf16[80,5120]{1,0:T(8,128)(2,1)} %collective-permute-done.20.refs_13_), channel_id=1, source_target_pairs={{0,1},{1,0},{2,3},{3,2},{4,5},{5,4},{6,7},{7,6},{8,9},{9,8},{10,11... | collective-permute-start | bytes 2457608 | tf_op jit(solution)/shard_map/ppermute | solution.py:30
  119.9 22.2 %collective-permute-start.29 = (bf16[80,5120]{1,0:T(8,128)(2,1)S(1)}, bf16[80,5120]{1,0:T(8,128)(2,1)}, u32[]{:S(2)}, u32[]{:S(2)}) collective-permute-start(bf16[80,5120]{1,0:T(8,128)(2,1)S(1)} %collective-permute-done.21.refs_14_), channel_id=1, source_target_pairs={{0,1},{1,0},{2,3},{3,2},{4,5},{5,4},{6,7},{7,6},{8,9},{9,8},{10,11... | collective-permute-start | bytes 2457608 | tf_op jit(solution)/shard_map/ppermute | solution.py:30
  133.6 8.5 %collective-permute-start.30 = (bf16[80,5120]{1,0:T(8,128)(2,1)S(1)}, bf16[80,5120]{1,0:T(8,128)(2,1)}, u32[]{:S(2)}, u32[]{:S(2)}) collective-permute-start(bf16[80,5120]{1,0:T(8,128)(2,1)S(1)} %collective-permute-done.22.refs_15_), channel_id=1, source_target_pairs={{0,1},{1,0},{2,3},{3,2},{4,5},{5,4},{6,7},{7,6},{8,9},{9,8},{10,11... | collective-permute-start | bytes 2457608 | tf_op jit(solution)/shard_map/ppermute | solution.py:30
  165.3 29.5 %all-to-all-start.1 = ((bf16[4,320,768]{2,1,0:T(8,128)(2,1)}), bf16[4,320,768]{2,1,0:T(8,128)(2,1)S(1)}, u32[]{:S(2)}, u32[]{:S(2)}) async-start(bf16[4,320,768]{2,1,0:T(8,128)(2,1)} %get-tuple-element.36), calls=%async_computation.1 | async-start | bytes 3932160 | tf_op jit(solution)/shard_map/all_to_all | solution.py:452
  197.0 5.2 %collective-permute-start.33 = (f32[4,768]{1,0:T(4,128)S(1)}, f32[4,768]{1,0:T(4,128)S(1)}, u32[]{:S(2)}, u32[]{:S(2)}) collective-permute-start(f32[4,768]{1,0:T(4,128)S(1)} %pad_maximum_fusion.1), channel_id=1, source_target_pairs={{0,8},{4,12},{8,0},{12,4},{1,9},{5,13},{9,1},{13,5},{2,10},{6,14},... | collective-permute-start | bytes 36872 | tf_op jit(solution)/shard_map/ppermute | solution.py:26
  (39 other events, 447.0 us)

commit v5 on v4

--- a/solution.py
+++ b/solution.py
@@ -436,16 +436,18 @@
     (qkv_z,) = after([qkv_z], rest_y, cosine, sine, key_start, gain, attn_step, step_block, *blocks)
     qkv_near = four_blocks(qkv_z, "y")
     ahead, behind = shift(rest_y, Z, 8, 1), shift(rest_y, Z, 8, -1)
-    (qkv_stack,) = after([jnp.stack(qkv_near)], ahead, behind)
+    early = [swap_core(block) for block in (rest_y, ahead, behind)]
+    (qkv_stack,) = after([jnp.stack(qkv_near)], ahead, behind, early[0])
     qkv_far = swap_core(qkv_stack)
     query, own, features, size = project(spot, blocks, qkv_near, qkv_far, gain, cosine, sine)
     before = lax.ppermute(own[:, rows - window :], ("zl", "co"), [(i, i + 1) for i in range(3)])
     recent = attention_recent(key_start, query, own)
-    (before,) = after([before], recent)
+    (before,) = after([before], recent, *early)
     attended = attention(key_start, query, before, own, recent)
     everyone = four_blocks(attended, "tp")
-    near = ring_z(rest_y, ahead, behind, {2: (before, recent), 3: (everyone[1], everyone[3])})
-    far = [swap_core(block) for block in near]
+    near = ring_z(rest_y, ahead, behind, {2: (recent,), 3: (everyone[1], everyone[3])})
+    (near[7],) = after([near[7]], everyone[2])
+    far = early + [swap_core(block) for block in near[3:]]
     parts, mixed = layer(
         spot, everyone, features, size, attn_step, up_scale[None], gate_scale[None], near, far
     )

time: 207 us -> 212 us (1.024)
  starting transfers between devices: 52.6 us -> 65.1 us
  waiting for transfers between devices: 86.7 us -> 79.4 us
    ppermute x25, starting transfers between devices: 37.5 us -> 48.7 us  [shift(): return lax.ppermute(block, axis, ring(count, step))]
    ppermute x25, waiting for transfers between devices: 59.8 us -> 53.9 us  [shift(): return lax.ppermute(block, axis, ring(count, step))]
    unnamed x70 -> x66, local copies, waits for them, and re-layouts: 8.06 us -> 7.51 us
  transfers between devices with their start and end apart: 37 -> 37, of which waited for: 16 -> 15; matrix products, arithmetic and copies ran while one was open for 5% -> 5% of each run, Pallas kernels for 10% -> 10%
where the time goes in v5:
time: 212 us; the launch traced here: 209 us
  waiting for transfers between devices  79.4 us (37%)
  starting transfers between devices  65.1 us (31%)
  Pallas kernels  43.4 us (20%)
  local copies, waits for them, and re-layouts  15.2 us (7%)
  other arithmetic  5.68 us (3%)
    ppermute x25, waiting for transfers between devices, shift(): return lax.ppermute(block, axis, ring(count, step))  53.9 us
    ppermute x25, starting transfers between devices, shift(): return lax.ppermute(block, axis, ring(count, step))  48.7 us
    all_to_all x1, waiting for transfers between devices, body(): landed = lax.all_to_all(parts, 'tp', 0, 0, tiled=True).astype(F32)  25.4 us
    pallas_call x1, Pallas kernels, layer(): pl.pallas_call(layer_kernel, out_shape=[jax.ShapeDtypeStruct((4, local, r...  22.3 us
    all_to_all x1, starting transfers between devices, body(): qkv_z = lax.all_to_all(everywhere, Z, 0, 0, tiled=True)  8.47 us
    pallas_call x1, Pallas kernels, attention(): pl.pallas_call(attention_kernel, out_shape=jax.ShapeDtypeStruct(query.sha...  7.53 us
    unnamed x66, local copies, waits for them, and re-layouts  7.51 us
    pallas_call x1, Pallas kernels, project(): pl.pallas_call(project_kernel, out_shape=[jax.ShapeDtypeStruct((local, ro...  5.84 us
  transfers between devices with their start and end apart: 37, of which 15 were waited for; matrix products, arithmetic and copies ran while one was open for 5% of the time, Pallas kernels for 10%

profile of v5, /device:TPU:16, one launch (start us, length us, event | category | flops | bytes accessed | tf_op | source)
XLA Modules:
  0.0 209.4 jit_solution(9456655973789762020)
XLA Ops:
  0.8 2.8 %collective-permute-start.3 = (bf16[20,320]{1,0:T(8,128)(2,1)S(1)}, bf16[20,320]{1,0:T(8,128)(2,1)S(1)}, u32[]{:S(2)}, u32[]{:S(2)}) collective-permute-start(bf16[20,320]{1,0:T(8,128)(2,1)S(1)} %convert_bitcast_fusion.1), channel_id=1, source_target_pairs={{0,12},{4,0},{8,4},{12,8},{1,13},{5,1},{9,5},{13,9},{2,14},{6,2},{... | collective-permute-start | bytes 38408 | tf_op jit(solution)/shard_map/ppermute | solution.py:26
  6.6 2.4 %collective-permute-start = (bf16[320,768]{1,0:T(8,128)(2,1)S(1)}, bf16[320,768]{1,0:T(8,128)(2,1)S(1)}, u32[]{:S(2)}, u32[]{:S(2)}) collective-permute-start(bf16[320,768]{1,0:T(8,128)(2,1)S(1)} %reshape.58.refs_0_), channel_id=1, source_target_pairs={{0,12},{4,0},{8,4},{12,8},{1,13},{5,1},{9,5},{13,9},{2,14},{6,2},{... | collective-permute-start | bytes 1474568 | tf_op jit(solution)/shard_map/ppermute | solution.py:26
  9.0 1.5 collective-permute-start.1
  13.7 8.5 %all-to-all-start = ((bf16[8,24,960]{2,1,0:T(8,128)(2,1)}), bf16[8,24,960]{2,1,0:T(8,128)(2,1)S(1)}, u32[]{:S(2)}, u32[]{:S(2)}) async-start(bf16[8,24,960]{2,1,0:T(8,128)(2,1)} %broadcast_in_dim.31), calls=%async_computation | async-start | bytes 786432 | tf_op jit(solution)/shard_map/all_to_all | solution.py:433
  24.3 2.9 %collective-permute-start.7 = (bf16[20,5120]{1,0:T(8,128)(2,1)S(1)}, bf16[20,5120]{1,0:T(8,128)(2,1)S(1)}, u32[]{:S(2)}, u32[]{:S(2)}) collective-permute-start(bf16[20,5120]{1,0:T(8,128)(2,1)S(1)} %concatenate.10.refs_0_), channel_id=1, source_target_pairs={{0,32},{16,48},{32,0},{48,16},{1,33},{17,49},{33,1},{49,17},{2,34}... | collective-permute-start | bytes 614408 | tf_op jit(solution)/shard_map/ppermute | solution.py:26
  27.2 4.7 %collective-permute-done.6.refs_1_ = bf16[20,5120]{1,0:T(8,128)(2,1)S(1)} collective-permute-done((bf16[20,5120]{1,0:T(8,128)(2,1)S(1)}, bf16[20,5120]{1,0:T(8,128)(2,1)S(1)}, u32[]{:S(2)}, u32[]{:S(2)}) %collective-permute-start.6) | collective-permute-done | bytes 204832 | tf_op jit(solution)/shard_map/ppermute | solution.py:26
  32.0 5.1 %collective-permute-start.8 = (bf16[20,5120]{1,0:T(8,128)(2,1)S(1)}, bf16[20,5120]{1,0:T(8,128)(2,1)S(1)}, u32[]{:S(2)}, u32[]{:S(2)}) collective-permute-start(bf16[20,5120]{1,0:T(8,128)(2,1)S(1)} %concatenate.10.refs_0_), channel_id=1, source_target_pairs={{0,16},{16,32},{32,48},{48,0},{1,17},{17,33},{33,49},{49,1},{2,18}... | collective-permute-start | bytes 614408 | tf_op jit(solution)/shard_map/ppermute | solution.py:26
  37.5 3.3 %collective-permute-done.8.refs_3_ = bf16[20,5120]{1,0:T(8,128)(2,1)S(1)} collective-permute-done((bf16[20,5120]{1,0:T(8,128)(2,1)S(1)}, bf16[20,5120]{1,0:T(8,128)(2,1)S(1)}, u32[]{:S(2)}, u32[]{:S(2)}) %collective-permute-start.8) | collective-permute-done | bytes 204832 | tf_op jit(solution)/shard_map/ppermute | solution.py:26
  41.5 2.5 %in_order.1.refs_9_ = bf16[80,5120]{1,0:T(8,128)(2,1)} custom-call(s32[4]{0:T(128)} %pad_add_fusion.place_ref, bf16[20,5120]{1,0:T(8,128)(2,1)} %copy-done.12, bf16[20,5120]{1,0:T(8,128)(2,1)} %copy-done.13, bf16[20,5120]{1,0:T(8,128)(2,1)} %copy-done.14, bf16[20,5120]{1,0:T(8,128)(2,1)} %copy-done.15), custom_call_target="tpu_custom_call" | custom-call | bytes 1638400 | tf_op jit(solution)/shard_map/in_order/pallas_call | solution.py:62
  44.9 1.7 collective-permute-start.12
  46.6 1.5 collective-permute-start.13
  48.1 4.5 %collective-permute-start.10 = (bf16[8,24,960]{2,1,0:T(8,128)(2,1)S(1)}, bf16[8,24,960]{2,1,0:T(8,128)(2,1)S(1)}, u32[]{:S(2)}, u32[]{:S(2)}) collective-permute-start(bf16[8,24,960]{2,1,0:T(8,128)(2,1)S(1)} %all-to-all-done.refs_4_), channel_id=1, source_target_pairs={{0,32},{16,48},{32,0},{48,16},{1,33},{17,49},{33,1},{49,17},{2,34}... | collective-permute-start | bytes 1105928 | tf_op jit(solution)/shard_map/ppermute | solution.py:26
  53.1 11.7 %collective-permute-start.11 = (bf16[8,24,960]{2,1,0:T(8,128)(2,1)S(1)}, bf16[8,24,960]{2,1,0:T(8,128)(2,1)S(1)}, u32[]{:S(2)}, u32[]{:S(2)}) collective-permute-start(bf16[8,24,960]{2,1,0:T(8,128)(2,1)S(1)} %all-to-all-done.refs_4_), channel_id=1, source_target_pairs={{0,16},{16,32},{32,48},{48,0},{1,17},{17,33},{33,49},{49,1},{2,18}... | collective-permute-start | bytes 1105928 | tf_op jit(solution)/shard_map/ppermute | solution.py:26
  64.8 6.1 %collective-permute-done.11.refs_7_ = bf16[8,24,960]{2,1,0:T(8,128)(2,1)S(1)} collective-permute-done((bf16[8,24,960]{2,1,0:T(8,128)(2,1)S(1)}, bf16[8,24,960]{2,1,0:T(8,128)(2,1)S(1)}, u32[]{:S(2)}, u32[]{:S(2)}) %collective-permute-start.11) | collective-permute-done | bytes 368672 | tf_op jit(solution)/shard_map/ppermute | solution.py:26
  70.9 1.4 pad_maximum_fusion
  73.4 2.3 %collective-permute-start.23 = (bf16[80,5120]{1,0:T(8,128)(2,1)}, bf16[80,5120]{1,0:T(8,128)(2,1)}, u32[]{:S(2)}, u32[]{:S(2)}) collective-permute-start(bf16[80,5120]{1,0:T(8,128)(2,1)} %collective-permute-done.13.refs_11_), channel_id=1, source_target_pairs={{0,194},{2,0},{64,2},{66,64},{128,66},{130,128},{192,130},{194,192... | collective-permute-start | bytes 2457608 | tf_op jit(solution)/shard_map/ppermute | solution.py:26
  79.5 5.8 %project.1 = (bf16[320,768]{1,0:T(8,128)(2,1)S(1)}, bf16[640,768]{1,0:T(8,128)(2,1)S(1)}, bf16[1280,768]{1,0:T(8,128)(2,1)S(1)}, f32[1,768]{1,0:T(1,128)S(1)}) custom-call(s32[4]{0:T(128)S(1)} %copy-done.1, bf16[320,768]{1,0:T(8,128)(2,1)S(1)} %reshape.58.refs_0_, bf16[320,768]{1,0:T(8,128)(2,1)S(1)} %copy-done.3, bf16[320,768]{1,0:T(8,128)(2,1)S(1)} %copy-done.5, ...), custom_call_target="tpu_custom_call" | custom-call | flops 1900000000 | bytes 12000000 | tf_op jit(solution)/shard_map/project/pallas_call | solution.py:235
  88.1 2.9 %collective-permute-start.16 = (bf16[640,512]{1,0:T(8,128)(2,1)S(1)}, bf16[640,512]{1,0:T(8,128)(2,1)}, u32[]{:S(2)}, u32[]{:S(2)}) collective-permute-start(bf16[640,512]{1,0:T(8,128)(2,1)S(1)} %slice.52), channel_id=1, source_target_pairs={{0,1},{1,2},{2,3},{4,5},{5,6},{6,7},{8,9},{9,10},{10,11},{12,13},{... | collective-permute-start | bytes 1966088 | tf_op jit(solution)/shard_map/ppermute | solution.py:443
  91.0 5.2 %attention_recent.1.recent_ref = bf16[320,256]{1,0:T(8,128)(2,1)} custom-call(s32[1,768]{1,0:T(1,128)} %broadcast_in_dim.30.start_ref, bf16[320,768]{1,0:T(8,128)(2,1)} %copy-done.8, bf16[640,768]{1,0:T(8,128)(2,1)} %copy-done), custom_call_target="tpu_custom_call" | custom-call | flops 260000000 | bytes 2000000 | tf_op jit(solution)/shard_map/attention_recent/pallas_call | solution.py:155
  96.3 3.2 %collective-permute-start.25 = (bf16[80,5120]{1,0:T(8,128)(2,1)}, bf16[80,5120]{1,0:T(8,128)(2,1)S(1)}, u32[]{:S(2)}, u32[]{:S(2)}) collective-permute-start(bf16[80,5120]{1,0:T(8,128)(2,1)} %collective-permute-done.23.refs_13_), channel_id=1, source_target_pairs={{0,194},{2,0},{64,2},{66,64},{128,66},{130,128},{192,130},{194,192... | collective-permute-start | bytes 2457608 | tf_op jit(solution)/shard_map/ppermute | solution.py:26
  99.6 7.5 %attention.1.refs_0_ = bf16[320,768]{1,0:T(8,128)(2,1)} custom-call(s32[1,768]{1,0:T(1,128)} %broadcast_in_dim.30.start_ref, bf16[320,768]{1,0:T(8,128)(2,1)} %copy-done.8, bf16[640,512]{1,0:T(8,128)(2,1)} %collective-permute-done.16.before_ref, bf16[640,768]{1,0:T(8,128)(2,1)} %copy-done, bf16[320,256]{1,0:T(8,128)(2,1)} %attention_recent.1.recent_ref), custom_call_target="tpu_custom_call" | custom-call | flops 520000000 | bytes 4000000 | tf_op jit(solution)/shard_map/attention/pallas_call | solution.py:166
  107.1 2.9 %collective-permute-start.19 = (bf16[320,768]{1,0:T(8,128)(2,1)}, bf16[320,768]{1,0:T(8,128)(2,1)S(1)}, u32[]{:S(2)}, u32[]{:S(2)}) collective-permute-start(bf16[320,768]{1,0:T(8,128)(2,1)} %attention.1.refs_0_), channel_id=1, source_target_pairs={{0,12},{4,0},{8,4},{12,8},{1,13},{5,1},{9,5},{13,9},{2,14},{6,2},{... | collective-permute-start | bytes 1474568 | tf_op jit(solution)/shard_map/ppermute | solution.py:26
  110.0 7.7 %collective-permute-done.24.refs_14_ = bf16[80,5120]{1,0:T(8,128)(2,1)S(1)} collective-permute-done((bf16[80,5120]{1,0:T(8,128)(2,1)}, bf16[80,5120]{1,0:T(8,128)(2,1)S(1)}, u32[]{:S(2)}, u32[]{:S(2)}) %collective-permute-start.24) | collective-permute-done | bytes 819232 | tf_op jit(solution)/shard_map/ppermute | solution.py:26
  118.0 3.3 %collective-permute-done.19.refs_1_ = bf16[320,768]{1,0:T(8,128)(2,1)S(1)} collective-permute-done((bf16[320,768]{1,0:T(8,128)(2,1)}, bf16[320,768]{1,0:T(8,128)(2,1)S(1)}, u32[]{:S(2)}, u32[]{:S(2)}) %collective-permute-start.19) | collective-permute-done | bytes 491552 | tf_op jit(solution)/shard_map/ppermute | solution.py:26
  121.3 3.3 %collective-permute-done.21.refs_3_ = bf16[320,768]{1,0:T(8,128)(2,1)S(1)} collective-permute-done((bf16[320,768]{1,0:T(8,128)(2,1)}, bf16[320,768]{1,0:T(8,128)(2,1)S(1)}, u32[]{:S(2)}, u32[]{:S(2)}) %collective-permute-start.21) | collective-permute-done | bytes 491552 | tf_op jit(solution)/shard_map/ppermute | solution.py:26
  125.3 13.3 %collective-permute-done.20.refs_2_ = bf16[320,768]{1,0:T(8,128)(2,1)S(1)} collective-permute-done((bf16[320,768]{1,0:T(8,128)(2,1)}, bf16[320,768]{1,0:T(8,128)(2,1)S(1)}, u32[]{:S(2)}, u32[]{:S(2)}) %collective-permute-start.20) | collective-permute-done | bytes 491552 | tf_op jit(solution)/shard_map/ppermute | solution.py:26
  138.6 6.5 %collective-permute-done.26.refs_16_ = bf16[80,5120]{1,0:T(8,128)(2,1)S(1)} collective-permute-done((bf16[80,5120]{1,0:T(8,128)(2,1)S(1)}, bf16[80,5120]{1,0:T(8,128)(2,1)S(1)}, u32[]{:S(2)}, u32[]{:S(2)}) %collective-permute-start.26) | collective-permute-done | bytes 819232 | tf_op jit(solution)/shard_map/ppermute | solution.py:26
  147.7 22.3 %layer.1 = (bf16[4,320,768]{2,1,0:T(8,128)(2,1)}, f32[320,768]{1,0:T(8,128)}) custom-call(s32[4]{0:T(128)} %pad_add_fusion.place_ref, bf16[320,768]{1,0:T(8,128)(2,1)} %attention.1.refs_0_, bf16[320,768]{1,0:T(8,128)(2,1)} %copy-done.29, bf16[320,768]{1,0:T(8,128)(2,1)} %copy-done.31, bf16[320,768]{1,0:T(8,128)(2,1)} %copy-done.30, ...), custom_call_target="tpu_custom_call" | custom-call | flops 10000000000 | bytes 20000000 | tf_op jit(solution)/shard_map/layer/pallas_call | solution.py:355
  170.0 3.6 %all-to-all-start.1 = ((bf16[4,320,768]{2,1,0:T(8,128)(2,1)}), bf16[4,320,768]{2,1,0:T(8,128)(2,1)S(1)}, u32[]{:S(2)}, u32[]{:S(2)}) async-start(bf16[4,320,768]{2,1,0:T(8,128)(2,1)} %get-tuple-element.38), calls=%async_computation.1 | async-start | bytes 3932160 | tf_op jit(solution)/shard_map/all_to_all | solution.py:454
  174.0 25.4 %all-to-all-done.1 = bf16[4,320,768]{2,1,0:T(8,128)(2,1)S(1)} async-done(((bf16[4,320,768]{2,1,0:T(8,128)(2,1)}), bf16[4,320,768]{2,1,0:T(8,128)(2,1)S(1)}, u32[]{:S(2)}, u32[]{:S(2)}) %all-to-all-start.1) | async-done | bytes 1966112 | tf_op jit(solution)/shard_map/all_to_all | solution.py:454
  201.6 1.5 collective-permute-start.33
  204.2 2.7 %collective-permute-done.33 = f32[4,768]{1,0:T(4,128)S(1)} collective-permute-done((f32[4,768]{1,0:T(4,128)S(1)}, f32[4,768]{1,0:T(4,128)S(1)}, u32[]{:S(2)}, u32[]{:S(2)}) %collective-permute-start.33) | collective-permute-done | bytes 12320 | tf_op jit(solution)/shard_map/ppermute | solution.py:26
  (164 shorter events, 28.7 us)
Async XLA Ops:
  0.8 11.8 %collective-permute-start.3 = (bf16[20,320]{1,0:T(8,128)(2,1)S(1)}, bf16[20,320]{1,0:T(8,128)(2,1)S(1)}, u32[]{:S(2)}, u32[]{:S(2)}) collective-permute-start(bf16[20,320]{1,0:T(8,128)(2,1)S(1)} %convert_bitcast_fusion.1), channel_id=1, source_target_pairs={{0,12},{4,0},{8,4},{12,8},{1,13},{5,1},{9,5},{13,9},{2,14},{6,2},{... | collective-permute-start | bytes 38408 | tf_op jit(solution)/shard_map/ppermute | solution.py:26
  3.5 9.1 %collective-permute-start.4 = (bf16[20,320]{1,0:T(8,128)(2,1)S(1)}, bf16[20,320]{1,0:T(8,128)(2,1)S(1)}, u32[]{:S(2)}, u32[]{:S(2)}) collective-permute-start(bf16[20,320]{1,0:T(8,128)(2,1)S(1)} %convert_bitcast_fusion.1), channel_id=1, source_target_pairs={{0,8},{4,12},{8,0},{12,4},{1,9},{5,13},{9,1},{13,5},{2,10},{6,14},... | collective-permute-start | bytes 38408 | tf_op jit(solution)/shard_map/ppermute | solution.py:26
  4.3 8.3 %collective-permute-start.5 = (bf16[20,320]{1,0:T(8,128)(2,1)S(1)}, bf16[20,320]{1,0:T(8,128)(2,1)S(1)}, u32[]{:S(2)}, u32[]{:S(2)}) collective-permute-start(bf16[20,320]{1,0:T(8,128)(2,1)S(1)} %convert_bitcast_fusion.1), channel_id=1, source_target_pairs={{0,4},{4,8},{8,12},{12,0},{1,5},{5,9},{9,13},{13,1},{2,6},{6,10},{... | collective-permute-start | bytes 38408 | tf_op jit(solution)/shard_map/ppermute | solution.py:26
  6.6 37.4 %collective-permute-start = (bf16[320,768]{1,0:T(8,128)(2,1)S(1)}, bf16[320,768]{1,0:T(8,128)(2,1)S(1)}, u32[]{:S(2)}, u32[]{:S(2)}) collective-permute-start(bf16[320,768]{1,0:T(8,128)(2,1)S(1)} %reshape.58.refs_0_), channel_id=1, source_target_pairs={{0,12},{4,0},{8,4},{12,8},{1,13},{5,1},{9,5},{13,9},{2,14},{6,2},{... | collective-permute-start | bytes 1474568 | tf_op jit(solution)/shard_map/ppermute | solution.py:26
  9.0 35.0 %collective-permute-start.1 = (bf16[320,768]{1,0:T(8,128)(2,1)S(1)}, bf16[320,768]{1,0:T(8,128)(2,1)S(1)}, u32[]{:S(2)}, u32[]{:S(2)}) collective-permute-start(bf16[320,768]{1,0:T(8,128)(2,1)S(1)} %reshape.58.refs_0_), channel_id=1, source_target_pairs={{0,8},{4,12},{8,0},{12,4},{1,9},{5,13},{9,1},{13,5},{2,10},{6,14},... | collective-permute-start | bytes 1474568 | tf_op jit(solution)/shard_map/ppermute | solution.py:26
  12.6 31.5 %collective-permute-start.2 = (bf16[320,768]{1,0:T(8,128)(2,1)S(1)}, bf16[320,768]{1,0:T(8,128)(2,1)S(1)}, u32[]{:S(2)}, u32[]{:S(2)}) collective-permute-start(bf16[320,768]{1,0:T(8,128)(2,1)S(1)} %reshape.58.refs_0_), channel_id=1, source_target_pairs={{0,4},{4,8},{8,12},{12,0},{1,5},{5,9},{9,13},{13,1},{2,6},{6,10},{... | collective-permute-start | bytes 1474568 | tf_op jit(solution)/shard_map/ppermute | solution.py:26
  13.7 31.1 %all-to-all-start = ((bf16[8,24,960]{2,1,0:T(8,128)(2,1)}), bf16[8,24,960]{2,1,0:T(8,128)(2,1)S(1)}, u32[]{:S(2)}, u32[]{:S(2)}) async-start(bf16[8,24,960]{2,1,0:T(8,128)(2,1)} %broadcast_in_dim.31), calls=%async_computation | async-start | bytes 786432 | tf_op jit(solution)/shard_map/all_to_all | solution.py:433
  23.2 8.7 %collective-permute-start.6 = (bf16[20,5120]{1,0:T(8,128)(2,1)S(1)}, bf16[20,5120]{1,0:T(8,128)(2,1)S(1)}, u32[]{:S(2)}, u32[]{:S(2)}) collective-permute-start(bf16[20,5120]{1,0:T(8,128)(2,1)S(1)} %concatenate.10.refs_0_), channel_id=1, source_target_pairs={{0,48},{16,0},{32,16},{48,32},{1,49},{17,1},{33,17},{49,33},{2,50}... | collective-permute-start | bytes 614408 | tf_op jit(solution)/shard_map/ppermute | solution.py:26
  24.3 13.2 %collective-permute-start.7 = (bf16[20,5120]{1,0:T(8,128)(2,1)S(1)}, bf16[20,5120]{1,0:T(8,128)(2,1)S(1)}, u32[]{:S(2)}, u32[]{:S(2)}) collective-permute-start(bf16[20,5120]{1,0:T(8,128)(2,1)S(1)} %concatenate.10.refs_0_), channel_id=1, source_target_pairs={{0,32},{16,48},{32,0},{48,16},{1,33},{17,49},{33,1},{49,17},{2,34}... | collective-permute-start | bytes 614408 | tf_op jit(solution)/shard_map/ppermute | solution.py:26
  32.0 8.8 %collective-permute-start.8 = (bf16[20,5120]{1,0:T(8,128)(2,1)S(1)}, bf16[20,5120]{1,0:T(8,128)(2,1)S(1)}, u32[]{:S(2)}, u32[]{:S(2)}) collective-permute-start(bf16[20,5120]{1,0:T(8,128)(2,1)S(1)} %concatenate.10.refs_0_), channel_id=1, source_target_pairs={{0,16},{16,32},{32,48},{48,0},{1,17},{17,33},{33,49},{49,1},{2,18}... | collective-permute-start | bytes 614408 | tf_op jit(solution)/shard_map/ppermute | solution.py:26
  44.9 8.2 %collective-permute-start.9 = (bf16[8,24,960]{2,1,0:T(8,128)(2,1)S(1)}, bf16[8,24,960]{2,1,0:T(8,128)(2,1)S(1)}, u32[]{:S(2)}, u32[]{:S(2)}) collective-permute-start(bf16[8,24,960]{2,1,0:T(8,128)(2,1)S(1)} %all-to-all-done.refs_4_), channel_id=1, source_target_pairs={{0,48},{16,0},{32,16},{48,32},{1,49},{17,1},{33,17},{49,33},{2,50}... | collective-permute-start | bytes 1105928 | tf_op jit(solution)/shard_map/ppermute | solution.py:26
  44.9 27.4 %collective-permute-start.12 = (bf16[80,5120]{1,0:T(8,128)(2,1)}, bf16[80,5120]{1,0:T(8,128)(2,1)}, u32[]{:S(2)}, u32[]{:S(2)}) collective-permute-start(bf16[80,5120]{1,0:T(8,128)(2,1)} %in_order.1.refs_9_), channel_id=1, source_target_pairs={{0,2},{2,64},{64,66},{66,128},{128,130},{130,192},{192,194},{194,0... | collective-permute-start | bytes 2457608 | tf_op jit(solution)/shard_map/ppermute | solution.py:26
  46.6 25.6 %collective-permute-start.13 = (bf16[80,5120]{1,0:T(8,128)(2,1)}, bf16[80,5120]{1,0:T(8,128)(2,1)}, u32[]{:S(2)}, u32[]{:S(2)}) collective-permute-start(bf16[80,5120]{1,0:T(8,128)(2,1)} %in_order.1.refs_9_), channel_id=1, source_target_pairs={{0,194},{2,0},{64,2},{66,64},{128,66},{130,128},{192,130},{194,192... | collective-permute-start | bytes 2457608 | tf_op jit(solution)/shard_map/ppermute | solution.py:26
  48.1 24.1 %collective-permute-start.14 = (bf16[80,5120]{1,0:T(8,128)(2,1)}, bf16[80,5120]{1,0:T(8,128)(2,1)S(1)}, u32[]{:S(2)}, u32[]{:S(2)}) collective-permute-start(bf16[80,5120]{1,0:T(8,128)(2,1)} %in_order.1.refs_9_), channel_id=1, source_target_pairs={{0,1},{1,0},{2,3},{3,2},{4,5},{5,4},{6,7},{7,6},{8,9},{9,8},{10,11... | collective-permute-start | bytes 2457608 | tf_op jit(solution)/shard_map/ppermute | solution.py:30
  48.1 16.7 %collective-permute-start.10 = (bf16[8,24,960]{2,1,0:T(8,128)(2,1)S(1)}, bf16[8,24,960]{2,1,0:T(8,128)(2,1)S(1)}, u32[]{:S(2)}, u32[]{:S(2)}) collective-permute-start(bf16[8,24,960]{2,1,0:T(8,128)(2,1)S(1)} %all-to-all-done.refs_4_), channel_id=1, source_target_pairs={{0,32},{16,48},{32,0},{48,16},{1,33},{17,49},{33,1},{49,17},{2,34}... | collective-permute-start | bytes 1105928 | tf_op jit(solution)/shard_map/ppermute | solution.py:26
  53.1 17.8 %collective-permute-start.11 = (bf16[8,24,960]{2,1,0:T(8,128)(2,1)S(1)}, bf16[8,24,960]{2,1,0:T(8,128)(2,1)S(1)}, u32[]{:S(2)}, u32[]{:S(2)}) collective-permute-start(bf16[8,24,960]{2,1,0:T(8,128)(2,1)S(1)} %all-to-all-done.refs_4_), channel_id=1, source_target_pairs={{0,16},{16,32},{32,48},{48,0},{1,17},{17,33},{33,49},{49,1},{2,18}... | collective-permute-start | bytes 1105928 | tf_op jit(solution)/shard_map/ppermute | solution.py:26
  72.4 23.8 %collective-permute-start.22 = (bf16[80,5120]{1,0:T(8,128)(2,1)}, bf16[80,5120]{1,0:T(8,128)(2,1)}, u32[]{:S(2)}, u32[]{:S(2)}) collective-permute-start(bf16[80,5120]{1,0:T(8,128)(2,1)} %collective-permute-done.12.refs_10_), channel_id=1, source_target_pairs={{0,2},{2,64},{64,66},{66,128},{128,130},{130,192},{192,194},{194,0... | collective-permute-start | bytes 2457608 | tf_op jit(solution)/shard_map/ppermute | solution.py:26
  73.4 22.8 %collective-permute-start.23 = (bf16[80,5120]{1,0:T(8,128)(2,1)}, bf16[80,5120]{1,0:T(8,128)(2,1)}, u32[]{:S(2)}, u32[]{:S(2)}) collective-permute-start(bf16[80,5120]{1,0:T(8,128)(2,1)} %collective-permute-done.13.refs_11_), channel_id=1, source_target_pairs={{0,194},{2,0},{64,2},{66,64},{128,66},{130,128},{192,130},{194,192... | collective-permute-start | bytes 2457608 | tf_op jit(solution)/shard_map/ppermute | solution.py:26
  75.9 23.7 %collective-permute-start.17 = (bf16[80,5120]{1,0:T(8,128)(2,1)}, bf16[80,5120]{1,0:T(8,128)(2,1)}, u32[]{:S(2)}, u32[]{:S(2)}) collective-permute-start(bf16[80,5120]{1,0:T(8,128)(2,1)} %collective-permute-done.12.refs_10_), channel_id=1, source_target_pairs={{0,1},{1,0},{2,3},{3,2},{4,5},{5,4},{6,7},{7,6},{8,9},{9,8},{10,11... | collective-permute-start | bytes 2457608 | tf_op jit(solution)/shard_map/ppermute | solution.py:30
  76.0 23.6 %collective-permute-start.18 = (bf16[80,5120]{1,0:T(8,128)(2,1)}, bf16[80,5120]{1,0:T(8,128)(2,1)}, u32[]{:S(2)}, u32[]{:S(2)}) collective-permute-start(bf16[80,5120]{1,0:T(8,128)(2,1)} %collective-permute-done.13.refs_11_), channel_id=1, source_target_pairs={{0,1},{1,0},{2,3},{3,2},{4,5},{5,4},{6,7},{7,6},{8,9},{9,8},{10,11... | collective-permute-start | bytes 2457608 | tf_op jit(solution)/shard_map/ppermute | solution.py:30
  88.1 11.4 %collective-permute-start.16 = (bf16[640,512]{1,0:T(8,128)(2,1)S(1)}, bf16[640,512]{1,0:T(8,128)(2,1)}, u32[]{:S(2)}, u32[]{:S(2)}) collective-permute-start(bf16[640,512]{1,0:T(8,128)(2,1)S(1)} %slice.52), channel_id=1, source_target_pairs={{0,1},{1,2},{2,3},{4,5},{5,6},{6,7},{8,9},{9,10},{10,11},{12,13},{... | collective-permute-start | bytes 1966088 | tf_op jit(solution)/shard_map/ppermute | solution.py:443
  96.3 21.5 %collective-permute-start.24 = (bf16[80,5120]{1,0:T(8,128)(2,1)}, bf16[80,5120]{1,0:T(8,128)(2,1)S(1)}, u32[]{:S(2)}, u32[]{:S(2)}) collective-permute-start(bf16[80,5120]{1,0:T(8,128)(2,1)} %collective-permute-done.22.refs_12_), channel_id=1, source_target_pairs={{0,2},{2,64},{64,66},{66,128},{128,130},{130,192},{192,194},{194,0... | collective-permute-start | bytes 2457608 | tf_op jit(solution)/shard_map/ppermute | solution.py:26
  96.3 21.6 %collective-permute-start.25 = (bf16[80,5120]{1,0:T(8,128)(2,1)}, bf16[80,5120]{1,0:T(8,128)(2,1)S(1)}, u32[]{:S(2)}, u32[]{:S(2)}) collective-permute-start(bf16[80,5120]{1,0:T(8,128)(2,1)} %collective-permute-done.23.refs_13_), channel_id=1, source_target_pairs={{0,194},{2,0},{64,2},{66,64},{128,66},{130,128},{192,130},{194,192... | collective-permute-start | bytes 2457608 | tf_op jit(solution)/shard_map/ppermute | solution.py:26
  107.1 14.2 %collective-permute-start.19 = (bf16[320,768]{1,0:T(8,128)(2,1)}, bf16[320,768]{1,0:T(8,128)(2,1)S(1)}, u32[]{:S(2)}, u32[]{:S(2)}) collective-permute-start(bf16[320,768]{1,0:T(8,128)(2,1)} %attention.1.refs_0_), channel_id=1, source_target_pairs={{0,12},{4,0},{8,4},{12,8},{1,13},{5,1},{9,5},{13,9},{2,14},{6,2},{... | collective-permute-start | bytes 1474568 | tf_op jit(solution)/shard_map/ppermute | solution.py:26
  110.0 14.6 %collective-permute-start.21 = (bf16[320,768]{1,0:T(8,128)(2,1)}, bf16[320,768]{1,0:T(8,128)(2,1)S(1)}, u32[]{:S(2)}, u32[]{:S(2)}) collective-permute-start(bf16[320,768]{1,0:T(8,128)(2,1)} %attention.1.refs_0_), channel_id=1, source_target_pairs={{0,4},{4,8},{8,12},{12,0},{1,5},{5,9},{9,13},{13,1},{2,6},{6,10},{... | collective-permute-start | bytes 1474568 | tf_op jit(solution)/shard_map/ppermute | solution.py:26
  124.6 20.5 %collective-permute-start.26 = (bf16[80,5120]{1,0:T(8,128)(2,1)S(1)}, bf16[80,5120]{1,0:T(8,128)(2,1)S(1)}, u32[]{:S(2)}, u32[]{:S(2)}) collective-permute-start(bf16[80,5120]{1,0:T(8,128)(2,1)S(1)} %collective-permute-done.24.refs_14_), channel_id=1, source_target_pairs={{0,2},{2,64},{64,66},{66,128},{128,130},{130,192},{192,194},{194,0... | collective-permute-start | bytes 2457608 | tf_op jit(solution)/shard_map/ppermute | solution.py:26
  124.6 14.0 %collective-permute-start.20 = (bf16[320,768]{1,0:T(8,128)(2,1)}, bf16[320,768]{1,0:T(8,128)(2,1)S(1)}, u32[]{:S(2)}, u32[]{:S(2)}) collective-permute-start(bf16[320,768]{1,0:T(8,128)(2,1)} %attention.1.refs_0_), channel_id=1, source_target_pairs={{0,8},{4,12},{8,0},{12,4},{1,9},{5,13},{9,1},{13,5},{2,10},{6,14},... | collective-permute-start | bytes 1474568 | tf_op jit(solution)/shard_map/ppermute | solution.py:26
  124.6 22.9 %collective-permute-start.27 = (bf16[80,5120]{1,0:T(8,128)(2,1)}, bf16[80,5120]{1,0:T(8,128)(2,1)}, u32[]{:S(2)}, u32[]{:S(2)}) collective-permute-start(bf16[80,5120]{1,0:T(8,128)(2,1)} %collective-permute-done.22.refs_12_), channel_id=1, source_target_pairs={{0,1},{1,0},{2,3},{3,2},{4,5},{5,4},{6,7},{7,6},{8,9},{9,8},{10,11... | collective-permute-start | bytes 2457608 | tf_op jit(solution)/shard_map/ppermute | solution.py:30
  124.7 22.8 %collective-permute-start.28 = (bf16[80,5120]{1,0:T(8,128)(2,1)}, bf16[80,5120]{1,0:T(8,128)(2,1)}, u32[]{:S(2)}, u32[]{:S(2)}) collective-permute-start(bf16[80,5120]{1,0:T(8,128)(2,1)} %collective-permute-done.23.refs_13_), channel_id=1, source_target_pairs={{0,1},{1,0},{2,3},{3,2},{4,5},{5,4},{6,7},{7,6},{8,9},{9,8},{10,11... | collective-permute-start | bytes 2457608 | tf_op jit(solution)/shard_map/ppermute | solution.py:30
  125.2 22.3 %collective-permute-start.29 = (bf16[80,5120]{1,0:T(8,128)(2,1)S(1)}, bf16[80,5120]{1,0:T(8,128)(2,1)}, u32[]{:S(2)}, u32[]{:S(2)}) collective-permute-start(bf16[80,5120]{1,0:T(8,128)(2,1)S(1)} %collective-permute-done.24.refs_14_), channel_id=1, source_target_pairs={{0,1},{1,0},{2,3},{3,2},{4,5},{5,4},{6,7},{7,6},{8,9},{9,8},{10,11... | collective-permute-start | bytes 2457608 | tf_op jit(solution)/shard_map/ppermute | solution.py:30
  138.6 8.8 %collective-permute-start.30 = (bf16[80,5120]{1,0:T(8,128)(2,1)S(1)}, bf16[80,5120]{1,0:T(8,128)(2,1)}, u32[]{:S(2)}, u32[]{:S(2)}) collective-permute-start(bf16[80,5120]{1,0:T(8,128)(2,1)S(1)} %collective-permute-done.25.refs_15_), channel_id=1, source_target_pairs={{0,1},{1,0},{2,3},{3,2},{4,5},{5,4},{6,7},{7,6},{8,9},{9,8},{10,11... | collective-permute-start | bytes 2457608 | tf_op jit(solution)/shard_map/ppermute | solution.py:30
  170.0 29.4 %all-to-all-start.1 = ((bf16[4,320,768]{2,1,0:T(8,128)(2,1)}), bf16[4,320,768]{2,1,0:T(8,128)(2,1)S(1)}, u32[]{:S(2)}, u32[]{:S(2)}) async-start(bf16[4,320,768]{2,1,0:T(8,128)(2,1)} %get-tuple-element.38), calls=%async_computation.1 | async-start | bytes 3932160 | tf_op jit(solution)/shard_map/all_to_all | solution.py:454
  (37 other events, 427.6 us)

commit v6 on v4

--- a/solution.py
+++ b/solution.py
@@ -436,6 +436,7 @@
     (qkv_z,) = after([qkv_z], rest_y, cosine, sine, key_start, gain, attn_step, step_block, *blocks)
     qkv_near = four_blocks(qkv_z, "y")
     ahead, behind = shift(rest_y, Z, 8, 1), shift(rest_y, Z, 8, -1)
+    early = [swap_core(block) for block in (rest_y, ahead, behind)]
     (qkv_stack,) = after([jnp.stack(qkv_near)], ahead, behind)
     qkv_far = swap_core(qkv_stack)
     query, own, features, size = project(spot, blocks, qkv_near, qkv_far, gain, cosine, sine)
@@ -445,7 +446,8 @@
     attended = attention(key_start, query, before, own, recent)
     everyone = four_blocks(attended, "tp")
     near = ring_z(rest_y, ahead, behind, {2: (before, recent), 3: (everyone[1], everyone[3])})
-    far = [swap_core(block) for block in near]
+    (near[7],) = after([near[7]], everyone[2])
+    far = early + [swap_core(block) for block in near[3:]]
     parts, mixed = layer(
         spot, everyone, features, size, attn_step, up_scale[None], gate_scale[None], near, far
     )

time: 207 us -> 208 us (level)
  waiting for transfers between devices: 86.7 us -> 84.4 us
    unnamed x70 -> x76, local copies, waits for them, and re-layouts: 8.06 us -> 10.1 us
  transfers between devices with their start and end apart: 37 -> 37, of which waited for: 16 -> 15; matrix products, arithmetic and copies ran while one was open for 5% -> 5% of each run, Pallas kernels for 10% -> 10%
where the time goes in v6:
time: 208 us; the launch traced here: 205 us
  waiting for transfers between devices  84.4 us (41%)
  starting transfers between devices  52.8 us (25%)
  Pallas kernels  43.4 us (21%)
  local copies, waits for them, and re-layouts  17.8 us (9%)
  other arithmetic  5.77 us (3%)
    ppermute x25, waiting for transfers between devices, shift(): return lax.ppermute(block, axis, ring(count, step))  57.9 us
    ppermute x25, starting transfers between devices, shift(): return lax.ppermute(block, axis, ring(count, step))  37.2 us
    all_to_all x1, waiting for transfers between devices, body(): landed = lax.all_to_all(parts, 'tp', 0, 0, tiled=True).astype(F32)  25.2 us
    pallas_call x1, Pallas kernels, layer(): pl.pallas_call(layer_kernel, out_shape=[jax.ShapeDtypeStruct((4, local, r...  22.3 us
    unnamed x76, local copies, waits for them, and re-layouts  10.1 us
    all_to_all x1, starting transfers between devices, body(): qkv_z = lax.all_to_all(everywhere, Z, 0, 0, tiled=True)  8.47 us
    pallas_call x1, Pallas kernels, attention(): pl.pallas_call(attention_kernel, out_shape=jax.ShapeDtypeStruct(query.sha...  7.53 us
    pallas_call x1, Pallas kernels, project(): pl.pallas_call(project_kernel, out_shape=[jax.ShapeDtypeStruct((local, ro...  5.85 us
  transfers between devices with their start and end apart: 37, of which 15 were waited for; matrix products, arithmetic and copies ran while one was open for 5% of the time, Pallas kernels for 10%

profile of v6, /device:TPU:16, one launch (start us, length us, event | category | flops | bytes accessed | tf_op | source)
XLA Modules:
  0.0 204.7 jit_solution(15053441671435387525)
XLA Ops:
  0.8 2.8 %collective-permute-start.3 = (bf16[20,320]{1,0:T(8,128)(2,1)S(1)}, bf16[20,320]{1,0:T(8,128)(2,1)S(1)}, u32[]{:S(2)}, u32[]{:S(2)}) collective-permute-start(bf16[20,320]{1,0:T(8,128)(2,1)S(1)} %convert_bitcast_fusion.1), channel_id=1, source_target_pairs={{0,12},{4,0},{8,4},{12,8},{1,13},{5,1},{9,5},{13,9},{2,14},{6,2},{... | collective-permute-start | bytes 38408 | tf_op jit(solution)/shard_map/ppermute | solution.py:26
  6.6 2.4 %collective-permute-start = (bf16[320,768]{1,0:T(8,128)(2,1)S(1)}, bf16[320,768]{1,0:T(8,128)(2,1)S(1)}, u32[]{:S(2)}, u32[]{:S(2)}) collective-permute-start(bf16[320,768]{1,0:T(8,128)(2,1)S(1)} %reshape.58.refs_0_), channel_id=1, source_target_pairs={{0,12},{4,0},{8,4},{12,8},{1,13},{5,1},{9,5},{13,9},{2,14},{6,2},{... | collective-permute-start | bytes 1474568 | tf_op jit(solution)/shard_map/ppermute | solution.py:26
  9.0 1.5 collective-permute-start.1
  14.2 8.5 %all-to-all-start = ((bf16[8,24,960]{2,1,0:T(8,128)(2,1)}), bf16[8,24,960]{2,1,0:T(8,128)(2,1)S(1)}, u32[]{:S(2)}, u32[]{:S(2)}) async-start(bf16[8,24,960]{2,1,0:T(8,128)(2,1)} %broadcast_in_dim.31), calls=%async_computation | async-start | bytes 786432 | tf_op jit(solution)/shard_map/all_to_all | solution.py:433
  22.8 2.9 %collective-permute-start.7 = (bf16[20,5120]{1,0:T(8,128)(2,1)S(1)}, bf16[20,5120]{1,0:T(8,128)(2,1)S(1)}, u32[]{:S(2)}, u32[]{:S(2)}) collective-permute-start(bf16[20,5120]{1,0:T(8,128)(2,1)S(1)} %concatenate.10.refs_0_), channel_id=1, source_target_pairs={{0,32},{16,48},{32,0},{48,16},{1,33},{17,49},{33,1},{49,17},{2,34}... | collective-permute-start | bytes 614408 | tf_op jit(solution)/shard_map/ppermute | solution.py:26
  27.4 5.4 %collective-permute-done.7.refs_2_ = bf16[20,5120]{1,0:T(8,128)(2,1)S(1)} collective-permute-done((bf16[20,5120]{1,0:T(8,128)(2,1)S(1)}, bf16[20,5120]{1,0:T(8,128)(2,1)S(1)}, u32[]{:S(2)}, u32[]{:S(2)}) %collective-permute-start.7) | collective-permute-done | bytes 204832 | tf_op jit(solution)/shard_map/ppermute | solution.py:26
  32.8 2.6 %collective-permute-done.8.refs_3_ = bf16[20,5120]{1,0:T(8,128)(2,1)S(1)} collective-permute-done((bf16[20,5120]{1,0:T(8,128)(2,1)S(1)}, bf16[20,5120]{1,0:T(8,128)(2,1)S(1)}, u32[]{:S(2)}, u32[]{:S(2)}) %collective-permute-start.8) | collective-permute-done | bytes 204832 | tf_op jit(solution)/shard_map/ppermute | solution.py:26
  36.0 2.5 %in_order.1.refs_9_ = bf16[80,5120]{1,0:T(8,128)(2,1)} custom-call(s32[4]{0:T(128)} %pad_add_fusion.place_ref, bf16[20,5120]{1,0:T(8,128)(2,1)} %copy-done.12, bf16[20,5120]{1,0:T(8,128)(2,1)} %copy-done.14, bf16[20,5120]{1,0:T(8,128)(2,1)} %copy-done.15, bf16[20,5120]{1,0:T(8,128)(2,1)} %copy-done.16), custom_call_target="tpu_custom_call" | custom-call | bytes 1638400 | tf_op jit(solution)/shard_map/in_order/pallas_call | solution.py:62
  38.5 1.7 collective-permute-start.12
  40.3 1.5 collective-permute-start.13
  43.7 2.9 %collective-permute-start.10 = (bf16[8,24,960]{2,1,0:T(8,128)(2,1)S(1)}, bf16[8,24,960]{2,1,0:T(8,128)(2,1)S(1)}, u32[]{:S(2)}, u32[]{:S(2)}) collective-permute-start(bf16[8,24,960]{2,1,0:T(8,128)(2,1)S(1)} %all-to-all-done.refs_4_), channel_id=1, source_target_pairs={{0,32},{16,48},{32,0},{48,16},{1,33},{17,49},{33,1},{49,17},{2,34}... | collective-permute-start | bytes 1105928 | tf_op jit(solution)/shard_map/ppermute | solution.py:26
  46.6 2.0 collective-permute-start.11
  48.6 6.5 %collective-permute-done.9.refs_5_ = bf16[8,24,960]{2,1,0:T(8,128)(2,1)S(1)} collective-permute-done((bf16[8,24,960]{2,1,0:T(8,128)(2,1)S(1)}, bf16[8,24,960]{2,1,0:T(8,128)(2,1)S(1)}, u32[]{:S(2)}, u32[]{:S(2)}) %collective-permute-start.9) | collective-permute-done | bytes 368672 | tf_op jit(solution)/shard_map/ppermute | solution.py:26
  55.2 2.1 %collective-permute-done.10.refs_6_ = bf16[8,24,960]{2,1,0:T(8,128)(2,1)S(1)} collective-permute-done((bf16[8,24,960]{2,1,0:T(8,128)(2,1)S(1)}, bf16[8,24,960]{2,1,0:T(8,128)(2,1)S(1)}, u32[]{:S(2)}, u32[]{:S(2)}) %collective-permute-start.10) | collective-permute-done | bytes 368672 | tf_op jit(solution)/shard_map/ppermute | solution.py:26
  57.3 5.3 %collective-permute-done.11.refs_7_ = bf16[8,24,960]{2,1,0:T(8,128)(2,1)S(1)} collective-permute-done((bf16[8,24,960]{2,1,0:T(8,128)(2,1)S(1)}, bf16[8,24,960]{2,1,0:T(8,128)(2,1)S(1)}, u32[]{:S(2)}, u32[]{:S(2)}) %collective-permute-start.11) | collective-permute-done | bytes 368672 | tf_op jit(solution)/shard_map/ppermute | solution.py:26
  62.5 1.4 pad_maximum_fusion
  64.5 3.0 %collective-permute-start.20 = (bf16[80,5120]{1,0:T(8,128)(2,1)}, bf16[80,5120]{1,0:T(8,128)(2,1)}, u32[]{:S(2)}, u32[]{:S(2)}) collective-permute-start(bf16[80,5120]{1,0:T(8,128)(2,1)} %collective-permute-done.13.refs_11_), channel_id=1, source_target_pairs={{0,194},{2,0},{64,2},{66,64},{128,66},{130,128},{192,130},{194,192... | collective-permute-start | bytes 2457608 | tf_op jit(solution)/shard_map/ppermute | solution.py:26
  70.8 5.8 %project.1 = (bf16[320,768]{1,0:T(8,128)(2,1)S(1)}, bf16[640,768]{1,0:T(8,128)(2,1)S(1)}, bf16[1280,768]{1,0:T(8,128)(2,1)S(1)}, f32[1,768]{1,0:T(1,128)S(1)}) custom-call(s32[4]{0:T(128)S(1)} %copy-done.1, bf16[320,768]{1,0:T(8,128)(2,1)S(1)} %reshape.58.refs_0_, bf16[320,768]{1,0:T(8,128)(2,1)S(1)} %copy-done.3, bf16[320,768]{1,0:T(8,128)(2,1)S(1)} %copy-done.5, ...), custom_call_target="tpu_custom_call" | custom-call | flops 1900000000 | bytes 12000000 | tf_op jit(solution)/shard_map/project/pallas_call | solution.py:235
  79.4 2.1 %collective-permute-start.15 = (bf16[640,512]{1,0:T(8,128)(2,1)S(1)}, bf16[640,512]{1,0:T(8,128)(2,1)S(1)}, u32[]{:S(2)}, u32[]{:S(2)}) collective-permute-start(bf16[640,512]{1,0:T(8,128)(2,1)S(1)} %slice.52), channel_id=1, source_target_pairs={{0,1},{1,2},{2,3},{4,5},{5,6},{6,7},{8,9},{9,10},{10,11},{12,13},{... | collective-permute-start | bytes 1966088 | tf_op jit(solution)/shard_map/ppermute | solution.py:443
  81.5 5.2 %attention_recent.1.recent_ref = bf16[320,256]{1,0:T(8,128)(2,1)} custom-call(s32[1,768]{1,0:T(1,128)} %broadcast_in_dim.30.start_ref, bf16[320,768]{1,0:T(8,128)(2,1)} %copy-done.8, bf16[640,768]{1,0:T(8,128)(2,1)} %copy-done), custom_call_target="tpu_custom_call" | custom-call | flops 260000000 | bytes 2000000 | tf_op jit(solution)/shard_map/attention_recent/pallas_call | solution.py:155
  86.8 5.7 %collective-permute-start.21 = (bf16[80,5120]{1,0:T(8,128)(2,1)}, bf16[80,5120]{1,0:T(8,128)(2,1)S(1)}, u32[]{:S(2)}, u32[]{:S(2)}) collective-permute-start(bf16[80,5120]{1,0:T(8,128)(2,1)} %collective-permute-done.19.refs_12_), channel_id=1, source_target_pairs={{0,2},{2,64},{64,66},{66,128},{128,130},{130,192},{192,194},{194,0... | collective-permute-start | bytes 2457608 | tf_op jit(solution)/shard_map/ppermute | solution.py:26
  93.7 7.5 %attention.1.refs_0_ = bf16[320,768]{1,0:T(8,128)(2,1)} custom-call(s32[1,768]{1,0:T(1,128)} %broadcast_in_dim.30.start_ref, bf16[320,768]{1,0:T(8,128)(2,1)} %copy-done.8, bf16[640,512]{1,0:T(8,128)(2,1)} %copy-done.33, bf16[640,768]{1,0:T(8,128)(2,1)} %copy-done, bf16[320,256]{1,0:T(8,128)(2,1)} %attention_recent.1.recent_ref), custom_call_target="tpu_custom_call" | custom-call | flops 520000000 | bytes 4000000 | tf_op jit(solution)/shard_map/attention/pallas_call | solution.py:166
  101.3 2.6 %collective-permute-start.16 = (bf16[320,768]{1,0:T(8,128)(2,1)}, bf16[320,768]{1,0:T(8,128)(2,1)S(1)}, u32[]{:S(2)}, u32[]{:S(2)}) collective-permute-start(bf16[320,768]{1,0:T(8,128)(2,1)} %attention.1.refs_0_), channel_id=1, source_target_pairs={{0,12},{4,0},{8,4},{12,8},{1,13},{5,1},{9,5},{13,9},{2,14},{6,2},{... | collective-permute-start | bytes 1474568 | tf_op jit(solution)/shard_map/ppermute | solution.py:26
  103.9 10.0 %collective-permute-done.16.refs_1_ = bf16[320,768]{1,0:T(8,128)(2,1)S(1)} collective-permute-done((bf16[320,768]{1,0:T(8,128)(2,1)}, bf16[320,768]{1,0:T(8,128)(2,1)S(1)}, u32[]{:S(2)}, u32[]{:S(2)}) %collective-permute-start.16) | collective-permute-done | bytes 491552 | tf_op jit(solution)/shard_map/ppermute | solution.py:26
  113.9 3.3 %collective-permute-done.18.refs_3_ = bf16[320,768]{1,0:T(8,128)(2,1)S(1)} collective-permute-done((bf16[320,768]{1,0:T(8,128)(2,1)}, bf16[320,768]{1,0:T(8,128)(2,1)S(1)}, u32[]{:S(2)}, u32[]{:S(2)}) %collective-permute-start.18) | collective-permute-done | bytes 491552 | tf_op jit(solution)/shard_map/ppermute | solution.py:26
  119.4 15.3 %collective-permute-done.17.refs_2_ = bf16[320,768]{1,0:T(8,128)(2,1)S(1)} collective-permute-done((bf16[320,768]{1,0:T(8,128)(2,1)}, bf16[320,768]{1,0:T(8,128)(2,1)S(1)}, u32[]{:S(2)}, u32[]{:S(2)}) %collective-permute-start.17) | collective-permute-done | bytes 491552 | tf_op jit(solution)/shard_map/ppermute | solution.py:26
  134.8 2.5 %collective-permute-done.23.refs_16_ = bf16[80,5120]{1,0:T(8,128)(2,1)S(1)} collective-permute-done((bf16[80,5120]{1,0:T(8,128)(2,1)S(1)}, bf16[80,5120]{1,0:T(8,128)(2,1)S(1)}, u32[]{:S(2)}, u32[]{:S(2)}) %collective-permute-start.23) | collective-permute-done | bytes 819232 | tf_op jit(solution)/shard_map/ppermute | solution.py:26
  143.2 22.3 %layer.1 = (bf16[4,320,768]{2,1,0:T(8,128)(2,1)}, f32[320,768]{1,0:T(8,128)}) custom-call(s32[4]{0:T(128)} %pad_add_fusion.place_ref, bf16[320,768]{1,0:T(8,128)(2,1)} %attention.1.refs_0_, bf16[320,768]{1,0:T(8,128)(2,1)} %copy-done.34, bf16[320,768]{1,0:T(8,128)(2,1)} %copy-done.36, bf16[320,768]{1,0:T(8,128)(2,1)} %copy-done.35, ...), custom_call_target="tpu_custom_call" | custom-call | flops 10000000000 | bytes 20000000 | tf_op jit(solution)/shard_map/layer/pallas_call | solution.py:355
  165.5 3.6 %all-to-all-start.1 = ((bf16[4,320,768]{2,1,0:T(8,128)(2,1)}), bf16[4,320,768]{2,1,0:T(8,128)(2,1)S(1)}, u32[]{:S(2)}, u32[]{:S(2)}) async-start(bf16[4,320,768]{2,1,0:T(8,128)(2,1)} %get-tuple-element.38), calls=%async_computation.1 | async-start | bytes 3932160 | tf_op jit(solution)/shard_map/all_to_all | solution.py:454
  169.5 25.2 %all-to-all-done.1 = bf16[4,320,768]{2,1,0:T(8,128)(2,1)S(1)} async-done(((bf16[4,320,768]{2,1,0:T(8,128)(2,1)}), bf16[4,320,768]{2,1,0:T(8,128)(2,1)S(1)}, u32[]{:S(2)}, u32[]{:S(2)}) %all-to-all-start.1) | async-done | bytes 1966112 | tf_op jit(solution)/shard_map/all_to_all | solution.py:454
  197.0 1.5 collective-permute-start.33
  199.5 2.7 %collective-permute-done.33 = f32[4,768]{1,0:T(4,128)S(1)} collective-permute-done((f32[4,768]{1,0:T(4,128)S(1)}, f32[4,768]{1,0:T(4,128)S(1)}, u32[]{:S(2)}, u32[]{:S(2)}) %collective-permute-start.33) | collective-permute-done | bytes 12320 | tf_op jit(solution)/shard_map/ppermute | solution.py:26
  (174 shorter events, 33.8 us)
Async XLA Ops:
  0.8 11.8 %collective-permute-start.3 = (bf16[20,320]{1,0:T(8,128)(2,1)S(1)}, bf16[20,320]{1,0:T(8,128)(2,1)S(1)}, u32[]{:S(2)}, u32[]{:S(2)}) collective-permute-start(bf16[20,320]{1,0:T(8,128)(2,1)S(1)} %convert_bitcast_fusion.1), channel_id=1, source_target_pairs={{0,12},{4,0},{8,4},{12,8},{1,13},{5,1},{9,5},{13,9},{2,14},{6,2},{... | collective-permute-start | bytes 38408 | tf_op jit(solution)/shard_map/ppermute | solution.py:26
  3.5 9.1 %collective-permute-start.4 = (bf16[20,320]{1,0:T(8,128)(2,1)S(1)}, bf16[20,320]{1,0:T(8,128)(2,1)S(1)}, u32[]{:S(2)}, u32[]{:S(2)}) collective-permute-start(bf16[20,320]{1,0:T(8,128)(2,1)S(1)} %convert_bitcast_fusion.1), channel_id=1, source_target_pairs={{0,8},{4,12},{8,0},{12,4},{1,9},{5,13},{9,1},{13,5},{2,10},{6,14},... | collective-permute-start | bytes 38408 | tf_op jit(solution)/shard_map/ppermute | solution.py:26
  4.3 8.3 %collective-permute-start.5 = (bf16[20,320]{1,0:T(8,128)(2,1)S(1)}, bf16[20,320]{1,0:T(8,128)(2,1)S(1)}, u32[]{:S(2)}, u32[]{:S(2)}) collective-permute-start(bf16[20,320]{1,0:T(8,128)(2,1)S(1)} %convert_bitcast_fusion.1), channel_id=1, source_target_pairs={{0,4},{4,8},{8,12},{12,0},{1,5},{5,9},{9,13},{13,1},{2,6},{6,10},{... | collective-permute-start | bytes 38408 | tf_op jit(solution)/shard_map/ppermute | solution.py:26
  6.6 35.6 %collective-permute-start = (bf16[320,768]{1,0:T(8,128)(2,1)S(1)}, bf16[320,768]{1,0:T(8,128)(2,1)S(1)}, u32[]{:S(2)}, u32[]{:S(2)}) collective-permute-start(bf16[320,768]{1,0:T(8,128)(2,1)S(1)} %reshape.58.refs_0_), channel_id=1, source_target_pairs={{0,12},{4,0},{8,4},{12,8},{1,13},{5,1},{9,5},{13,9},{2,14},{6,2},{... | collective-permute-start | bytes 1474568 | tf_op jit(solution)/shard_map/ppermute | solution.py:26
  9.0 33.2 %collective-permute-start.1 = (bf16[320,768]{1,0:T(8,128)(2,1)S(1)}, bf16[320,768]{1,0:T(8,128)(2,1)S(1)}, u32[]{:S(2)}, u32[]{:S(2)}) collective-permute-start(bf16[320,768]{1,0:T(8,128)(2,1)S(1)} %reshape.58.refs_0_), channel_id=1, source_target_pairs={{0,8},{4,12},{8,0},{12,4},{1,9},{5,13},{9,1},{13,5},{2,10},{6,14},... | collective-permute-start | bytes 1474568 | tf_op jit(solution)/shard_map/ppermute | solution.py:26
  12.6 29.7 %collective-permute-start.2 = (bf16[320,768]{1,0:T(8,128)(2,1)S(1)}, bf16[320,768]{1,0:T(8,128)(2,1)S(1)}, u32[]{:S(2)}, u32[]{:S(2)}) collective-permute-start(bf16[320,768]{1,0:T(8,128)(2,1)S(1)} %reshape.58.refs_0_), channel_id=1, source_target_pairs={{0,4},{4,8},{8,12},{12,0},{1,5},{5,9},{9,13},{13,1},{2,6},{6,10},{... | collective-permute-start | bytes 1474568 | tf_op jit(solution)/shard_map/ppermute | solution.py:26
  12.8 12.9 %collective-permute-start.6 = (bf16[20,5120]{1,0:T(8,128)(2,1)S(1)}, bf16[20,5120]{1,0:T(8,128)(2,1)S(1)}, u32[]{:S(2)}, u32[]{:S(2)}) collective-permute-start(bf16[20,5120]{1,0:T(8,128)(2,1)S(1)} %concatenate.10.refs_0_), channel_id=1, source_target_pairs={{0,48},{16,0},{32,16},{48,32},{1,49},{17,1},{33,17},{49,33},{2,50}... | collective-permute-start | bytes 614408 | tf_op jit(solution)/shard_map/ppermute | solution.py:26
  14.2 28.9 %all-to-all-start = ((bf16[8,24,960]{2,1,0:T(8,128)(2,1)}), bf16[8,24,960]{2,1,0:T(8,128)(2,1)S(1)}, u32[]{:S(2)}, u32[]{:S(2)}) async-start(bf16[8,24,960]{2,1,0:T(8,128)(2,1)} %broadcast_in_dim.31), calls=%async_computation | async-start | bytes 786432 | tf_op jit(solution)/shard_map/all_to_all | solution.py:433
  22.8 10.0 %collective-permute-start.7 = (bf16[20,5120]{1,0:T(8,128)(2,1)S(1)}, bf16[20,5120]{1,0:T(8,128)(2,1)S(1)}, u32[]{:S(2)}, u32[]{:S(2)}) collective-permute-start(bf16[20,5120]{1,0:T(8,128)(2,1)S(1)} %concatenate.10.refs_0_), channel_id=1, source_target_pairs={{0,32},{16,48},{32,0},{48,16},{1,33},{17,49},{33,1},{49,17},{2,34}... | collective-permute-start | bytes 614408 | tf_op jit(solution)/shard_map/ppermute | solution.py:26
  25.7 9.6 %collective-permute-start.8 = (bf16[20,5120]{1,0:T(8,128)(2,1)S(1)}, bf16[20,5120]{1,0:T(8,128)(2,1)S(1)}, u32[]{:S(2)}, u32[]{:S(2)}) collective-permute-start(bf16[20,5120]{1,0:T(8,128)(2,1)S(1)} %concatenate.10.refs_0_), channel_id=1, source_target_pairs={{0,16},{16,32},{32,48},{48,0},{1,17},{17,33},{33,49},{49,1},{2,18}... | collective-permute-start | bytes 614408 | tf_op jit(solution)/shard_map/ppermute | solution.py:26
  38.5 25.4 %collective-permute-start.12 = (bf16[80,5120]{1,0:T(8,128)(2,1)}, bf16[80,5120]{1,0:T(8,128)(2,1)}, u32[]{:S(2)}, u32[]{:S(2)}) collective-permute-start(bf16[80,5120]{1,0:T(8,128)(2,1)} %in_order.1.refs_9_), channel_id=1, source_target_pairs={{0,2},{2,64},{64,66},{66,128},{128,130},{130,192},{192,194},{194,0... | collective-permute-start | bytes 2457608 | tf_op jit(solution)/shard_map/ppermute | solution.py:26
  40.3 23.6 %collective-permute-start.13 = (bf16[80,5120]{1,0:T(8,128)(2,1)}, bf16[80,5120]{1,0:T(8,128)(2,1)}, u32[]{:S(2)}, u32[]{:S(2)}) collective-permute-start(bf16[80,5120]{1,0:T(8,128)(2,1)} %in_order.1.refs_9_), channel_id=1, source_target_pairs={{0,194},{2,0},{64,2},{66,64},{128,66},{130,128},{192,130},{194,192... | collective-permute-start | bytes 2457608 | tf_op jit(solution)/shard_map/ppermute | solution.py:26
  43.1 12.1 %collective-permute-start.9 = (bf16[8,24,960]{2,1,0:T(8,128)(2,1)S(1)}, bf16[8,24,960]{2,1,0:T(8,128)(2,1)S(1)}, u32[]{:S(2)}, u32[]{:S(2)}) collective-permute-start(bf16[8,24,960]{2,1,0:T(8,128)(2,1)S(1)} %all-to-all-done.refs_4_), channel_id=1, source_target_pairs={{0,48},{16,0},{32,16},{48,32},{1,49},{17,1},{33,17},{49,33},{2,50}... | collective-permute-start | bytes 1105928 | tf_op jit(solution)/shard_map/ppermute | solution.py:26
  43.7 13.6 %collective-permute-start.10 = (bf16[8,24,960]{2,1,0:T(8,128)(2,1)S(1)}, bf16[8,24,960]{2,1,0:T(8,128)(2,1)S(1)}, u32[]{:S(2)}, u32[]{:S(2)}) collective-permute-start(bf16[8,24,960]{2,1,0:T(8,128)(2,1)S(1)} %all-to-all-done.refs_4_), channel_id=1, source_target_pairs={{0,32},{16,48},{32,0},{48,16},{1,33},{17,49},{33,1},{49,17},{2,34}... | collective-permute-start | bytes 1105928 | tf_op jit(solution)/shard_map/ppermute | solution.py:26
  46.6 15.9 %collective-permute-start.11 = (bf16[8,24,960]{2,1,0:T(8,128)(2,1)S(1)}, bf16[8,24,960]{2,1,0:T(8,128)(2,1)S(1)}, u32[]{:S(2)}, u32[]{:S(2)}) collective-permute-start(bf16[8,24,960]{2,1,0:T(8,128)(2,1)S(1)} %all-to-all-done.refs_4_), channel_id=1, source_target_pairs={{0,16},{16,32},{32,48},{48,0},{1,17},{17,33},{33,49},{49,1},{2,18}... | collective-permute-start | bytes 1105928 | tf_op jit(solution)/shard_map/ppermute | solution.py:26
  64.2 22.6 %collective-permute-start.19 = (bf16[80,5120]{1,0:T(8,128)(2,1)}, bf16[80,5120]{1,0:T(8,128)(2,1)}, u32[]{:S(2)}, u32[]{:S(2)}) collective-permute-start(bf16[80,5120]{1,0:T(8,128)(2,1)} %collective-permute-done.12.refs_10_), channel_id=1, source_target_pairs={{0,2},{2,64},{64,66},{66,128},{128,130},{130,192},{192,194},{194,0... | collective-permute-start | bytes 2457608 | tf_op jit(solution)/shard_map/ppermute | solution.py:26
  64.5 22.3 %collective-permute-start.20 = (bf16[80,5120]{1,0:T(8,128)(2,1)}, bf16[80,5120]{1,0:T(8,128)(2,1)}, u32[]{:S(2)}, u32[]{:S(2)}) collective-permute-start(bf16[80,5120]{1,0:T(8,128)(2,1)} %collective-permute-done.13.refs_11_), channel_id=1, source_target_pairs={{0,194},{2,0},{64,2},{66,64},{128,66},{130,128},{192,130},{194,192... | collective-permute-start | bytes 2457608 | tf_op jit(solution)/shard_map/ppermute | solution.py:26
  79.4 7.3 %collective-permute-start.15 = (bf16[640,512]{1,0:T(8,128)(2,1)S(1)}, bf16[640,512]{1,0:T(8,128)(2,1)S(1)}, u32[]{:S(2)}, u32[]{:S(2)}) collective-permute-start(bf16[640,512]{1,0:T(8,128)(2,1)S(1)} %slice.52), channel_id=1, source_target_pairs={{0,1},{1,2},{2,3},{4,5},{5,6},{6,7},{8,9},{9,10},{10,11},{12,13},{... | collective-permute-start | bytes 1966088 | tf_op jit(solution)/shard_map/ppermute | solution.py:443
  86.8 30.4 %collective-permute-start.21 = (bf16[80,5120]{1,0:T(8,128)(2,1)}, bf16[80,5120]{1,0:T(8,128)(2,1)S(1)}, u32[]{:S(2)}, u32[]{:S(2)}) collective-permute-start(bf16[80,5120]{1,0:T(8,128)(2,1)} %collective-permute-done.19.refs_12_), channel_id=1, source_target_pairs={{0,2},{2,64},{64,66},{66,128},{128,130},{130,192},{192,194},{194,0... | collective-permute-start | bytes 2457608 | tf_op jit(solution)/shard_map/ppermute | solution.py:26
  92.5 25.5 %collective-permute-start.22 = (bf16[80,5120]{1,0:T(8,128)(2,1)}, bf16[80,5120]{1,0:T(8,128)(2,1)S(1)}, u32[]{:S(2)}, u32[]{:S(2)}) collective-permute-start(bf16[80,5120]{1,0:T(8,128)(2,1)} %collective-permute-done.20.refs_13_), channel_id=1, source_target_pairs={{0,194},{2,0},{64,2},{66,64},{128,66},{130,128},{192,130},{194,192... | collective-permute-start | bytes 2457608 | tf_op jit(solution)/shard_map/ppermute | solution.py:26
  101.3 12.6 %collective-permute-start.16 = (bf16[320,768]{1,0:T(8,128)(2,1)}, bf16[320,768]{1,0:T(8,128)(2,1)S(1)}, u32[]{:S(2)}, u32[]{:S(2)}) collective-permute-start(bf16[320,768]{1,0:T(8,128)(2,1)} %attention.1.refs_0_), channel_id=1, source_target_pairs={{0,12},{4,0},{8,4},{12,8},{1,13},{5,1},{9,5},{13,9},{2,14},{6,2},{... | collective-permute-start | bytes 1474568 | tf_op jit(solution)/shard_map/ppermute | solution.py:26
  103.9 13.3 %collective-permute-start.18 = (bf16[320,768]{1,0:T(8,128)(2,1)}, bf16[320,768]{1,0:T(8,128)(2,1)S(1)}, u32[]{:S(2)}, u32[]{:S(2)}) collective-permute-start(bf16[320,768]{1,0:T(8,128)(2,1)} %attention.1.refs_0_), channel_id=1, source_target_pairs={{0,4},{4,8},{8,12},{12,0},{1,5},{5,9},{9,13},{13,1},{2,6},{6,10},{... | collective-permute-start | bytes 1474568 | tf_op jit(solution)/shard_map/ppermute | solution.py:26
  118.0 19.2 %collective-permute-start.23 = (bf16[80,5120]{1,0:T(8,128)(2,1)S(1)}, bf16[80,5120]{1,0:T(8,128)(2,1)S(1)}, u32[]{:S(2)}, u32[]{:S(2)}) collective-permute-start(bf16[80,5120]{1,0:T(8,128)(2,1)S(1)} %collective-permute-done.21.refs_14_), channel_id=1, source_target_pairs={{0,2},{2,64},{64,66},{66,128},{128,130},{130,192},{192,194},{194,0... | collective-permute-start | bytes 2457608 | tf_op jit(solution)/shard_map/ppermute | solution.py:26
  118.9 18.3 %collective-permute-start.24 = (bf16[80,5120]{1,0:T(8,128)(2,1)S(1)}, bf16[80,5120]{1,0:T(8,128)(2,1)S(1)}, u32[]{:S(2)}, u32[]{:S(2)}) collective-permute-start(bf16[80,5120]{1,0:T(8,128)(2,1)S(1)} %copy-done.13), channel_id=1, source_target_pairs={{0,1},{1,0},{2,3},{3,2},{4,5},{5,4},{6,7},{7,6},{8,9},{9,8},{10,11... | collective-permute-start | bytes 2457608 | tf_op jit(solution)/shard_map/ppermute | solution.py:30
  118.9 18.8 %collective-permute-start.25 = (bf16[80,5120]{1,0:T(8,128)(2,1)}, bf16[80,5120]{1,0:T(8,128)(2,1)S(1)}, u32[]{:S(2)}, u32[]{:S(2)}) collective-permute-start(bf16[80,5120]{1,0:T(8,128)(2,1)} %collective-permute-done.12.refs_10_), channel_id=1, source_target_pairs={{0,1},{1,0},{2,3},{3,2},{4,5},{5,4},{6,7},{7,6},{8,9},{9,8},{10,11... | collective-permute-start | bytes 2457608 | tf_op jit(solution)/shard_map/ppermute | solution.py:30
  119.4 18.8 %collective-permute-start.26 = (bf16[80,5120]{1,0:T(8,128)(2,1)}, bf16[80,5120]{1,0:T(8,128)(2,1)S(1)}, u32[]{:S(2)}, u32[]{:S(2)}) collective-permute-start(bf16[80,5120]{1,0:T(8,128)(2,1)} %collective-permute-done.13.refs_11_), channel_id=1, source_target_pairs={{0,1},{1,0},{2,3},{3,2},{4,5},{5,4},{6,7},{7,6},{8,9},{9,8},{10,11... | collective-permute-start | bytes 2457608 | tf_op jit(solution)/shard_map/ppermute | solution.py:30
  119.4 15.3 %collective-permute-start.17 = (bf16[320,768]{1,0:T(8,128)(2,1)}, bf16[320,768]{1,0:T(8,128)(2,1)S(1)}, u32[]{:S(2)}, u32[]{:S(2)}) collective-permute-start(bf16[320,768]{1,0:T(8,128)(2,1)} %attention.1.refs_0_), channel_id=1, source_target_pairs={{0,8},{4,12},{8,0},{12,4},{1,9},{5,13},{9,1},{13,5},{2,10},{6,14},... | collective-permute-start | bytes 1474568 | tf_op jit(solution)/shard_map/ppermute | solution.py:26
  134.8 7.5 %collective-permute-start.27 = (bf16[80,5120]{1,0:T(8,128)(2,1)}, bf16[80,5120]{1,0:T(8,128)(2,1)}, u32[]{:S(2)}, u32[]{:S(2)}) collective-permute-start(bf16[80,5120]{1,0:T(8,128)(2,1)} %collective-permute-done.19.refs_12_), channel_id=1, source_target_pairs={{0,1},{1,0},{2,3},{3,2},{4,5},{5,4},{6,7},{7,6},{8,9},{9,8},{10,11... | collective-permute-start | bytes 2457608 | tf_op jit(solution)/shard_map/ppermute | solution.py:30
  137.2 5.0 %collective-permute-start.28 = (bf16[80,5120]{1,0:T(8,128)(2,1)}, bf16[80,5120]{1,0:T(8,128)(2,1)}, u32[]{:S(2)}, u32[]{:S(2)}) collective-permute-start(bf16[80,5120]{1,0:T(8,128)(2,1)} %collective-permute-done.20.refs_13_), channel_id=1, source_target_pairs={{0,1},{1,0},{2,3},{3,2},{4,5},{5,4},{6,7},{7,6},{8,9},{9,8},{10,11... | collective-permute-start | bytes 2457608 | tf_op jit(solution)/shard_map/ppermute | solution.py:30
  137.2 5.0 %collective-permute-start.29 = (bf16[80,5120]{1,0:T(8,128)(2,1)S(1)}, bf16[80,5120]{1,0:T(8,128)(2,1)S(1)}, u32[]{:S(2)}, u32[]{:S(2)}) collective-permute-start(bf16[80,5120]{1,0:T(8,128)(2,1)S(1)} %collective-permute-done.21.refs_14_), channel_id=1, source_target_pairs={{0,1},{1,0},{2,3},{3,2},{4,5},{5,4},{6,7},{7,6},{8,9},{9,8},{10,11... | collective-permute-start | bytes 2457608 | tf_op jit(solution)/shard_map/ppermute | solution.py:30
  165.5 29.2 %all-to-all-start.1 = ((bf16[4,320,768]{2,1,0:T(8,128)(2,1)}), bf16[4,320,768]{2,1,0:T(8,128)(2,1)S(1)}, u32[]{:S(2)}, u32[]{:S(2)}) async-start(bf16[4,320,768]{2,1,0:T(8,128)(2,1)} %get-tuple-element.38), calls=%async_computation.1 | async-start | bytes 3932160 | tf_op jit(solution)/shard_map/all_to_all | solution.py:454
  197.0 5.2 %collective-permute-start.33 = (f32[4,768]{1,0:T(4,128)S(1)}, f32[4,768]{1,0:T(4,128)S(1)}, u32[]{:S(2)}, u32[]{:S(2)}) collective-permute-start(f32[4,768]{1,0:T(4,128)S(1)} %pad_maximum_fusion.1), channel_id=1, source_target_pairs={{0,8},{4,12},{8,0},{12,4},{1,9},{5,13},{9,1},{13,5},{2,10},{6,14},... | collective-permute-start | bytes 36872 | tf_op jit(solution)/shard_map/ppermute | solution.py:26
  (42 other events, 411.0 us)
